TPU v7x, 32 devices: a whole 2x2x4 slice. The times are simulated.
32 devices in a mesh: phase: 2 (over core), dp: 8 (over z, y), mp: 2 (over x).
Axes of the slice: x: 2, y: 2, z: 4, core: 2. Of those that a mesh axis runs over, the one named last changes fastest.
Arguments:
- segments: bfloat16 [2, 16, 64, 4096], P(None, 'dp', 'mp'), may hold values from -6 to 6
- memory_in: bfloat16 [16, 64, 4096], P('dp', 'mp'), may hold values from -6 to 6
- seg_lengths: int32 [2, 16], P(None, 'dp'), may hold values from 1 to 64, as said below
- routes: int32 [2, 8], replicated, may hold values from 0 to 7, each once within a row
- w_query: bfloat16 [2, 4096, 4096], P('phase', None, 'mp'), may hold values from -12 to 12
- w_key: bfloat16 [2, 4096, 1024], P('phase', None, 'mp'), may hold values from -1 to 1
- value_weight: bfloat16 [2, 4096, 1024], P('phase', None, 'mp'), may hold values from -0.09375 to 0.09375
- w_out: bfloat16 [2, 4096, 4096], P('phase', 'mp'), may hold values from -0.09375 to 0.09375
- norm_gain: bfloat16 [2, 4096], P('phase'), may hold values from 0.099609375 to 1.8984375
Outputs:
- mem_states: bfloat16 [2, 2, 16, 64, 4096], P('phase', None, 'dp', 'mp')
- seg_states: bfloat16 [2, 2, 16, 64, 4096], P('phase', None, 'dp', 'mp')
Inputs may be any that keep to these rules, and one draw needn't show every extreme that they name: Each row m is a permutation of the data groups: slot m of group g hands its memory to slot m of group routes[m, g]. `seg_lengths`: some entry equals 64.
All inputs are finite; a program needn't handle non-finite values.
Results may differ from a plain program's by a relative error of at most 0.025.
Values may be sent and summed in bfloat16 or wider, within the bound.
No kernel may reach another device: no remote copies, remote signals or barrier semaphores. Data moves between devices by JAX's collectives and lax.ppermute only.
A program may use at most 192 MiB of HBM per device.

v0:
```python
import jax
import jax.numpy as jnp
from jax import lax
from jax.sharding import PartitionSpec as P

HEAD_SIZE = 128


EPSILON = 1e-05


def shifted(value, axis, steps):
    count = lax.axis_size(axis)
    pairs = [(source, (source + steps) % count) for source in range(count)]
    return lax.ppermute(value, axis, pairs)


def norm_rows(rows, gain):
    values = rows.astype(jnp.float32)
    scaled = values * lax.rsqrt(jnp.mean(values * values, axis=-1, keepdims=True) + EPSILON)
    return (scaled * gain.astype(jnp.float32)).astype(jnp.bfloat16)


def section_layer(mem_x, seg_x, length, w_query, w_key, value_weight, w_out, gain):
    mem_dev = mem_x.shape[0]
    seg_dev = seg_x.shape[0]
    raw_mem, raw_seg = (
        lax.all_gather(mem_x, "mp", axis=0, tiled=True),
        lax.all_gather(seg_x, "mp", axis=0, tiled=True),
    )
    all_mem = norm_rows(raw_mem, gain)
    all_seg = norm_rows(raw_seg, gain)
    mem_rows = all_mem.shape[0]
    normed = jnp.concatenate([all_mem, all_seg], axis=0)
    rows_total = normed.shape[0]
    kv_dev = w_key.shape[1] // HEAD_SIZE
    query_dev = w_query.shape[1] // HEAD_SIZE
    per_group = query_dev // kv_dev
    heads_of_query = jnp.dot(normed, w_query, preferred_element_type=jnp.float32).astype(
        jnp.bfloat16
    )
    heads_of_query = heads_of_query.reshape(rows_total, kv_dev, per_group, HEAD_SIZE)
    heads_of_key = jnp.dot(normed, w_key, preferred_element_type=jnp.float32).astype(jnp.bfloat16)
    heads_of_key = heads_of_key.reshape(rows_total, kv_dev, HEAD_SIZE)
    heads_of_value = jnp.dot(normed, value_weight, preferred_element_type=jnp.float32).astype(
        jnp.bfloat16
    )
    heads_of_value = heads_of_value.reshape(rows_total, kv_dev, HEAD_SIZE)
    scores = jnp.einsum(
        "qcgd,kcd->cgqk", heads_of_query, heads_of_key, preferred_element_type=jnp.float32
    ) * HEAD_SIZE ** (-0.5)
    query_pos = lax.broadcasted_iota(jnp.int32, (rows_total, rows_total), 0)
    key_pos = lax.broadcasted_iota(jnp.int32, (rows_total, rows_total), 1)
    visible = (key_pos < mem_rows) | (key_pos - mem_rows < length) & (
        (query_pos < mem_rows) | (key_pos <= query_pos)
    )
    scores = jnp.where(visible, scores, -1e30)
    row_max = jnp.max(scores, axis=-1, keepdims=True)
    exponent = jnp.exp(scores - row_max)
    attn = (exponent / jnp.sum(exponent, axis=-1, keepdims=True)).astype(jnp.bfloat16)
    attended = jnp.einsum(
        "cgqk,kcd->qcgd", attn, heads_of_value, preferred_element_type=jnp.float32
    )
    attended = attended.astype(jnp.bfloat16).reshape(rows_total, query_dev * HEAD_SIZE)
    attended_mem = attended[:mem_rows]
    attended_seg = attended[mem_rows:]
    block_rows = mem_dev + seg_dev
    blocks = block_rows * lax.axis_size("mp") // block_rows
    term_mem = jnp.dot(attended_mem, w_out, preferred_element_type=jnp.float32).reshape(
        blocks, mem_dev, -1
    )
    term_seg = jnp.dot(attended_seg, w_out, preferred_element_type=jnp.float32).reshape(
        blocks, seg_dev, -1
    )
    summed = lax.psum_scatter(
        jnp.concatenate([term_mem, term_seg], axis=1)
        .reshape(block_rows * lax.axis_size("mp"), -1)
        .astype(jnp.bfloat16),
        "mp",
        scatter_dimension=0,
        tiled=True,
    ).astype(jnp.float32)
    new_mem = (mem_x.astype(jnp.float32) + summed[:mem_dev]).astype(jnp.bfloat16)
    new_seg = (seg_x.astype(jnp.float32) + summed[mem_dev:]).astype(jnp.bfloat16)
    return (new_mem, new_seg)


def route_memory(arrived, perm_row, group_index):
    group_count = perm_row.shape[0]
    group_ids = jnp.arange(group_count, dtype=jnp.int32)
    target = jnp.sum(jnp.where(group_ids == group_index, perm_row, 0))
    outgoing = jnp.where(
        (group_ids == target)[:, None, None], arrived[None], jnp.zeros_like(arrived)[None]
    )
    received = lax.all_to_all(outgoing, "dp", split_axis=0, concat_axis=0, tiled=True)
    return jnp.sum(received.astype(jnp.float32), axis=0).astype(jnp.bfloat16)


def per_device(
    segments, memory_in, seg_lengths, routes, w_query, w_key, value_weight, w_out, norm_gain
):
    rounds = segments.shape[0]
    slot_count = memory_in.shape[0]
    phase_count = lax.axis_size("phase")
    step_count = rounds * slot_count + phase_count - 1
    phase_index = lax.axis_index("phase")
    group_index = lax.axis_index("dp")
    is_first = phase_index == 0
    items = rounds * slot_count
    lengths_flat = seg_lengths.reshape(items)
    item_ids = jnp.arange(items, dtype=jnp.int32)
    mem_buf = jnp.where(is_first, memory_in[0], jnp.zeros_like(memory_in[0]))
    seg_buf = jnp.where(is_first, segments[0, 0], jnp.zeros_like(segments[0, 0]))
    mem_hist = jnp.zeros((items,) + memory_in.shape[1:], jnp.bfloat16)
    seg_hist = jnp.zeros((items,) + segments.shape[2:], jnp.bfloat16)
    for step in range(step_count):
        item_index = step - phase_index
        is_valid = (item_index >= 0) & (item_index < items)
        clipped = jnp.clip(item_index, 0, items - 1)
        length = jnp.sum(jnp.where(item_ids == clipped, lengths_flat, 0))
        mem_new, seg_new = section_layer(
            mem_buf, seg_buf, length, w_query[0], w_key[0], value_weight[0], w_out[0], norm_gain[0]
        )
        mem_current = lax.dynamic_index_in_dim(mem_hist, clipped, 0, keepdims=False)
        seg_current = lax.dynamic_index_in_dim(seg_hist, clipped, 0, keepdims=False)
        mem_hist = lax.dynamic_update_index_in_dim(
            mem_hist, jnp.where(is_valid, mem_new, mem_current), clipped, 0
        )
        seg_hist = lax.dynamic_update_index_in_dim(
            seg_hist, jnp.where(is_valid, seg_new, seg_current), clipped, 0
        )
        if step + 1 < step_count:
            mem_pass, seg_pass = shifted((mem_new, seg_new), "phase", 1)
            next_item = step + 1
            if next_item < items:
                next_round, next_slot = divmod(next_item, slot_count)
                if next_round == 0:
                    first_mem = memory_in[next_slot]
                else:
                    first_mem = route_memory(mem_pass, routes[next_slot], group_index)
                first_seg = segments[next_round, next_slot]
            else:
                first_mem = jnp.zeros_like(mem_pass)
                first_seg = jnp.zeros_like(seg_pass)
            mem_buf = jnp.where(is_first, first_mem, mem_pass)
            seg_buf = jnp.where(is_first, first_seg, seg_pass)
    mem_states = mem_hist.reshape((1, rounds, slot_count) + memory_in.shape[1:])
    seg_states = seg_hist.reshape((1, rounds, slot_count) + segments.shape[2:])
    return (mem_states, seg_states)


def solution(mesh):
    return jax.shard_map(
        per_device,
        mesh=mesh,
        in_specs=(
            P(None, "dp", "mp", None),
            P("dp", "mp", None),
            P(None, "dp"),
            P(),
            P("phase", None, "mp"),
            P("phase", None, "mp"),
            P("phase", None, "mp"),
            P("phase", "mp", None),
            P("phase", None),
        ),
        out_specs=(P("phase", None, "dp", "mp", None), P("phase", None, "dp", "mp", None)),
        check_vma=False,
    )
```

profile of v0, /device:TPU:0, one launch (start us, length us, event | category | flops | bytes accessed | tf_op | source)
XLA Modules:
  0.0 495.5 jit_solution(5529236552270811867)
XLA Ops:
  13.1 9.9 %all-gather.1 = bf16[1,1,64,4096]{3,2,1,0:T(8,128)(2,1)S(1)} all-gather(bf16[1,1,32,4096]{3,2,1,0:T(8,128)(2,1)S(1)} %slice_select_fusion), channel_id=3, replica_groups=mesh['phase'=2,'dp'=8,'mp'=2] {'mp'}, dimensions={2}, use_global_device_ids=true | all-gather | bytes 786432 | tf_op jit(solution)/shard_map/all_gather | solution.py:29
  24.2 8.1 %all-gather = bf16[1,64,4096]{2,1,0:T(8,128)(2,1)S(1)} all-gather(bf16[1,32,4096]{2,1,0:T(8,128)(2,1)S(1)} %slice_select_fusion.1), channel_id=2, replica_groups=mesh['phase'=2,'dp'=8,'mp'=2] {'mp'}, dimensions={1}, use_global_device_ids=true | all-gather | bytes 786432 | tf_op jit(solution)/shard_map/all_gather | solution.py:28
  34.5 8.1 %fusion.85 = bf16[128,2048]{1,0:T(8,128)(2,1)S(1)} fusion(bf16[1,4096,2048]{2,1,0:T(8,128)(2,1)} %param.13, bf16[64,4096]{1,0:T(8,128)(2,1)S(1)} %get-tuple-element.52, bf16[64,4096]{1,0:T(8,128)(2,1)S(1)} %get-tuple-element.51), kind=kOutput, calls=%fused_computation.65 | convolution fusion | flops 2149842944 | bytes 18350080 | tf_op jit(solution)/shard_map/dot_general | solution.py:39
  48.8 8.8 %fusion.35 = bf16[2,32,4096]{2,1,0:T(8,128)(2,1)S(1)} fusion(bf16[2,32,2048]{2,1,0:T(8,128)(2,1)S(1)} %dot_general.130, bf16[1,2048,4096]{2,1,0:T(8,128)(2,1)} %param.16), kind=kOutput, calls=%fused_computation.35 | convolution fusion | flops 1074003968 | bytes 17563648 | tf_op jit(solution)/shard_map/dot_general | solution.py:69
  57.6 8.8 %fusion.38 = bf16[2,32,4096]{2,1,0:T(8,128)(2,1)S(1)} fusion(bf16[2,32,2048]{2,1,0:T(8,128)(2,1)S(1)} %dot_general.132, bf16[1,2048,4096]{2,1,0:T(8,128)(2,1)} %param.16), kind=kOutput, calls=%fused_computation.36 | convolution fusion | flops 1074003968 | bytes 17563648 | tf_op jit(solution)/shard_map/dot_general | solution.py:72
  67.5 9.4 %reduce-scatter.8.cloned.1.call-start = ((), (), s32[]{:S(2)}) async-start(), calls=%async_computation.8 | async-start | bytes 1572864 | tf_op jit(solution)/shard_map/reduce_scatter | solution.py:75
  77.0 12.3 %reduce-scatter.6.cloned.1.call-done = bf16[64,4096]{1,0:T(8,128)(2,1)} async-done(((bf16[128,4096]{1,0:T(8,128)(2,1)}), bf16[64,4096]{1,0:T(8,128)(2,1)}) %reduce-scatter.6.cloned.1.call-update) | async-done | bytes 524304 | tf_op jit(solution)/shard_map/reduce_scatter | solution.py:75
  92.7 8.9 %all_gather.32 = bf16[64,4096]{1,0:T(8,128)(2,1)S(1)} all-gather(bf16[32,4096]{1,0:T(8,128)(2,1)S(1)} %bitcast_select_fusion.9), channel_id=1, replica_groups=mesh['phase'=2,'dp'=8,'mp'=2] {'mp'}, dimensions={0}, use_global_device_ids=true | all-gather | bytes 786432 | tf_op jit(solution)/shard_map/all_gather | solution.py:28
  102.8 8.0 %all_gather.33 = bf16[64,4096]{1,0:T(8,128)(2,1)S(1)} all-gather(bf16[32,4096]{1,0:T(8,128)(2,1)S(1)} %bitcast_select_fusion.8), channel_id=1, replica_groups=mesh['phase'=2,'dp'=8,'mp'=2] {'mp'}, dimensions={0}, use_global_device_ids=true | all-gather | bytes 786432 | tf_op jit(solution)/shard_map/all_gather | solution.py:29
  112.2 8.3 %fusion.88 = bf16[128,2048]{1,0:T(8,128)(2,1)S(1)} fusion(bf16[1,4096,2048]{2,1,0:T(8,128)(2,1)} %param.13, bf16[64,4096]{1,0:T(8,128)(2,1)S(1)} %get-tuple-element.50, bf16[64,4096]{1,0:T(8,128)(2,1)S(1)} %get-tuple-element.49), kind=kOutput, calls=%fused_computation.66 | convolution fusion | flops 2149842944 | bytes 18350080 | tf_op jit(solution)/shard_map/dot_general | solution.py:39
  129.5 8.8 %fusion.41 = bf16[2,32,4096]{2,1,0:T(8,128)(2,1)S(1)} fusion(bf16[2,32,2048]{2,1,0:T(8,128)(2,1)S(1)} %dot_general.139, bf16[1,2048,4096]{2,1,0:T(8,128)(2,1)} %param.16), kind=kOutput, calls=%fused_computation.37 | convolution fusion | flops 1074003968 | bytes 17563648 | tf_op jit(solution)/shard_map/dot_general | solution.py:69
  140.4 8.8 %fusion.44 = bf16[2,32,4096]{2,1,0:T(8,128)(2,1)S(1)} fusion(bf16[2,32,2048]{2,1,0:T(8,128)(2,1)S(1)} %dot_general.141, bf16[1,2048,4096]{2,1,0:T(8,128)(2,1)} %param.16), kind=kOutput, calls=%fused_computation.38 | convolution fusion | flops 1074003968 | bytes 17563648 | tf_op jit(solution)/shard_map/dot_general | solution.py:72
  150.4 20.5 %reduce-scatter.8.cloned.1.call-done = bf16[64,4096]{1,0:T(8,128)(2,1)} async-done(((bf16[128,4096]{1,0:T(8,128)(2,1)}), bf16[64,4096]{1,0:T(8,128)(2,1)}) %reduce-scatter.8.cloned.1.call-update) | async-done | bytes 524304 | tf_op jit(solution)/shard_map/reduce_scatter | solution.py:75
  184.4 9.0 %all_gather.35 = bf16[64,4096]{1,0:T(8,128)(2,1)S(1)} all-gather(bf16[32,4096]{1,0:T(8,128)(2,1)S(1)} %bitcast_select_fusion.6), channel_id=1, replica_groups=mesh['phase'=2,'dp'=8,'mp'=2] {'mp'}, dimensions={0}, use_global_device_ids=true | all-gather | bytes 786432 | tf_op jit(solution)/shard_map/all_gather | solution.py:29
  193.6 36.7 %all-to-all-done = bf16[8,32,4096]{2,1,0:T(8,128)(2,1)S(1)} async-done(((bf16[8,32,4096]{2,1,0:T(8,128)(2,1)}), bf16[8,32,4096]{2,1,0:T(8,128)(2,1)S(1)}, u32[]{:S(2)}, u32[]{:S(2)}) %all-to-all-start) | async-done | bytes 2097184 | tf_op jit(solution)/shard_map/all_to_all | solution.py:95
  230.7 8.1 %all_gather.34 = bf16[64,4096]{1,0:T(8,128)(2,1)S(1)} all-gather(bf16[32,4096]{1,0:T(8,128)(2,1)S(1)} %broadcast_select_fusion.5), channel_id=1, replica_groups=mesh['phase'=2,'dp'=8,'mp'=2] {'mp'}, dimensions={0}, use_global_device_ids=true | all-gather | bytes 786432 | tf_op jit(solution)/shard_map/all_gather | solution.py:28
  240.2 8.3 %fusion.91 = bf16[128,2048]{1,0:T(8,128)(2,1)S(1)} fusion(bf16[1,4096,2048]{2,1,0:T(8,128)(2,1)} %param.13, bf16[64,4096]{1,0:T(8,128)(2,1)S(1)} %get-tuple-element.48, bf16[64,4096]{1,0:T(8,128)(2,1)S(1)} %get-tuple-element.47), kind=kOutput, calls=%fused_computation.67 | convolution fusion | flops 2149842944 | bytes 18350080 | tf_op jit(solution)/shard_map/dot_general | solution.py:39
  251.4 8.8 %fusion.47 = bf16[2,32,4096]{2,1,0:T(8,128)(2,1)S(1)} fusion(bf16[2,32,2048]{2,1,0:T(8,128)(2,1)S(1)} %dot_general.148, bf16[1,2048,4096]{2,1,0:T(8,128)(2,1)} %param.16), kind=kOutput, calls=%fused_computation.39 | convolution fusion | flops 1074003968 | bytes 17563648 | tf_op jit(solution)/shard_map/dot_general | solution.py:69
  260.6 8.8 %fusion.50 = bf16[2,32,4096]{2,1,0:T(8,128)(2,1)S(1)} fusion(bf16[2,32,2048]{2,1,0:T(8,128)(2,1)S(1)} %dot_general.150, bf16[1,2048,4096]{2,1,0:T(8,128)(2,1)} %param.16), kind=kOutput, calls=%fused_computation.40 | convolution fusion | flops 1074003968 | bytes 17563648 | tf_op jit(solution)/shard_map/dot_general | solution.py:72
  272.4 17.6 %reduce-scatter.10.cloned.1.call-done = bf16[64,4096]{1,0:T(8,128)(2,1)} async-done(((bf16[128,4096]{1,0:T(8,128)(2,1)}), bf16[64,4096]{1,0:T(8,128)(2,1)}) %reduce-scatter.10.cloned.1.call-update) | async-done | bytes 524304 | tf_op jit(solution)/shard_map/reduce_scatter | solution.py:75
  303.6 9.0 %all_gather.37 = bf16[64,4096]{1,0:T(8,128)(2,1)S(1)} all-gather(bf16[32,4096]{1,0:T(8,128)(2,1)S(1)} %bitcast_select_fusion.4), channel_id=1, replica_groups=mesh['phase'=2,'dp'=8,'mp'=2] {'mp'}, dimensions={0}, use_global_device_ids=true | all-gather | bytes 786432 | tf_op jit(solution)/shard_map/all_gather | solution.py:29
  312.8 36.5 %all-to-all-done.1 = bf16[8,32,4096]{2,1,0:T(8,128)(2,1)S(1)} async-done(((bf16[8,32,4096]{2,1,0:T(8,128)(2,1)}), bf16[8,32,4096]{2,1,0:T(8,128)(2,1)S(1)}, u32[]{:S(2)}, u32[]{:S(2)}) %all-to-all-start.1) | async-done | bytes 2097184 | tf_op jit(solution)/shard_map/all_to_all | solution.py:95
  360.0 8.3 %fusion.94 = bf16[128,2048]{1,0:T(8,128)(2,1)S(1)} fusion(bf16[1,4096,2048]{2,1,0:T(8,128)(2,1)} %param.13, bf16[64,4096]{1,0:T(8,128)(2,1)S(1)} %get-tuple-element.46, bf16[64,4096]{1,0:T(8,128)(2,1)S(1)} %get-tuple-element.45), kind=kOutput, calls=%fused_computation.68 | convolution fusion | flops 2149842944 | bytes 18350080 | tf_op jit(solution)/shard_map/dot_general | solution.py:39
  371.2 8.8 %fusion.53 = bf16[2,32,4096]{2,1,0:T(8,128)(2,1)S(1)} fusion(bf16[2,32,2048]{2,1,0:T(8,128)(2,1)S(1)} %dot_general.157, bf16[1,2048,4096]{2,1,0:T(8,128)(2,1)} %param.16), kind=kOutput, calls=%fused_computation.41 | convolution fusion | flops 1074003968 | bytes 17563648 | tf_op jit(solution)/shard_map/dot_general | solution.py:69
  380.5 8.9 %fusion.56 = bf16[2,32,4096]{2,1,0:T(8,128)(2,1)S(1)} fusion(bf16[2,32,2048]{2,1,0:T(8,128)(2,1)S(1)} %dot_general.159, bf16[1,2048,4096]{2,1,0:T(8,128)(2,1)} %param.16), kind=kOutput, calls=%fused_computation.42 | convolution fusion | flops 1074003968 | bytes 17563648 | tf_op jit(solution)/shard_map/dot_general | solution.py:72
  390.6 19.3 %reduce-scatter.12.cloned.1.call-done = bf16[64,4096]{1,0:T(8,128)(2,1)} async-done(((bf16[128,4096]{1,0:T(8,128)(2,1)}), bf16[64,4096]{1,0:T(8,128)(2,1)}) %reduce-scatter.12.cloned.1.call-update) | async-done | bytes 524304 | tf_op jit(solution)/shard_map/reduce_scatter | solution.py:75
  413.6 9.2 %all_gather.39 = bf16[64,4096]{1,0:T(8,128)(2,1)S(1)} all-gather(bf16[32,4096]{1,0:T(8,128)(2,1)S(1)} %broadcast_select_fusion.2), channel_id=1, replica_groups=mesh['phase'=2,'dp'=8,'mp'=2] {'mp'}, dimensions={0}, use_global_device_ids=true | all-gather | bytes 786432 | tf_op jit(solution)/shard_map/all_gather | solution.py:29
  423.1 8.2 %all_gather.38 = bf16[64,4096]{1,0:T(8,128)(2,1)S(1)} all-gather(bf16[32,4096]{1,0:T(8,128)(2,1)S(1)} %broadcast_select_fusion.3), channel_id=1, replica_groups=mesh['phase'=2,'dp'=8,'mp'=2] {'mp'}, dimensions={0}, use_global_device_ids=true | all-gather | bytes 786432 | tf_op jit(solution)/shard_map/all_gather | solution.py:28
  432.6 8.3 %fusion.97 = bf16[128,2048]{1,0:T(8,128)(2,1)S(1)} fusion(bf16[1,4096,2048]{2,1,0:T(8,128)(2,1)} %param.13, bf16[64,4096]{1,0:T(8,128)(2,1)S(1)} %get-tuple-element.44, bf16[64,4096]{1,0:T(8,128)(2,1)S(1)} %get-tuple-element.43), kind=kOutput, calls=%fused_computation.69 | convolution fusion | flops 2149842944 | bytes 18350080 | tf_op jit(solution)/shard_map/dot_general | solution.py:39
  446.3 8.8 %fusion.59 = bf16[2,32,4096]{2,1,0:T(8,128)(2,1)S(1)} fusion(bf16[2,32,2048]{2,1,0:T(8,128)(2,1)S(1)} %dot_general.166, bf16[1,2048,4096]{2,1,0:T(8,128)(2,1)} %param.16), kind=kOutput, calls=%fused_computation.43 | convolution fusion | flops 1074003968 | bytes 17563648 | tf_op jit(solution)/shard_map/dot_general | solution.py:69
  455.5 8.8 %fusion.62 = bf16[2,32,4096]{2,1,0:T(8,128)(2,1)S(1)} fusion(bf16[2,32,2048]{2,1,0:T(8,128)(2,1)S(1)} %dot_general.168, bf16[1,2048,4096]{2,1,0:T(8,128)(2,1)} %param.16), kind=kOutput, calls=%fused_computation.44 | convolution fusion | flops 1074003968 | bytes 17563648 | tf_op jit(solution)/shard_map/dot_general | solution.py:72
  465.5 20.5 %reduce-scatter.14.cloned.1.call-done = bf16[64,4096]{1,0:T(8,128)(2,1)} async-done(((bf16[128,4096]{1,0:T(8,128)(2,1)}), bf16[64,4096]{1,0:T(8,128)(2,1)}) %reduce-scatter.14.cloned.1.call-update) | async-done | bytes 524304 | tf_op jit(solution)/shard_map/reduce_scatter | solution.py:75
  (219 shorter events, 99.5 us)
Async XLA Ops:
  7.2 82.1 %reduce-scatter.6.cloned.1.call-start = ((), (), s32[]{:S(2)}) async-start(), calls=%async_computation.7 | async-start | bytes 1572864 | tf_op jit(solution)/shard_map/reduce_scatter | solution.py:75
  7.2 26.4 %copy-start.16 = (bf16[1,4096,512]{2,1,0:T(8,128)(2,1)S(1)}, bf16[1,4096,512]{2,1,0:T(8,128)(2,1)}, u32[]{:S(2)}) copy-start(bf16[1,4096,512]{2,1,0:T(8,128)(2,1)} %param.14) | copy-start | bytes 12582916
  66.4 24.1 %copy-start.6 = (bf16[2,32,4096]{2,1,0:T(8,128)(2,1)S(1)}, bf16[2,32,4096]{2,1,0:T(8,128)(2,1)}, u32[]{:S(2)}) copy-start(bf16[2,32,4096]{2,1,0:T(8,128)(2,1)} %param.10) | copy-start | bytes 1572868
  67.5 103.3 %reduce-scatter.8.cloned.1.call-start = ((), (), s32[]{:S(2)}) async-start(), calls=%async_computation.8 | async-start | bytes 1572864 | tf_op jit(solution)/shard_map/reduce_scatter | solution.py:75
  90.6 20.8 %copy-start.17 = (bf16[1,4096,512]{2,1,0:T(8,128)(2,1)S(1)}, bf16[1,4096,512]{2,1,0:T(8,128)(2,1)}, u32[]{:S(2)}) copy-start(bf16[1,4096,512]{2,1,0:T(8,128)(2,1)} %param.14) | copy-start | bytes 12582916
  90.6 2.0 collective-permute-start
  92.0 9.8 %collective-permute-start.1 = (bf16[32,4096]{1,0:T(8,128)(2,1)S(1)}, bf16[32,4096]{1,0:T(8,128)(2,1)S(1)}, u32[]{:S(2)}, u32[]{:S(2)}) collective-permute-start(bf16[32,4096]{1,0:T(8,128)(2,1)S(1)} %get-tuple-element.16), channel_id=1, source_target_pairs={{0,16},{16,0},{1,17},{17,1},{2,18},{18,2},{3,19},{19,3},{4,20},{20... | collective-permute-start | bytes 786440 | tf_op jit(solution)/shard_map/ppermute | solution.py:15
  112.2 8.4 %copy-start.21 = (bf16[1,4096,512]{2,1,0:T(8,128)(2,1)S(1)}, bf16[1,4096,512]{2,1,0:T(8,128)(2,1)}, u32[]{:S(2)}) copy-start(bf16[1,4096,512]{2,1,0:T(8,128)(2,1)} %param.15) | copy-start | bytes 12582916
  129.5 8.9 %copy-start.7 = (bf16[64,4,4,128]{3,0,2,1:T(8,128)(2,1)S(1)}, bf16[64,4,4,128]{3,0,2,1:T(8,128)(2,1)}, u32[]{:S(2)}) copy-start(bf16[64,4,4,128]{3,0,2,1:T(8,128)(2,1)} %get-tuple-element.40) | copy-start | bytes 786436
  149.2 23.7 %copy-start.15 = (s32[2,8]{1,0:T(2,128)S(1)}, s32[2,8]{1,0:T(2,128)}, u32[]{:S(2)}) copy-start(s32[2,8]{1,0:T(2,128)} %param.12) | copy-start | bytes 196
  172.9 1.7 collective-permute-start.2
  176.2 54.1 %all-to-all-start = ((bf16[8,32,4096]{2,1,0:T(8,128)(2,1)}), bf16[8,32,4096]{2,1,0:T(8,128)(2,1)S(1)}, u32[]{:S(2)}, u32[]{:S(2)}) async-start(bf16[8,32,4096]{2,1,0:T(8,128)(2,1)} %broadcast_select_fusion.1), calls=%async_computation.2 | async-start | bytes 4194304 | tf_op jit(solution)/shard_map/all_to_all | solution.py:95
  181.7 108.3 %reduce-scatter.10.cloned.1.call-start = ((), (), s32[]{:S(2)}) async-start(), calls=%async_computation.9 | async-start | bytes 1572864 | tf_op jit(solution)/shard_map/reduce_scatter | solution.py:75
  181.8 1.6 collective-permute-start.3
  230.7 8.7 %copy-start.18 = (bf16[1,4096,512]{2,1,0:T(8,128)(2,1)S(1)}, bf16[1,4096,512]{2,1,0:T(8,128)(2,1)}, u32[]{:S(2)}) copy-start(bf16[1,4096,512]{2,1,0:T(8,128)(2,1)} %param.14) | copy-start | bytes 12582916
  240.2 8.3 %copy-start.22 = (bf16[1,4096,512]{2,1,0:T(8,128)(2,1)S(1)}, bf16[1,4096,512]{2,1,0:T(8,128)(2,1)}, u32[]{:S(2)}) copy-start(bf16[1,4096,512]{2,1,0:T(8,128)(2,1)} %param.15) | copy-start | bytes 12582916
  292.2 1.5 collective-permute-start.4
  295.3 54.0 %all-to-all-start.1 = ((bf16[8,32,4096]{2,1,0:T(8,128)(2,1)}), bf16[8,32,4096]{2,1,0:T(8,128)(2,1)S(1)}, u32[]{:S(2)}, u32[]{:S(2)}) async-start(bf16[8,32,4096]{2,1,0:T(8,128)(2,1)} %broadcast_select_fusion), calls=%async_computation.4 | async-start | bytes 4194304 | tf_op jit(solution)/shard_map/all_to_all | solution.py:95
  300.8 109.1 %reduce-scatter.12.cloned.1.call-start = ((), (), s32[]{:S(2)}) async-start(), calls=%async_computation.10 | async-start | bytes 1572864 | tf_op jit(solution)/shard_map/reduce_scatter | solution.py:75
  301.0 1.6 collective-permute-start.5
  350.4 8.9 %copy-start.19 = (bf16[1,4096,512]{2,1,0:T(8,128)(2,1)S(1)}, bf16[1,4096,512]{2,1,0:T(8,128)(2,1)}, u32[]{:S(2)}) copy-start(bf16[1,4096,512]{2,1,0:T(8,128)(2,1)} %param.14) | copy-start | bytes 12582916
  360.0 8.3 %copy-start.23 = (bf16[1,4096,512]{2,1,0:T(8,128)(2,1)S(1)}, bf16[1,4096,512]{2,1,0:T(8,128)(2,1)}, u32[]{:S(2)}) copy-start(bf16[1,4096,512]{2,1,0:T(8,128)(2,1)} %param.15) | copy-start | bytes 12582916
  380.4 10.1 %copy-start.4 = (bf16[4,32,4096]{2,1,0:T(8,128)(2,1)S(1)}, bf16[4,32,4096]{2,1,0:T(8,128)(2,1)}, u32[]{:S(2)}) copy-start(bf16[4,32,4096]{2,1,0:T(8,128)(2,1)} %get-tuple-element.29) | copy-start | bytes 3145732
  380.4 10.1 %copy-start.1 = (bf16[4,32,4096]{2,1,0:T(8,128)(2,1)S(1)}, bf16[4,32,4096]{2,1,0:T(8,128)(2,1)}, u32[]{:S(2)}) copy-start(bf16[4,32,4096]{2,1,0:T(8,128)(2,1)} %get-tuple-element.11) | copy-start | bytes 3145732
  390.5 95.5 %reduce-scatter.14.cloned.1.call-start = ((), (), s32[]{:S(2)}) async-start(), calls=%async_computation.11 | async-start | bytes 1572864 | tf_op jit(solution)/shard_map/reduce_scatter | solution.py:75
  411.0 20.8 %copy-start.20 = (bf16[1,4096,512]{2,1,0:T(8,128)(2,1)S(1)}, bf16[1,4096,512]{2,1,0:T(8,128)(2,1)}, u32[]{:S(2)}) copy-start(bf16[1,4096,512]{2,1,0:T(8,128)(2,1)} %param.14) | copy-start | bytes 12582916
  411.2 1.6 collective-permute-start.7
  411.3 11.7 %collective-permute-start.6 = (bf16[32,4096]{1,0:T(8,128)(2,1)S(1)}, bf16[32,4096]{1,0:T(8,128)(2,1)S(1)}, u32[]{:S(2)}, u32[]{:S(2)}) collective-permute-start(bf16[32,4096]{1,0:T(8,128)(2,1)S(1)} %get-tuple-element.28), channel_id=1, source_target_pairs={{0,16},{16,0},{1,17},{17,1},{2,18},{18,2},{3,19},{19,3},{4,20},{20... | collective-permute-start | bytes 786440 | tf_op jit(solution)/shard_map/ppermute | solution.py:15
  423.0 8.4 %copy-start.10 = (bf16[32,4096]{1,0:T(8,128)(2,1)}, bf16[32,4096]{1,0:T(8,128)(2,1)S(1)}, u32[]{:S(2)}) copy-start(bf16[32,4096]{1,0:T(8,128)(2,1)S(1)} %collective-permute-done.6) | copy-start | bytes 786436
  432.6 8.4 %copy-start.24 = (bf16[1,4096,512]{2,1,0:T(8,128)(2,1)S(1)}, bf16[1,4096,512]{2,1,0:T(8,128)(2,1)}, u32[]{:S(2)}) copy-start(bf16[1,4096,512]{2,1,0:T(8,128)(2,1)} %param.15) | copy-start | bytes 12582916
  464.3 22.7 %copy-start.9 = (bf16[32,4096]{1,0:T(8,128)(2,1)S(1)}, bf16[32,4096]{1,0:T(8,128)(2,1)}, u32[]{:S(2)}) copy-start(bf16[32,4096]{1,0:T(8,128)(2,1)} %copy-done.8) | copy-start | bytes 786436
  464.3 22.7 %copy-start.11 = (bf16[32,4096]{1,0:T(8,128)(2,1)S(1)}, bf16[32,4096]{1,0:T(8,128)(2,1)}, u32[]{:S(2)}) copy-start(bf16[32,4096]{1,0:T(8,128)(2,1)} %copy-done.10) | copy-start | bytes 786436
  (8 other events, 13.1 us)
Sparse Core Ops, SparseCore 0:
  67.6 21.6 reduce-scatter.5
  150.4 20.3 reduce-scatter.7
  270.6 19.4 reduce-scatter.9
  390.6 19.2 reduce-scatter.11
  465.5 20.3 reduce-scatter.13
where the time goes:
time: 505 us; the launch traced here: 496 us
  waiting for transfers between devices  169 us (33%)
  matrix products  152 us (30%)
  blocking collectives  85.7 us (17%)
  other arithmetic  37.4 us (7%)
  starting transfers between devices  22.2 us (4%)
  between operations  15.3 us (3%)
  local copies, waits for them, and re-layouts  13.8 us (3%)
    reduce_scatter x5, waiting for transfers between devices, section_layer(): lax.psum_scatter(jnp.concatenate([term_mem, term_seg], axis=1).reshape(bl...  90.2 us
    all_to_all x2, waiting for transfers between devices, route_memory(): lax.all_to_all(outgoing, 'dp', split_axis=0, concat_axis=0, tiled=True)  73.2 us
    all_gather x5, blocking collectives, section_layer(): lax.all_gather(seg_x, 'mp', axis=0, tiled=True)  45.2 us
    dot_general x5, matrix products, section_layer(): jnp.dot(attended_seg, w_out, preferred_element_type=jnp.float32)  44.1 us
    dot_general x5, matrix products, section_layer(): jnp.dot(attended_mem, w_out, preferred_element_type=jnp.float32)  44 us
    dot_general x5, matrix products, section_layer(): jnp.dot(normed, w_query, preferred_element_type=jnp.float32)  41.3 us
    all_gather x5, blocking collectives, section_layer(): lax.all_gather(mem_x, 'mp', axis=0, tiled=True)  40.5 us
    all_to_all x2, starting transfers between devices, route_memory(): lax.all_to_all(outgoing, 'dp', split_axis=0, concat_axis=0, tiled=True)  11 us
  transfers between devices with their start and end apart: 15, of which 12 were waited for; matrix products, arithmetic and copies ran while one was open for 2% of the time, Pallas kernels for 0%

commit v1 on v0

v1 whole, which is shorter than its diff:
```python
import functools

import jax
import jax.numpy as jnp
from jax import lax
from jax.experimental import pallas as pl
from jax.experimental.pallas import tpu as pltpu
from jax.sharding import PartitionSpec as P


HEAD_SIZE = 128
EPSILON = 1e-05
TILE = 512
AXES = ("phase", "dp", "mp")
VMEM_SMALL = 16 << 20


ANY = pl.BlockSpec(memory_space=pl.ANY)
VMEM = pl.BlockSpec(memory_space=pltpu.VMEM)
SMEM = pl.BlockSpec(memory_space=pltpu.SMEM)
HBM = pl.BlockSpec(memory_space=pltpu.HBM)
BF16 = jnp.bfloat16
F32 = jnp.float32


def rows_of(count, width):
    return jax.ShapeDtypeStruct((count, width), BF16)


def column(j):
    return pl.ds(pl.multiple_of(j * TILE, TILE), TILE)


def out_tile(weights, first, q_dim, j):
    per_slab = weights.shape[1] // q_dim
    return weights.at[first + j // per_slab, pl.ds(pl.multiple_of(j % per_slab * q_dim, q_dim), q_dim)]


def load_kernel(w_query, w_key, value_weight, weights, sem):
    copies = []
    for source in (w_query, w_key, value_weight):
        for j in range(source.shape[1] // TILE):
            n = len(copies)
            copies.append(
                pltpu.make_async_copy(source.at[:, pl.ds(j * TILE, TILE)], weights.at[n], sem.at[n])
            )
    for copy in copies:
        copy.start()
    for copy in copies:
        copy.wait()


def load_weights(w_query, w_key, value_weight, w_out):
    width = w_query.shape[0]
    tiles = (w_query.shape[1] + w_key.shape[1] + value_weight.shape[1]) // TILE
    slabs = tiles + w_out.shape[0] * w_out.shape[1] // (width * TILE)
    return pl.pallas_call(
        load_kernel,
        out_shape=pltpu.VMEM((slabs, width, TILE), BF16),
        in_specs=[HBM] * 3,
        out_specs=VMEM,
        scratch_shapes=[pltpu.SemaphoreType.DMA((tiles,))],
        compiler_params=pltpu.CompilerParams(vmem_limit_bytes=VMEM_SMALL),
        cost_estimate=pl.CostEstimate(
            flops=0, bytes_accessed=2 * tiles * TILE * width, transcendentals=0
        ),
        name="load_weights",
    )(w_query, w_key, value_weight)


def section_kernel(cfg, plan, lengths, gain, *refs):
    round_index, slot, want, load, spots, q_tiles, k_tiles, half, ns = cfg
    refs = list(refs)
    blocks = [refs.pop(0) for _ in range(1 + max(s[0] for s in spots))]
    weights = refs.pop(0)
    w_out_in = refs.pop(0) if load else None
    if want:
        own_term, peer_term, x_own = [refs.pop(0) for _ in range(3)]
    else:
        term_out = refs.pop(0)
    if load:
        refs.pop(0)
    x, normed, qkv, attended = [refs.pop(0) for _ in range(4)]
    t_other = refs.pop(0) if want else None
    sem_in = refs.pop(0)
    sem_out = refs.pop(0) if load else None
    qkv_tiles, out_tiles = q_tiles + 2 * k_tiles, weights.shape[1] // TILE
    rows, q_dim = attended.shape
    nm = half - ns

    def in_copies():
        copies = []
        for n, (ref, index, first, to_other, at, size) in enumerate(spots):
            source = blocks[ref]
            if index:
                source = source.at[index]
            target = t_other if to_other else x
            copies.append(
                pltpu.make_async_copy(
                    source.at[pl.ds(first, size)], target.at[pl.ds(at, size)], sem_in.at[n]
                )
            )
        return copies

    def out_copy(j):
        return pltpu.make_async_copy(w_out_in.at[:, column(j)], out_tile(weights, qkv_tiles, q_dim, j), sem_out.at[j])

    active = plan[0] == want

    @pl.when(active)
    def _():
        for copy in in_copies():
            copy.start()

    if load:
        for j in range(out_tiles):
            out_copy(j).start()

    @pl.when(active)
    def _():
        for copy in in_copies():
            copy.wait()
        step = 16

        @pl.loop(0, rows // step)
        def _(b):
            at = pl.ds(pl.multiple_of(b * step, step), step)
            values = x[at, :].astype(F32)
            if want:
                rounded = (values + t_other[at, :].astype(F32)).astype(BF16)

                @pl.when(b * step < half)
                def _():
                    x_own[at, :] = rounded

                values = rounded.astype(F32)
            scale = lax.rsqrt(jnp.mean(values * values, axis=-1, keepdims=True) + EPSILON)
            normed[at, :] = (values * scale * gain[...].astype(F32)).astype(BF16)

        @pl.loop(0, qkv_tiles // 2)
        def _(pair):
            for u in range(2):
                j = pair * 2 + u
                qkv[j] = jnp.dot(normed[...], weights[j], preferred_element_type=F32).astype(BF16)

        mp = plan[1]
        length = lengths[round_index, slot]

        def place(axis):
            at = lax.broadcasted_iota(jnp.int32, (rows, rows), axis)
            inside = lax.rem(at, half)
            owner = jnp.where(at < half, mp, 1 - mp)
            return inside < nm, inside - nm + owner * ns

        query_mem, query_seg = place(0)
        key_mem, key_seg = place(1)
        visible = key_mem | (key_seg < length) & (query_mem | (key_seg <= query_seg))
        kv_heads = k_tiles * TILE // HEAD_SIZE
        per_group = (q_tiles * TILE // HEAD_SIZE) // kv_heads
        visible = jnp.concatenate([visible] * per_group, axis=0)

        def head(base, h):
            lane = (h * HEAD_SIZE) % TILE
            return qkv[base + h * HEAD_SIZE // TILE, :, lane : lane + HEAD_SIZE]

        for c in range(kv_heads):
            heads = [c * per_group + n for n in range(per_group)]
            queries = jnp.concatenate([head(0, h) for h in heads], axis=0)
            scores = lax.dot_general(
                queries, head(q_tiles, c), (((1,), (1,)), ((), ())), preferred_element_type=F32
            ) * HEAD_SIZE ** (-0.5)
            scores = jnp.where(visible, scores, -1e30)
            exponent = jnp.exp(scores - jnp.max(scores, axis=-1, keepdims=True))
            attn = (exponent / jnp.sum(exponent, axis=-1, keepdims=True)).astype(BF16)
            result = jnp.dot(attn, head(q_tiles + k_tiles, c), preferred_element_type=F32)
            for n, h in enumerate(heads):
                attended[:, h * HEAD_SIZE : (h + 1) * HEAD_SIZE] = result[
                    n * rows : (n + 1) * rows
                ].astype(BF16)

        @pl.loop(0, out_tiles // 2)
        def _(pair):
            for u in range(2):
                j = pair * 2 + u
                if load:
                    out_copy(j).wait()
                term = jnp.dot(
                    attended[...],
                    out_tile(weights, qkv_tiles, q_dim, j)[...],
                    preferred_element_type=F32,
                ).astype(BF16)
                if want:
                    own_term[:, column(j)] = term[:half]
                    peer_term[:, column(j)] = term[half:]
                else:
                    own = x[:half, column(j)].astype(F32) + term[:half].astype(F32)
                    term_out[:half, column(j)] = own.astype(BF16)
                    term_out[half:, column(j)] = term[half:]

    if load:

        @pl.when(jnp.logical_not(active))
        def _():
            for j in range(out_tiles):
                out_copy(j).wait()


def section(plan, lengths, gain, blocks, spots, weights, w_out, dims, round_index, slot, want):
    q_tiles, k_tiles, half, ns = dims
    load = w_out is not None
    width = weights.shape[1]
    rows, q_dim, qkv_tiles = 2 * half, q_tiles * TILE, q_tiles + 2 * k_tiles
    weights = pltpu.with_memory_space_constraint(weights, pltpu.VMEM)
    if want:
        out_shape = [rows_of(half, width)] * 3
    else:
        out_shape = [rows_of(rows, width)]
    aliases = {}
    if load:
        aliases[3 + len(blocks)] = len(out_shape)
        out_shape.append(pltpu.VMEM(weights.shape, BF16))
    scratch = [
        pltpu.VMEM((rows, width), BF16),
        pltpu.VMEM((rows, width), BF16),
        pltpu.VMEM((qkv_tiles, rows, TILE), BF16),
        pltpu.VMEM((rows, q_dim), BF16),
    ]
    if want:
        scratch.append(pltpu.VMEM((rows, width), BF16))
    scratch.append(pltpu.SemaphoreType.DMA((len(spots),)))
    if load:
        scratch.append(pltpu.SemaphoreType.DMA((width // TILE,)))
    return pl.pallas_call(
        functools.partial(
            section_kernel,
            (round_index, slot, want, load, tuple(spots), q_tiles, k_tiles, half, ns),
        ),
        out_shape=out_shape,
        in_specs=[SMEM, SMEM, VMEM] + [ANY] * len(blocks) + [VMEM] + [HBM] * load,
        out_specs=[VMEM] * len(out_shape),
        scratch_shapes=scratch,
        input_output_aliases=aliases,
        compiler_params=pltpu.CompilerParams(vmem_limit_bytes=VMEM_SMALL),
        cost_estimate=pl.CostEstimate(
            flops=2 * rows * width * (qkv_tiles * TILE + q_dim),
            bytes_accessed=2 * width * (qkv_tiles * TILE + q_dim),
            transcendentals=0,
        ),
    )(plan, lengths, gain, *blocks, weights, *([w_out] if load else []))


def pick_kernel(entries, count, plan, *refs):
    sources, targets, sem = refs[:count], refs[count:-1], refs[-1]

    @pl.when(plan[0] == 1)
    def _():
        for t, (target, entry) in enumerate(zip(targets, entries)):
            for n, source in enumerate(sources):

                @pl.when(plan[entry] == n)
                def _(source=source, target=target, t=t):
                    pltpu.make_async_copy(source, target, sem.at[t]).start()

        for t, target in enumerate(targets):
            pltpu.make_async_copy(sources[0], target, sem.at[t]).wait()


def pick(plan, entries, sources):
    shape = jax.ShapeDtypeStruct(sources[0].shape, sources[0].dtype)
    return pl.pallas_call(
        functools.partial(pick_kernel, tuple(entries), len(sources)),
        out_shape=[shape] * len(entries),
        in_specs=[SMEM] + [ANY] * len(sources),
        out_specs=[VMEM] * len(entries),
        scratch_shapes=[pltpu.SemaphoreType.DMA((len(entries),))],
        compiler_params=pltpu.CompilerParams(vmem_limit_bytes=4 << 20),
        name="pick",
    )(plan, *sources)


def finish_kernel(cfg, plan, x_own, own_term, arrived, back, *refs):
    round_index, slot, nm = cfg
    out_mem, out_seg, rows, term, other, sem = refs[-6:]
    half = rows.shape[0]

    def load(n, source, target):
        return pltpu.make_async_copy(source, target, sem.at[n])

    @pl.when(plan[0] == 0)
    def _():
        copy = load(0, back, rows)
        copy.start()
        copy.wait()

    @pl.when(plan[0] != 0)
    def _():
        copies = [load(0, x_own, rows), load(1, own_term, term), load(2, arrived, other)]
        for copy in copies:
            copy.start()
        for copy in copies:
            copy.wait()
        step = 16

        @pl.loop(0, half // step)
        def _(b):
            at = pl.ds(pl.multiple_of(b * step, step), step)
            added = term[at, :].astype(F32) + other[at, :].astype(F32)
            rows[at, :] = (rows[at, :].astype(F32) + added).astype(BF16)

    copies = [
        load(0, rows.at[pl.ds(0, nm)], out_mem.at[0, round_index, slot]),
        load(1, rows.at[pl.ds(nm, half - nm)], out_seg.at[0, round_index, slot]),
    ]
    for copy in copies:
        copy.start()
    for copy in copies:
        copy.wait()


def finish(plan, values, outs, shapes, round_index, slot, nm):
    half, width = values[0].shape
    return pl.pallas_call(
        functools.partial(finish_kernel, (round_index, slot, nm)),
        out_shape=[jax.ShapeDtypeStruct(shape, BF16) for shape in shapes],
        in_specs=[SMEM] + [ANY] * (4 + len(outs)),
        out_specs=[HBM] * 2,
        scratch_shapes=[pltpu.VMEM((half, width), BF16)] * 3 + [pltpu.SemaphoreType.DMA((3,))],
        input_output_aliases={5 + n: n for n in range(len(outs))},
        compiler_params=pltpu.CompilerParams(vmem_limit_bytes=4 << 20),
    )(plan, *values, *outs)


def per_device(
    segments, memory_in, seg_lengths, routes, w_query, w_key, value_weight, w_out, norm_gain
):
    rounds, slots = segments.shape[0], segments.shape[1]
    nm, ns = memory_in.shape[1], segments.shape[2]
    half = nm + ns
    groups = lax.axis_size("dp")
    phase, group, mp = (lax.axis_index(a) for a in AXES)
    inner = 2 if groups % 2 == 0 else 1
    outer = groups // inner

    def flat(p, g, i):
        return (p * groups + g) * 2 + i

    def send(value, pairs_of):
        pairs = [pair for g in range(groups) for i in range(2) for pair in pairs_of(g, i)]
        return lax.ppermute(value, AXES, pairs)

    def within(p):
        return lambda g, i: [(flat(p, g, i), flat(p, g, 1 - i))]

    def across(p, flip):
        return lambda g, i: [(flat(p, g, i), flat(1 - p, g, 1 - i if flip else i))]

    def along(step_outer, step_inner):
        def pairs(g, i):
            o, n = divmod(g, inner)
            target = (o + step_outer) % outer * inner + (n + step_inner) % inner
            return [(flat(1, g, i), flat(1, target, i))]

        return pairs

    ids = jnp.arange(groups, dtype=jnp.int32)
    mine_o, mine_n = group // inner, group % inner
    targets = mine_o * inner + (mine_n + jnp.arange(inner, dtype=jnp.int32)) % inner
    hit = routes[:, None, :] == targets[None, :, None]
    source = jnp.sum(jnp.where(hit, ids[None, None, :], 0), axis=-1)
    hops = (mine_o - source // inner + outer) % outer
    side = (mine_n - source[:, :1] % inner + inner) % inner
    entries = 1 + inner
    plan = jnp.concatenate(
        [
            jnp.stack([phase, mp]).astype(jnp.int32),
            jnp.concatenate([hops, side], axis=1).reshape(slots * entries),
        ]
    )

    def route(m, rows):
        base = 2 + m * entries
        held = [rows] + [send(rows, along(k, 0)) for k in range(1, outer)]
        picked = pick(plan, [base + k for k in range(inner)], held)
        if inner == 1:
            return picked[0]
        arrived = [send(picked[k], along(0, k)) for k in range(1, inner)]
        return pick(plan, [base + inner], [picked[0]] + arrived)[0]

    def gather_rows(m):
        rows = jnp.concatenate([memory_in[m], segments[0, m]], axis=0)
        return send(rows, within(0))

    weights = load_weights(w_query[0], w_key[0], value_weight[0], w_out[0])
    dims = (w_query.shape[2] // TILE, w_key.shape[2] // TILE, half, ns)
    first_peer = [gather_rows(m) for m in range(slots)]
    later_peer = send(segments[1:], within(0)) if rounds > 1 else None
    mem_own = mem_peer = None
    shapes = [(1, rounds, slots, n) + memory_in.shape[2:] for n in (nm, ns)]
    outs = []
    for r in range(rounds):
        sent = []
        for m in range(slots):
            if r == 0:
                blocks = [memory_in, segments, first_peer[m]]
                spots = [
                    (0, (m,), 0, False, 0, nm),
                    (1, (0, m), 0, False, nm, ns),
                    (2, (), 0, False, half, half),
                ]
            else:
                blocks = [mem_own[m], segments, mem_peer[m], later_peer]
                spots = [
                    (0, (), 0, False, 0, nm),
                    (1, (r, m), 0, False, nm, ns),
                    (2, (), 0, False, half, nm),
                    (3, (r - 1, m), 0, False, half + nm, ns),
                ]
            last = w_out[0] if r == 0 and m == 0 else None
            result = section(
                plan, seg_lengths, norm_gain, blocks, spots, weights, last, dims, r, m, 0
            )
            if len(result) == 2:
                weights = result[1]
            other = send(result[0], across(0, True))
            kept = send(result[0], across(0, False))
            sent.append((kept, other))
        spots = [
            (0, (), 0, False, 0, 2 * half),
            (1, (), half, True, 0, half),
            (1, (), 0, True, half, half),
        ]
        next_own, next_peer = [], []
        for m in range(slots):
            own_term, peer_term, x_own = section(
                plan, seg_lengths, norm_gain, sent[m], spots, weights, None, dims, r, m, 1
            )
            arrived = send(peer_term, within(1))
            back = send(x_own, across(1, False))
            if r + 1 < rounds:
                new_mem = (
                    x_own[:nm].astype(F32)
                    + (own_term[:nm].astype(F32) + arrived[:nm].astype(F32))
                ).astype(BF16)
                routed = route(m, new_mem)
                next_peer.append(send(routed, across(1, True)))
                next_own.append(send(routed, across(1, False)))
            outs = finish(plan, (x_own, own_term, arrived, back), outs, shapes, r, m, nm)
        mem_own, mem_peer = next_own, next_peer
    return tuple(outs)


def solution(mesh):
    specs = (
        P(None, "dp", "mp", None),
        P("dp", "mp", None),
        P(None, "dp"),
        P(),
        P("phase", None, "mp"),
        P("phase", None, "mp"),
        P("phase", None, "mp"),
        P("phase", "mp", None),
        P("phase", None),
    )
    out_specs = (P("phase", None, "dp", "mp", None), P("phase", None, "dp", "mp", None))
    step = jax.shard_map(
        per_device, mesh=mesh, in_specs=specs, out_specs=out_specs, check_vma=False
    )

    def run(segments, memory_in, *rest):
        whole = step
        return whole(segments, memory_in, *rest)

    return run
```

time: 505 us -> 212 us (0.42)
  the two profiles are of different devices: /device:TPU:0 before, /device:TPU:1 now
where the time goes in v1:
time: 212 us; the launch traced here: 210 us
  Pallas kernels  82.1 us (39%)
  starting transfers between devices  81.7 us (39%)
  waiting for transfers between devices  29 us (14%)
  local copies, waits for them, and re-layouts  12.8 us (6%)
  other arithmetic  2.93 us (1%)
    ppermute x31, starting transfers between devices, send(): return lax.ppermute(value, AXES, pairs)  81.7 us
    pallas_call x8, Pallas kernels, section(): pl.pallas_call(functools.partial(section_kernel, (round_index, slot, want...  64.5 us
    ppermute x31, waiting for transfers between devices, send(): return lax.ppermute(value, AXES, pairs)  29 us
    unnamed x50, local copies, waits for them, and re-layouts  10.6 us
    pallas_call x1, Pallas kernels, load_weights(): pl.pallas_call(load_kernel, out_shape=pltpu.VMEM((slabs, width, TILE), BF...  8.36 us
    pallas_call x4, Pallas kernels, finish(): pl.pallas_call(functools.partial(finish_kernel, (round_index, slot, nm)),...  6.76 us
  transfers between devices with their start and end apart: 31, of which 6 were waited for; matrix products, arithmetic and copies ran while one was open for 1% of the time, Pallas kernels for 38%

profile of v1, /device:TPU:1, one launch (start us, length us, event | category | flops | bytes accessed | tf_op | source)
XLA Modules:
  0.0 210.2 jit_solution(12897814313166660415)
XLA Ops:
  5.4 8.4 %load_weights.1.refs_3_ = bf16[10,4096,512]{2,1,0:T(8,128)(2,1)S(1)} custom-call(bf16[4096,2048]{1,0:T(8,128)(2,1)} %bitcast.14, bf16[4096,512]{1,0:T(8,128)(2,1)} %bitcast.16, bf16[4096,512]{1,0:T(8,128)(2,1)} %bitcast.17), custom_call_target="tpu_custom_call" | custom-call | bytes 25165824 | tf_op jit(solution)/shard_map/load_weights/pallas_call | solution.py:57
  15.2 7.8 %shard_map.104 = (bf16[128,4096]{1,0:T(8,128)(2,1)}, bf16[10,4096,512]{2,1,0:T(8,128)(2,1)S(1)}) custom-call(s32[8]{0:T(128)} %pad_add_fusion.1.plan, s32[2,2]{1,0:T(2,128)} %lengths.15, bf16[1,4096]{1,0:T(2,128)(2,1)} %gain.15, bf16[2,32,4096]{2,1,0:T(8,128)(2,1)} %refs_0_.3, bf16[2,2,32,4096]{3,2,1,0:T(8,128)(2,1)} %refs_1_.7, ...), custom_call_target="tpu_custom_call", output_to_operand_aliasing={{1}: (6, {})} | custom-call | flops 5368709120 | bytes 41943040 | tf_op jit(solution)/shard_map/pallas_call | solution.py:233
  26.4 1.7 shard_map.105
  30.7 11.3 %collective-permute-done.16.refs_0_ = bf16[128,4096]{1,0:T(8,128)(2,1)S(1)} collective-permute-done((bf16[128,4096]{1,0:T(8,128)(2,1)}, bf16[128,4096]{1,0:T(8,128)(2,1)S(1)}, u32[]{:S(2)}, u32[]{:S(2)}) %collective-permute-start.16) | collective-permute-done | bytes 1048608 | tf_op jit(solution)/shard_map/ppermute | solution.py:349
  42.0 13.3 %collective-permute-done.17.refs_1_ = bf16[128,4096]{1,0:T(8,128)(2,1)S(1)} collective-permute-done((bf16[128,4096]{1,0:T(8,128)(2,1)}, bf16[128,4096]{1,0:T(8,128)(2,1)S(1)}, u32[]{:S(2)}, u32[]{:S(2)}) %collective-permute-start.17) | collective-permute-done | bytes 1048608 | tf_op jit(solution)/shard_map/ppermute | solution.py:349
  56.3 12.8 %shard_map.109 = (bf16[64,4096]{1,0:T(8,128)(2,1)}, bf16[64,4096]{1,0:T(8,128)(2,1)}, bf16[64,4096]{1,0:T(8,128)(2,1)}) custom-call(s32[8]{0:T(128)} %pad_add_fusion.1.plan, s32[2,2]{1,0:T(2,128)} %lengths.15, bf16[1,4096]{1,0:T(2,128)(2,1)} %gain.15, bf16[128,4096]{1,0:T(8,128)(2,1)} %copy-done.16, bf16[128,4096]{1,0:T(8,128)(2,1)} %copy-done.18, ...), custom_call_target="tpu_custom_call" | custom-call | flops 5368709120 | bytes 41943040 | tf_op jit(solution)/shard_map/pallas_call | solution.py:233
  69.1 2.1 collective-permute-start.18
  73.1 12.9 %shard_map.106 = (bf16[64,4096]{1,0:T(8,128)(2,1)}, bf16[64,4096]{1,0:T(8,128)(2,1)}, bf16[64,4096]{1,0:T(8,128)(2,1)}) custom-call(s32[8]{0:T(128)} %pad_add_fusion.1.plan, s32[2,2]{1,0:T(2,128)} %lengths.15, bf16[1,4096]{1,0:T(2,128)(2,1)} %gain.15, bf16[128,4096]{1,0:T(8,128)(2,1)} %copy-done.15, bf16[128,4096]{1,0:T(8,128)(2,1)} %copy-done.17, ...), custom_call_target="tpu_custom_call" | custom-call | flops 5368709120 | bytes 41943040 | tf_op jit(solution)/shard_map/pallas_call | solution.py:233
  86.1 3.4 %collective-permute-start.4 = (bf16[64,4096]{1,0:T(8,128)(2,1)}, bf16[64,4096]{1,0:T(8,128)(2,1)S(1)}, u32[]{:S(2)}, u32[]{:S(2)}) collective-permute-start(bf16[64,4096]{1,0:T(8,128)(2,1)} %get-tuple-element.29), channel_id=1, source_target_pairs={{16,17},{17,16},{18,19},{19,18},{20,21},{21,20},{22,23},{23,22},{2... | collective-permute-start | bytes 1572872 | tf_op jit(solution)/shard_map/ppermute | solution.py:349
  89.6 3.2 %collective-permute-start.19 = (bf16[32,4096]{1,0:T(8,128)(2,1)S(1)}, bf16[32,4096]{1,0:T(8,128)(2,1)S(1)}, u32[]{:S(2)}, u32[]{:S(2)}) collective-permute-start(bf16[32,4096]{1,0:T(8,128)(2,1)S(1)} %add_convert_fusion.refs_0_), channel_id=1, source_target_pairs={{16,20},{17,21},{18,22},{19,23},{20,24},{21,25},{22,26},{23,27},{2... | collective-permute-start | bytes 786440 | tf_op jit(solution)/shard_map/ppermute | solution.py:349
  92.8 4.2 %collective-permute-start.20 = (bf16[32,4096]{1,0:T(8,128)(2,1)S(1)}, bf16[32,4096]{1,0:T(8,128)(2,1)S(1)}, u32[]{:S(2)}, u32[]{:S(2)}) collective-permute-start(bf16[32,4096]{1,0:T(8,128)(2,1)S(1)} %add_convert_fusion.refs_0_), channel_id=1, source_target_pairs={{16,24},{17,25},{18,26},{19,27},{20,28},{21,29},{22,30},{23,31},{2... | collective-permute-start | bytes 786440 | tf_op jit(solution)/shard_map/ppermute | solution.py:349
  97.0 3.0 %collective-permute-start.21 = (bf16[32,4096]{1,0:T(8,128)(2,1)S(1)}, bf16[32,4096]{1,0:T(8,128)(2,1)S(1)}, u32[]{:S(2)}, u32[]{:S(2)}) collective-permute-start(bf16[32,4096]{1,0:T(8,128)(2,1)S(1)} %add_convert_fusion.refs_0_), channel_id=1, source_target_pairs={{16,28},{17,29},{18,30},{19,31},{20,16},{21,17},{22,18},{23,19},{2... | collective-permute-start | bytes 786440 | tf_op jit(solution)/shard_map/ppermute | solution.py:349
  101.1 2.3 %collective-permute-start.5 = (bf16[32,4096]{1,0:T(8,128)(2,1)S(1)}, bf16[32,4096]{1,0:T(8,128)(2,1)S(1)}, u32[]{:S(2)}, u32[]{:S(2)}) collective-permute-start(bf16[32,4096]{1,0:T(8,128)(2,1)S(1)} %add_convert_fusion.1.refs_0_), channel_id=1, source_target_pairs={{16,20},{17,21},{18,22},{19,23},{20,24},{21,25},{22,26},{23,27},{2... | collective-permute-start | bytes 786440 | tf_op jit(solution)/shard_map/ppermute | solution.py:349
  103.5 2.0 collective-permute-start.6
  105.4 4.7 %collective-permute-start.7 = (bf16[32,4096]{1,0:T(8,128)(2,1)S(1)}, bf16[32,4096]{1,0:T(8,128)(2,1)S(1)}, u32[]{:S(2)}, u32[]{:S(2)}) collective-permute-start(bf16[32,4096]{1,0:T(8,128)(2,1)S(1)} %add_convert_fusion.1.refs_0_), channel_id=1, source_target_pairs={{16,28},{17,29},{18,30},{19,31},{20,16},{21,17},{22,18},{23,19},{2... | collective-permute-start | bytes 786440 | tf_op jit(solution)/shard_map/ppermute | solution.py:349
  110.9 3.1 %collective-permute-start.22 = (bf16[32,4096]{1,0:T(8,128)(2,1)S(1)}, bf16[32,4096]{1,0:T(8,128)(2,1)S(1)}, u32[]{:S(2)}, u32[]{:S(2)}) collective-permute-start(bf16[32,4096]{1,0:T(8,128)(2,1)S(1)} %get-tuple-element.40), channel_id=1, source_target_pairs={{16,18},{17,19},{18,16},{19,17},{20,22},{21,23},{22,20},{23,21},{2... | collective-permute-start | bytes 786440 | tf_op jit(solution)/shard_map/ppermute | solution.py:349
  117.6 3.1 %collective-permute-start.8 = (bf16[32,4096]{1,0:T(8,128)(2,1)S(1)}, bf16[32,4096]{1,0:T(8,128)(2,1)S(1)}, u32[]{:S(2)}, u32[]{:S(2)}) collective-permute-start(bf16[32,4096]{1,0:T(8,128)(2,1)S(1)} %get-tuple-element.31), channel_id=1, source_target_pairs={{16,18},{17,19},{18,16},{19,17},{20,22},{21,23},{22,20},{23,21},{2... | collective-permute-start | bytes 786440 | tf_op jit(solution)/shard_map/ppermute | solution.py:349
  129.5 1.7 shard_map.110
  131.3 1.4 collective-permute-start.25
  135.5 1.7 shard_map.107
  139.8 23.3 %collective-permute-start.29 = (bf16[64,4096]{1,0:T(8,128)(2,1)S(1)}, bf16[64,4096]{1,0:T(8,128)(2,1)S(1)}, u32[]{:S(2)}, u32[]{:S(2)}) collective-permute-start(bf16[64,4096]{1,0:T(8,128)(2,1)S(1)} %copy-done.3), channel_id=1, source_target_pairs={{16,0},{17,1},{18,2},{19,3},{20,4},{21,5},{22,6},{23,7},{24,8},{25... | collective-permute-start | bytes 1572872 | tf_op jit(solution)/shard_map/ppermute | solution.py:349
  163.2 1.3 collective-permute-start.30
  165.5 13.0 %shard_map.111 = (bf16[64,4096]{1,0:T(8,128)(2,1)}, bf16[64,4096]{1,0:T(8,128)(2,1)}, bf16[64,4096]{1,0:T(8,128)(2,1)}) custom-call(s32[8]{0:T(128)} %pad_add_fusion.1.plan, s32[2,2]{1,0:T(2,128)} %lengths.15, bf16[1,4096]{1,0:T(2,128)(2,1)} %gain.15, bf16[128,4096]{1,0:T(8,128)(2,1)} %copy-done.13, bf16[128,4096]{1,0:T(8,128)(2,1)} %copy-done.14, ...), custom_call_target="tpu_custom_call" | custom-call | flops 5368709120 | bytes 41943040 | tf_op jit(solution)/shard_map/pallas_call | solution.py:233
  178.5 3.1 %collective-permute-start.27 = (bf16[64,4096]{1,0:T(8,128)(2,1)}, bf16[64,4096]{1,0:T(8,128)(2,1)S(1)}, u32[]{:S(2)}, u32[]{:S(2)}) collective-permute-start(bf16[64,4096]{1,0:T(8,128)(2,1)} %get-tuple-element.43), channel_id=1, source_target_pairs={{16,17},{17,16},{18,19},{19,18},{20,21},{21,20},{22,23},{23,22},{2... | collective-permute-start | bytes 1572872 | tf_op jit(solution)/shard_map/ppermute | solution.py:349
  181.7 1.6 collective-permute-start.28
  183.3 12.8 %shard_map.108 = (bf16[64,4096]{1,0:T(8,128)(2,1)}, bf16[64,4096]{1,0:T(8,128)(2,1)}, bf16[64,4096]{1,0:T(8,128)(2,1)}) custom-call(s32[8]{0:T(128)} %pad_add_fusion.1.plan, s32[2,2]{1,0:T(2,128)} %lengths.15, bf16[1,4096]{1,0:T(2,128)(2,1)} %gain.15, bf16[128,4096]{1,0:T(8,128)(2,1)} %copy-done.12, bf16[128,4096]{1,0:T(8,128)(2,1)} %collective-permute-done.13.refs_1_, ...), custom_call_target="tpu_custom_call" | custom-call | flops 5368709120 | bytes 41943040 | tf_op jit(solution)/shard_map/pallas_call | solution.py:233
  196.1 2.2 %collective-permute-start.14 = (bf16[64,4096]{1,0:T(8,128)(2,1)}, bf16[64,4096]{1,0:T(8,128)(2,1)S(1)}, u32[]{:S(2)}, u32[]{:S(2)}) collective-permute-start(bf16[64,4096]{1,0:T(8,128)(2,1)} %get-tuple-element.34), channel_id=1, source_target_pairs={{16,17},{17,16},{18,19},{19,18},{20,21},{21,20},{22,23},{23,22},{2... | collective-permute-start | bytes 1572872 | tf_op jit(solution)/shard_map/ppermute | solution.py:349
  199.6 1.7 shard_map.112
  201.3 1.7 shard_map.113
  203.1 1.7 shard_map.114
  204.8 1.4 collective-permute-done.14.arrived
  208.3 1.7 shard_map.115
  (111 shorter events, 38.8 us)
Async XLA Ops:
  2.8 22.7 %collective-permute-start = (bf16[64,4096]{1,0:T(8,128)(2,1)S(1)}, bf16[64,4096]{1,0:T(8,128)(2,1)S(1)}, u32[]{:S(2)}, u32[]{:S(2)}) collective-permute-start(bf16[64,4096]{1,0:T(8,128)(2,1)S(1)} %pad_maximum_fusion), channel_id=1, source_target_pairs={{0,1},{1,0},{2,3},{3,2},{4,5},{5,4},{6,7},{7,6},{8,9},{9,8},{10,11... | collective-permute-start | bytes 1572872 | tf_op jit(solution)/shard_map/ppermute | solution.py:349
  3.6 10.8 %collective-permute-start.1 = (bf16[64,4096]{1,0:T(8,128)(2,1)S(1)}, bf16[64,4096]{1,0:T(8,128)(2,1)S(1)}, u32[]{:S(2)}, u32[]{:S(2)}) collective-permute-start(bf16[64,4096]{1,0:T(8,128)(2,1)S(1)} %pad_maximum_fusion.1), channel_id=1, source_target_pairs={{0,1},{1,0},{2,3},{3,2},{4,5},{5,4},{6,7},{7,6},{8,9},{9,8},{10,11... | collective-permute-start | bytes 1572872 | tf_op jit(solution)/shard_map/ppermute | solution.py:349
  22.9 19.1 %collective-permute-start.16 = (bf16[128,4096]{1,0:T(8,128)(2,1)}, bf16[128,4096]{1,0:T(8,128)(2,1)S(1)}, u32[]{:S(2)}, u32[]{:S(2)}) collective-permute-start(bf16[128,4096]{1,0:T(8,128)(2,1)} %get-tuple-element.35), channel_id=1, source_target_pairs={{0,16},{1,17},{2,18},{3,19},{4,20},{5,21},{6,22},{7,23},{8,24},{9,... | collective-permute-start | bytes 3145736 | tf_op jit(solution)/shard_map/ppermute | solution.py:349
  24.2 31.1 %collective-permute-start.17 = (bf16[128,4096]{1,0:T(8,128)(2,1)}, bf16[128,4096]{1,0:T(8,128)(2,1)S(1)}, u32[]{:S(2)}, u32[]{:S(2)}) collective-permute-start(bf16[128,4096]{1,0:T(8,128)(2,1)} %get-tuple-element.35), channel_id=1, source_target_pairs={{0,17},{1,16},{2,19},{3,18},{4,21},{5,20},{6,23},{7,22},{8,25},{9,... | collective-permute-start | bytes 3145736 | tf_op jit(solution)/shard_map/ppermute | solution.py:349
  28.1 43.1 %collective-permute-start.2 = (bf16[128,4096]{1,0:T(8,128)(2,1)}, bf16[128,4096]{1,0:T(8,128)(2,1)S(1)}, u32[]{:S(2)}, u32[]{:S(2)}) collective-permute-start(bf16[128,4096]{1,0:T(8,128)(2,1)} %shard_map.105), channel_id=1, source_target_pairs={{0,16},{1,17},{2,18},{3,19},{4,20},{5,21},{6,22},{7,23},{8,24},{9,... | collective-permute-start | bytes 3145736 | tf_op jit(solution)/shard_map/ppermute | solution.py:349
  29.4 41.8 %collective-permute-start.3 = (bf16[128,4096]{1,0:T(8,128)(2,1)}, bf16[128,4096]{1,0:T(8,128)(2,1)S(1)}, u32[]{:S(2)}, u32[]{:S(2)}) collective-permute-start(bf16[128,4096]{1,0:T(8,128)(2,1)} %shard_map.105), channel_id=1, source_target_pairs={{0,17},{1,16},{2,19},{3,18},{4,21},{5,20},{6,23},{7,22},{8,25},{9,... | collective-permute-start | bytes 3145736 | tf_op jit(solution)/shard_map/ppermute | solution.py:349
  69.1 44.9 %copy-start.10 = (bf16[2,2,32,4096]{3,2,1,0:T(8,128)(2,1)S(1)}, bf16[2,2,32,4096]{3,2,1,0:T(8,128)(2,1)}, u32[]{:S(2)}) copy-start(bf16[2,2,32,4096]{3,2,1,0:T(8,128)(2,1)} %refs_1_.7) | copy-start | bytes 3145732
  69.1 20.3 %collective-permute-start.18 = (bf16[64,4096]{1,0:T(8,128)(2,1)}, bf16[64,4096]{1,0:T(8,128)(2,1)S(1)}, u32[]{:S(2)}, u32[]{:S(2)}) collective-permute-start(bf16[64,4096]{1,0:T(8,128)(2,1)} %get-tuple-element.38), channel_id=1, source_target_pairs={{16,17},{17,16},{18,19},{19,18},{20,21},{21,20},{22,23},{23,22},{2... | collective-permute-start | bytes 1572872 | tf_op jit(solution)/shard_map/ppermute | solution.py:349
  86.1 13.9 %collective-permute-start.4 = (bf16[64,4096]{1,0:T(8,128)(2,1)}, bf16[64,4096]{1,0:T(8,128)(2,1)S(1)}, u32[]{:S(2)}, u32[]{:S(2)}) collective-permute-start(bf16[64,4096]{1,0:T(8,128)(2,1)} %get-tuple-element.29), channel_id=1, source_target_pairs={{16,17},{17,16},{18,19},{19,18},{20,21},{21,20},{22,23},{23,22},{2... | collective-permute-start | bytes 1572872 | tf_op jit(solution)/shard_map/ppermute | solution.py:349
  89.6 15.8 %collective-permute-start.19 = (bf16[32,4096]{1,0:T(8,128)(2,1)S(1)}, bf16[32,4096]{1,0:T(8,128)(2,1)S(1)}, u32[]{:S(2)}, u32[]{:S(2)}) collective-permute-start(bf16[32,4096]{1,0:T(8,128)(2,1)S(1)} %add_convert_fusion.refs_0_), channel_id=1, source_target_pairs={{16,20},{17,21},{18,22},{19,23},{20,24},{21,25},{22,26},{23,27},{2... | collective-permute-start | bytes 786440 | tf_op jit(solution)/shard_map/ppermute | solution.py:349
  92.8 17.4 %collective-permute-start.20 = (bf16[32,4096]{1,0:T(8,128)(2,1)S(1)}, bf16[32,4096]{1,0:T(8,128)(2,1)S(1)}, u32[]{:S(2)}, u32[]{:S(2)}) collective-permute-start(bf16[32,4096]{1,0:T(8,128)(2,1)S(1)} %add_convert_fusion.refs_0_), channel_id=1, source_target_pairs={{16,24},{17,25},{18,26},{19,27},{20,28},{21,29},{22,30},{23,31},{2... | collective-permute-start | bytes 786440 | tf_op jit(solution)/shard_map/ppermute | solution.py:349
  97.0 13.2 %collective-permute-start.21 = (bf16[32,4096]{1,0:T(8,128)(2,1)S(1)}, bf16[32,4096]{1,0:T(8,128)(2,1)S(1)}, u32[]{:S(2)}, u32[]{:S(2)}) collective-permute-start(bf16[32,4096]{1,0:T(8,128)(2,1)S(1)} %add_convert_fusion.refs_0_), channel_id=1, source_target_pairs={{16,28},{17,29},{18,30},{19,31},{20,16},{21,17},{22,18},{23,19},{2... | collective-permute-start | bytes 786440 | tf_op jit(solution)/shard_map/ppermute | solution.py:349
  101.1 13.7 %collective-permute-start.5 = (bf16[32,4096]{1,0:T(8,128)(2,1)S(1)}, bf16[32,4096]{1,0:T(8,128)(2,1)S(1)}, u32[]{:S(2)}, u32[]{:S(2)}) collective-permute-start(bf16[32,4096]{1,0:T(8,128)(2,1)S(1)} %add_convert_fusion.1.refs_0_), channel_id=1, source_target_pairs={{16,20},{17,21},{18,22},{19,23},{20,24},{21,25},{22,26},{23,27},{2... | collective-permute-start | bytes 786440 | tf_op jit(solution)/shard_map/ppermute | solution.py:349
  103.5 12.3 %collective-permute-start.6 = (bf16[32,4096]{1,0:T(8,128)(2,1)S(1)}, bf16[32,4096]{1,0:T(8,128)(2,1)S(1)}, u32[]{:S(2)}, u32[]{:S(2)}) collective-permute-start(bf16[32,4096]{1,0:T(8,128)(2,1)S(1)} %add_convert_fusion.1.refs_0_), channel_id=1, source_target_pairs={{16,24},{17,25},{18,26},{19,27},{20,28},{21,29},{22,30},{23,31},{2... | collective-permute-start | bytes 786440 | tf_op jit(solution)/shard_map/ppermute | solution.py:349
  105.4 11.5 %collective-permute-start.7 = (bf16[32,4096]{1,0:T(8,128)(2,1)S(1)}, bf16[32,4096]{1,0:T(8,128)(2,1)S(1)}, u32[]{:S(2)}, u32[]{:S(2)}) collective-permute-start(bf16[32,4096]{1,0:T(8,128)(2,1)S(1)} %add_convert_fusion.1.refs_0_), channel_id=1, source_target_pairs={{16,28},{17,29},{18,30},{19,31},{20,16},{21,17},{22,18},{23,19},{2... | collective-permute-start | bytes 786440 | tf_op jit(solution)/shard_map/ppermute | solution.py:349
  110.9 9.9 %collective-permute-start.22 = (bf16[32,4096]{1,0:T(8,128)(2,1)S(1)}, bf16[32,4096]{1,0:T(8,128)(2,1)S(1)}, u32[]{:S(2)}, u32[]{:S(2)}) collective-permute-start(bf16[32,4096]{1,0:T(8,128)(2,1)S(1)} %get-tuple-element.40), channel_id=1, source_target_pairs={{16,18},{17,19},{18,16},{19,17},{20,22},{21,23},{22,20},{23,21},{2... | collective-permute-start | bytes 786440 | tf_op jit(solution)/shard_map/ppermute | solution.py:349
  114.1 13.8 %collective-permute-start.11 = (bf16[1,2,32,4096]{3,2,1,0:T(8,128)(2,1)S(1)}, bf16[1,2,32,4096]{3,2,1,0:T(8,128)(2,1)S(1)}, u32[]{:S(2)}, u32[]{:S(2)}) collective-permute-start(bf16[1,2,32,4096]{3,2,1,0:T(8,128)(2,1)S(1)} %slice.44), channel_id=1, source_target_pairs={{0,1},{1,0},{2,3},{3,2},{4,5},{5,4},{6,7},{7,6},{8,9},{9,8},{10,11... | collective-permute-start | bytes 1572872 | tf_op jit(solution)/shard_map/ppermute | solution.py:349
  117.6 7.1 %collective-permute-start.8 = (bf16[32,4096]{1,0:T(8,128)(2,1)S(1)}, bf16[32,4096]{1,0:T(8,128)(2,1)S(1)}, u32[]{:S(2)}, u32[]{:S(2)}) collective-permute-start(bf16[32,4096]{1,0:T(8,128)(2,1)S(1)} %get-tuple-element.31), channel_id=1, source_target_pairs={{16,18},{17,19},{18,16},{19,17},{20,22},{21,23},{22,20},{23,21},{2... | collective-permute-start | bytes 786440 | tf_op jit(solution)/shard_map/ppermute | solution.py:349
  121.3 6.6 %collective-permute-start.23 = (bf16[32,4096]{1,0:T(8,128)(2,1)S(1)}, bf16[32,4096]{1,0:T(8,128)(2,1)S(1)}, u32[]{:S(2)}, u32[]{:S(2)}) collective-permute-start(bf16[32,4096]{1,0:T(8,128)(2,1)S(1)} %pick.7), channel_id=1, source_target_pairs={{16,0},{17,1},{18,2},{19,3},{20,4},{21,5},{22,6},{23,7},{24,8},{25... | collective-permute-start | bytes 786440 | tf_op jit(solution)/shard_map/ppermute | solution.py:349
  122.7 5.3 %collective-permute-start.24 = (bf16[32,4096]{1,0:T(8,128)(2,1)S(1)}, bf16[32,4096]{1,0:T(8,128)(2,1)S(1)}, u32[]{:S(2)}, u32[]{:S(2)}) collective-permute-start(bf16[32,4096]{1,0:T(8,128)(2,1)S(1)} %pick.7), channel_id=1, source_target_pairs={{16,1},{17,0},{18,3},{19,2},{20,5},{21,4},{22,7},{23,6},{24,9},{25... | collective-permute-start | bytes 786440 | tf_op jit(solution)/shard_map/ppermute | solution.py:349
  125.3 8.7 %collective-permute-start.9 = (bf16[32,4096]{1,0:T(8,128)(2,1)S(1)}, bf16[32,4096]{1,0:T(8,128)(2,1)S(1)}, u32[]{:S(2)}, u32[]{:S(2)}) collective-permute-start(bf16[32,4096]{1,0:T(8,128)(2,1)S(1)} %pick.5), channel_id=1, source_target_pairs={{16,0},{17,1},{18,2},{19,3},{20,4},{21,5},{22,6},{23,7},{24,8},{25... | collective-permute-start | bytes 786440 | tf_op jit(solution)/shard_map/ppermute | solution.py:349
  126.6 7.4 %collective-permute-start.10 = (bf16[32,4096]{1,0:T(8,128)(2,1)S(1)}, bf16[32,4096]{1,0:T(8,128)(2,1)S(1)}, u32[]{:S(2)}, u32[]{:S(2)}) collective-permute-start(bf16[32,4096]{1,0:T(8,128)(2,1)S(1)} %pick.5), channel_id=1, source_target_pairs={{16,1},{17,0},{18,3},{19,2},{20,5},{21,4},{22,7},{23,6},{24,9},{25... | collective-permute-start | bytes 786440 | tf_op jit(solution)/shard_map/ppermute | solution.py:349
  131.3 31.9 %collective-permute-start.25 = (bf16[128,4096]{1,0:T(8,128)(2,1)}, bf16[128,4096]{1,0:T(8,128)(2,1)S(1)}, u32[]{:S(2)}, u32[]{:S(2)}) collective-permute-start(bf16[128,4096]{1,0:T(8,128)(2,1)} %shard_map.110), channel_id=1, source_target_pairs={{0,16},{1,17},{2,18},{3,19},{4,20},{5,21},{6,22},{7,23},{8,24},{9,... | collective-permute-start | bytes 3145736 | tf_op jit(solution)/shard_map/ppermute | solution.py:349
  132.7 31.8 %collective-permute-start.26 = (bf16[128,4096]{1,0:T(8,128)(2,1)}, bf16[128,4096]{1,0:T(8,128)(2,1)S(1)}, u32[]{:S(2)}, u32[]{:S(2)}) collective-permute-start(bf16[128,4096]{1,0:T(8,128)(2,1)} %shard_map.110), channel_id=1, source_target_pairs={{0,17},{1,16},{2,19},{3,18},{4,21},{5,20},{6,23},{7,22},{8,25},{9,... | collective-permute-start | bytes 3145736 | tf_op jit(solution)/shard_map/ppermute | solution.py:349
  137.2 44.4 %collective-permute-start.12 = (bf16[128,4096]{1,0:T(8,128)(2,1)}, bf16[128,4096]{1,0:T(8,128)(2,1)S(1)}, u32[]{:S(2)}, u32[]{:S(2)}) collective-permute-start(bf16[128,4096]{1,0:T(8,128)(2,1)} %shard_map.107), channel_id=1, source_target_pairs={{0,16},{1,17},{2,18},{3,19},{4,20},{5,21},{6,22},{7,23},{8,24},{9,... | collective-permute-start | bytes 3145736 | tf_op jit(solution)/shard_map/ppermute | solution.py:349
  138.5 44.8 %collective-permute-start.13 = (bf16[128,4096]{1,0:T(8,128)(2,1)}, bf16[128,4096]{1,0:T(8,128)(2,1)}, u32[]{:S(2)}, u32[]{:S(2)}) collective-permute-start(bf16[128,4096]{1,0:T(8,128)(2,1)} %shard_map.107), channel_id=1, source_target_pairs={{0,17},{1,16},{2,19},{3,18},{4,21},{5,20},{6,23},{7,22},{8,25},{9,... | collective-permute-start | bytes 3145736 | tf_op jit(solution)/shard_map/ppermute | solution.py:349
  139.8 61.5 %collective-permute-start.29 = (bf16[64,4096]{1,0:T(8,128)(2,1)S(1)}, bf16[64,4096]{1,0:T(8,128)(2,1)S(1)}, u32[]{:S(2)}, u32[]{:S(2)}) collective-permute-start(bf16[64,4096]{1,0:T(8,128)(2,1)S(1)} %copy-done.3), channel_id=1, source_target_pairs={{16,0},{17,1},{18,2},{19,3},{20,4},{21,5},{22,6},{23,7},{24,8},{25... | collective-permute-start | bytes 1572872 | tf_op jit(solution)/shard_map/ppermute | solution.py:349
  163.2 35.1 %collective-permute-start.30 = (bf16[64,4096]{1,0:T(8,128)(2,1)S(1)}, bf16[64,4096]{1,0:T(8,128)(2,1)S(1)}, u32[]{:S(2)}, u32[]{:S(2)}) collective-permute-start(bf16[64,4096]{1,0:T(8,128)(2,1)S(1)} %copy-done.1), channel_id=1, source_target_pairs={{16,0},{17,1},{18,2},{19,3},{20,4},{21,5},{22,6},{23,7},{24,8},{25... | collective-permute-start | bytes 1572872 | tf_op jit(solution)/shard_map/ppermute | solution.py:349
  178.5 24.5 %collective-permute-start.27 = (bf16[64,4096]{1,0:T(8,128)(2,1)}, bf16[64,4096]{1,0:T(8,128)(2,1)S(1)}, u32[]{:S(2)}, u32[]{:S(2)}) collective-permute-start(bf16[64,4096]{1,0:T(8,128)(2,1)} %get-tuple-element.43), channel_id=1, source_target_pairs={{16,17},{17,16},{18,19},{19,18},{20,21},{21,20},{22,23},{23,22},{2... | collective-permute-start | bytes 1572872 | tf_op jit(solution)/shard_map/ppermute | solution.py:349
  181.7 21.4 %collective-permute-start.28 = (bf16[64,4096]{1,0:T(8,128)(2,1)}, bf16[64,4096]{1,0:T(8,128)(2,1)S(1)}, u32[]{:S(2)}, u32[]{:S(2)}) collective-permute-start(bf16[64,4096]{1,0:T(8,128)(2,1)} %get-tuple-element.41.x_own), channel_id=1, source_target_pairs={{16,0},{17,1},{18,2},{19,3},{20,4},{21,5},{22,6},{23,7},{24,8},{25... | collective-permute-start | bytes 1572872 | tf_op jit(solution)/shard_map/ppermute | solution.py:349
  196.1 10.1 %collective-permute-start.14 = (bf16[64,4096]{1,0:T(8,128)(2,1)}, bf16[64,4096]{1,0:T(8,128)(2,1)S(1)}, u32[]{:S(2)}, u32[]{:S(2)}) collective-permute-start(bf16[64,4096]{1,0:T(8,128)(2,1)} %get-tuple-element.34), channel_id=1, source_target_pairs={{16,17},{17,16},{18,19},{19,18},{20,21},{21,20},{22,23},{23,22},{2... | collective-permute-start | bytes 1572872 | tf_op jit(solution)/shard_map/ppermute | solution.py:349
  198.3 8.0 %collective-permute-start.15 = (bf16[64,4096]{1,0:T(8,128)(2,1)}, bf16[64,4096]{1,0:T(8,128)(2,1)S(1)}, u32[]{:S(2)}, u32[]{:S(2)}) collective-permute-start(bf16[64,4096]{1,0:T(8,128)(2,1)} %get-tuple-element.32.x_own), channel_id=1, source_target_pairs={{16,0},{17,1},{18,2},{19,3},{20,4},{21,5},{22,6},{23,7},{24,8},{25... | collective-permute-start | bytes 1572872 | tf_op jit(solution)/shard_map/ppermute | solution.py:349
  (24 other events, 198.6 us)

commit v2 on v1

--- a/solution.py
+++ b/solution.py
@@ -12,7 +12,7 @@
 EPSILON = 1e-05
 TILE = 512
 AXES = ("phase", "dp", "mp")
-VMEM_SMALL = 16 << 20
+VMEM_SMALL = 14 << 20
 
 
 ANY = pl.BlockSpec(memory_space=pl.ANY)
@@ -36,7 +36,7 @@
     return weights.at[first + j // per_slab, pl.ds(pl.multiple_of(j % per_slab * q_dim, q_dim), q_dim)]
 
 
-def load_kernel(w_query, w_key, value_weight, weights, sem):
+def load_kernel(plan, w_query, w_key, value_weight, weights, sem):
     copies = []
     for source in (w_query, w_key, value_weight):
         for j in range(source.shape[1] // TILE):
@@ -50,14 +50,14 @@
         copy.wait()
 
 
-def load_weights(w_query, w_key, value_weight, w_out):
+def load_weights(plan, w_query, w_key, value_weight, w_out):
     width = w_query.shape[0]
     tiles = (w_query.shape[1] + w_key.shape[1] + value_weight.shape[1]) // TILE
     slabs = tiles + w_out.shape[0] * w_out.shape[1] // (width * TILE)
     return pl.pallas_call(
         load_kernel,
         out_shape=pltpu.VMEM((slabs, width, TILE), BF16),
-        in_specs=[HBM] * 3,
+        in_specs=[SMEM] + [HBM] * 3,
         out_specs=VMEM,
         scratch_shapes=[pltpu.SemaphoreType.DMA((tiles,))],
         compiler_params=pltpu.CompilerParams(vmem_limit_bytes=VMEM_SMALL),
@@ -65,7 +65,7 @@
             flops=0, bytes_accessed=2 * tiles * TILE * width, transcendentals=0
         ),
         name="load_weights",
-    )(w_query, w_key, value_weight)
+    )(plan, w_query, w_key, value_weight)
 
 
 def section_kernel(cfg, plan, lengths, gain, *refs):
@@ -112,14 +112,19 @@
         for copy in in_copies():
             copy.start()
 
-    if load:
+    def start_out():
         for j in range(out_tiles):
             out_copy(j).start()
+
+    if load:
+        pl.when(jnp.logical_not(active))(start_out)
 
     @pl.when(active)
     def _():
         for copy in in_copies():
             copy.wait()
+        if load:
+            start_out()
         step = 16
 
         @pl.loop(0, rows // step)
@@ -211,6 +216,11 @@
     width = weights.shape[1]
     rows, q_dim, qkv_tiles = 2 * half, q_tiles * TILE, q_tiles + 2 * k_tiles
     weights = pltpu.with_memory_space_constraint(weights, pltpu.VMEM)
+    near_blocks = (0, 1) if want else (2, 3) if round_index == 0 else (0, 2)
+    blocks = [
+        pltpu.with_memory_space_constraint(b, pltpu.VMEM) if n in near_blocks else b
+        for n, b in enumerate(blocks)
+    ]
     if want:
         out_shape = [rows_of(half, width)] * 3
     else:
@@ -354,10 +364,13 @@
     def across(p, flip):
         return lambda g, i: [(flat(p, g, i), flat(1 - p, g, 1 - i if flip else i))]
 
+    def hop(place, step):
+        return place ^ step if outer & (outer - 1) == 0 else (place + step) % outer
+
     def along(step_outer, step_inner):
         def pairs(g, i):
             o, n = divmod(g, inner)
-            target = (o + step_outer) % outer * inner + (n + step_inner) % inner
+            target = hop(o, step_outer) * inner + (n + step_inner) % inner
             return [(flat(1, g, i), flat(1, target, i))]
 
         return pairs
@@ -367,7 +380,11 @@
     targets = mine_o * inner + (mine_n + jnp.arange(inner, dtype=jnp.int32)) % inner
     hit = routes[:, None, :] == targets[None, :, None]
     source = jnp.sum(jnp.where(hit, ids[None, None, :], 0), axis=-1)
-    hops = (mine_o - source // inner + outer) % outer
+    source_o = source // inner
+    if outer & (outer - 1) == 0:
+        hops = (mine_o ^ source_o) & (outer - 1)
+    else:
+        hops = (mine_o - source_o + outer) % outer
     side = (mine_n - source[:, :1] % inner + inner) % inner
     entries = 1 + inner
     plan = jnp.concatenate(
@@ -386,14 +403,14 @@
         arrived = [send(picked[k], along(0, k)) for k in range(1, inner)]
         return pick(plan, [base + inner], [picked[0]] + arrived)[0]
 
-    def gather_rows(m):
-        rows = jnp.concatenate([memory_in[m], segments[0, m]], axis=0)
-        return send(rows, within(0))
-
-    weights = load_weights(w_query[0], w_key[0], value_weight[0], w_out[0])
+    weights = load_weights(plan, w_query[0], w_key[0], value_weight[0], w_out[0])
     dims = (w_query.shape[2] // TILE, w_key.shape[2] // TILE, half, ns)
-    first_peer = [gather_rows(m) for m in range(slots)]
-    later_peer = send(segments[1:], within(0)) if rounds > 1 else None
+    first_mem = send(memory_in, within(0))
+    first_seg = send(segments[:1], within(0))
+    later_peer = None
+    if rounds > 1:
+        later_peer = send(segments[1:], within(1))
+        later_peer = send(later_peer, across(1, False))
     mem_own = mem_peer = None
     shapes = [(1, rounds, slots, n) + memory_in.shape[2:] for n in (nm, ns)]
     outs = []
@@ -401,11 +418,12 @@
         sent = []
         for m in range(slots):
             if r == 0:
-                blocks = [memory_in, segments, first_peer[m]]
+                blocks = [memory_in, segments, first_mem, first_seg]
                 spots = [
                     (0, (m,), 0, False, 0, nm),
                     (1, (0, m), 0, False, nm, ns),
-                    (2, (), 0, False, half, half),
+                    (2, (m,), 0, False, half, nm),
+                    (3, (0, m), 0, False, half + nm, ns),
                 ]
             else:
                 blocks = [mem_own[m], segments, mem_peer[m], later_peer]
@@ -444,7 +462,10 @@
                 routed = route(m, new_mem)
                 next_peer.append(send(routed, across(1, True)))
                 next_own.append(send(routed, across(1, False)))
-            outs = finish(plan, (x_own, own_term, arrived, back), outs, shapes, r, m, nm)
+            values = (x_own, own_term, arrived, back)
+            if r + 1 == rounds:
+                values = [pltpu.with_memory_space_constraint(v, pltpu.VMEM) for v in values]
+            outs = finish(plan, values, outs, shapes, r, m, nm)
         mem_own, mem_peer = next_own, next_peer
     return tuple(outs)
 

time: 212 us -> 193 us (0.910)
  local copies, waits for them, and re-layouts: 12.8 us -> 4.27 us
  waiting for transfers between devices: 29 us -> 23 us
  Pallas kernels: 82.1 us -> 77.3 us
    unnamed x50 -> x22, local copies, waits for them, and re-layouts: 10.6 us -> 2.92 us
    ppermute x31 -> x32, waiting for transfers between devices: 29 us -> 23 us  [send(): return lax.ppermute(value, AXES, pairs)]
    pallas_call x8, Pallas kernels: 64.5 us -> 59.1 us  [section(): pl.pallas_call(functools.partial(section_kernel, (round_index, slot, want...]
    squeeze x2 -> x0, local copies, waits for them, and re-layouts: 2.13 us -> none  [gather_rows(): rows = jnp.concatenate([memory_in[m], segments[0, m]], axis=0)]
    ppermute x31 -> x32, starting transfers between devices: 81.7 us -> 82.1 us  [send(): return lax.ppermute(value, AXES, pairs)]
  transfers between devices with their start and end apart: 31 -> 32, of which waited for: 6 -> 5; matrix products, arithmetic and copies ran while one was open for 1% -> 2% of each run, Pallas kernels for 38% -> 36%
where the time goes in v2:
time: 193 us; the launch traced here: 191 us
  starting transfers between devices  82.1 us (43%)
  Pallas kernels  77.3 us (40%)
  waiting for transfers between devices  23 us (12%)
  local copies, waits for them, and re-layouts  4.27 us (2%)
  other arithmetic  2.83 us (1%)
    ppermute x32, starting transfers between devices, send(): return lax.ppermute(value, AXES, pairs)  82.1 us
    pallas_call x8, Pallas kernels, section(): pl.pallas_call(functools.partial(section_kernel, (round_index, slot, want...  59.1 us
    ppermute x32, waiting for transfers between devices, send(): return lax.ppermute(value, AXES, pairs)  23 us
    pallas_call x1, Pallas kernels, load_weights(): pl.pallas_call(load_kernel, out_shape=pltpu.VMEM((slabs, width, TILE), BF...  9.02 us
    pallas_call x4, Pallas kernels, finish(): pl.pallas_call(functools.partial(finish_kernel, (round_index, slot, nm)),...  6.76 us
  transfers between devices with their start and end apart: 32, of which 5 were waited for; matrix products, arithmetic and copies ran while one was open for 2% of the time, Pallas kernels for 36%

profile of v2, /device:TPU:1, one launch (start us, length us, event | category | flops | bytes accessed | tf_op | source)
XLA Modules:
  0.0 191.1 jit_solution(9016145847218773837)
XLA Ops:
  5.0 9.0 %load_weights.1.refs_4_ = bf16[10,4096,512]{2,1,0:T(8,128)(2,1)S(1)} custom-call(s32[8]{0:T(128)} %pad_add_fusion.1.plan, bf16[4096,2048]{1,0:T(8,128)(2,1)} %bitcast.6, bf16[4096,512]{1,0:T(8,128)(2,1)} %bitcast.8, bf16[4096,512]{1,0:T(8,128)(2,1)} %bitcast.9), custom_call_target="tpu_custom_call" | custom-call | bytes 25165824 | tf_op jit(solution)/shard_map/load_weights/pallas_call | solution.py:57
  14.1 7.8 %shard_map.104 = (bf16[128,4096]{1,0:T(8,128)(2,1)}, bf16[10,4096,512]{2,1,0:T(8,128)(2,1)S(1)}) custom-call(s32[8]{0:T(128)} %pad_add_fusion.1.plan, s32[2,2]{1,0:T(2,128)} %lengths.15, bf16[1,4096]{1,0:T(2,128)(2,1)} %gain.15, bf16[2,32,4096]{2,1,0:T(8,128)(2,1)} %refs_0_.3, bf16[2,2,32,4096]{3,2,1,0:T(8,128)(2,1)} %refs_1_.7, ...), custom_call_target="tpu_custom_call", output_to_operand_aliasing={{1}: (7, {})} | custom-call | flops 5368709120 | bytes 41943040 | tf_op jit(solution)/shard_map/pallas_call | solution.py:243
  24.5 1.7 shard_map.105
  28.8 18.9 %collective-permute-done.18.refs_1_ = bf16[128,4096]{1,0:T(8,128)(2,1)S(1)} collective-permute-done((bf16[128,4096]{1,0:T(8,128)(2,1)}, bf16[128,4096]{1,0:T(8,128)(2,1)S(1)}, u32[]{:S(2)}, u32[]{:S(2)}) %collective-permute-start.18) | collective-permute-done | bytes 1048608 | tf_op jit(solution)/shard_map/ppermute | solution.py:359
  47.7 11.4 %shard_map.109 = (bf16[64,4096]{1,0:T(8,128)(2,1)}, bf16[64,4096]{1,0:T(8,128)(2,1)}, bf16[64,4096]{1,0:T(8,128)(2,1)}) custom-call(s32[8]{0:T(128)} %pad_add_fusion.1.plan, s32[2,2]{1,0:T(2,128)} %lengths.15, bf16[1,4096]{1,0:T(2,128)(2,1)} %gain.15, bf16[128,4096]{1,0:T(8,128)(2,1)S(1)} %collective-permute-done.17.refs_0_, ...), custom_call_target="tpu_custom_call" | custom-call | flops 5368709120 | bytes 41943040 | tf_op jit(solution)/shard_map/pallas_call | solution.py:243
  59.1 1.9 %collective-permute-start.19 = (bf16[64,4096]{1,0:T(8,128)(2,1)}, bf16[64,4096]{1,0:T(8,128)(2,1)S(1)}, u32[]{:S(2)}, u32[]{:S(2)}) collective-permute-start(bf16[64,4096]{1,0:T(8,128)(2,1)} %get-tuple-element.38), channel_id=1, source_target_pairs={{16,17},{17,16},{18,19},{19,18},{20,21},{21,20},{22,23},{23,22},{2... | collective-permute-start | bytes 1572872 | tf_op jit(solution)/shard_map/ppermute | solution.py:359
  61.1 3.5 %collective-permute-start.11 = (bf16[1,2,32,4096]{3,2,1,0:T(8,128)(2,1)S(1)}, bf16[1,2,32,4096]{3,2,1,0:T(8,128)(2,1)S(1)}, u32[]{:S(2)}, u32[]{:S(2)}) collective-permute-start(bf16[1,2,32,4096]{3,2,1,0:T(8,128)(2,1)S(1)} %get-tuple-element.50), channel_id=1, source_target_pairs={{16,17},{17,16},{18,19},{19,18},{20,21},{21,20},{22,23},{23,22},{2... | collective-permute-start | bytes 1572872 | tf_op jit(solution)/shard_map/ppermute | solution.py:359
  64.6 11.6 %shard_map.106 = (bf16[64,4096]{1,0:T(8,128)(2,1)}, bf16[64,4096]{1,0:T(8,128)(2,1)}, bf16[64,4096]{1,0:T(8,128)(2,1)}) custom-call(s32[8]{0:T(128)} %pad_add_fusion.1.plan, s32[2,2]{1,0:T(2,128)} %lengths.15, bf16[1,4096]{1,0:T(2,128)(2,1)} %gain.15, bf16[128,4096]{1,0:T(8,128)(2,1)S(1)} %collective-permute-done.2.refs_0_, ...), custom_call_target="tpu_custom_call" | custom-call | flops 5368709120 | bytes 41943040 | tf_op jit(solution)/shard_map/pallas_call | solution.py:243
  76.2 1.9 %collective-permute-start.4 = (bf16[64,4096]{1,0:T(8,128)(2,1)}, bf16[64,4096]{1,0:T(8,128)(2,1)S(1)}, u32[]{:S(2)}, u32[]{:S(2)}) collective-permute-start(bf16[64,4096]{1,0:T(8,128)(2,1)} %get-tuple-element.29), channel_id=1, source_target_pairs={{16,17},{17,16},{18,19},{19,18},{20,21},{21,20},{22,23},{23,22},{2... | collective-permute-start | bytes 1572872 | tf_op jit(solution)/shard_map/ppermute | solution.py:359
  78.3 5.4 %collective-permute-start.22 = (bf16[32,4096]{1,0:T(8,128)(2,1)S(1)}, bf16[32,4096]{1,0:T(8,128)(2,1)S(1)}, u32[]{:S(2)}, u32[]{:S(2)}) collective-permute-start(bf16[32,4096]{1,0:T(8,128)(2,1)S(1)} %add_convert_fusion.refs_0_), channel_id=1, source_target_pairs={{16,28},{17,29},{18,30},{19,31},{20,24},{21,25},{22,26},{23,27},{2... | collective-permute-start | bytes 786440 | tf_op jit(solution)/shard_map/ppermute | solution.py:359
  83.7 1.9 %collective-permute-start.21 = (bf16[32,4096]{1,0:T(8,128)(2,1)S(1)}, bf16[32,4096]{1,0:T(8,128)(2,1)S(1)}, u32[]{:S(2)}, u32[]{:S(2)}) collective-permute-start(bf16[32,4096]{1,0:T(8,128)(2,1)S(1)} %add_convert_fusion.refs_0_), channel_id=1, source_target_pairs={{16,24},{17,25},{18,26},{19,27},{20,28},{21,29},{22,30},{23,31},{2... | collective-permute-start | bytes 786440 | tf_op jit(solution)/shard_map/ppermute | solution.py:359
  85.6 2.2 %collective-permute-start.20 = (bf16[32,4096]{1,0:T(8,128)(2,1)S(1)}, bf16[32,4096]{1,0:T(8,128)(2,1)S(1)}, u32[]{:S(2)}, u32[]{:S(2)}) collective-permute-start(bf16[32,4096]{1,0:T(8,128)(2,1)S(1)} %add_convert_fusion.refs_0_), channel_id=1, source_target_pairs={{16,20},{17,21},{18,22},{19,23},{20,16},{21,17},{22,18},{23,19},{2... | collective-permute-start | bytes 786440 | tf_op jit(solution)/shard_map/ppermute | solution.py:359
  89.0 5.2 %collective-permute-start.7 = (bf16[32,4096]{1,0:T(8,128)(2,1)S(1)}, bf16[32,4096]{1,0:T(8,128)(2,1)S(1)}, u32[]{:S(2)}, u32[]{:S(2)}) collective-permute-start(bf16[32,4096]{1,0:T(8,128)(2,1)S(1)} %add_convert_fusion.1.refs_0_), channel_id=1, source_target_pairs={{16,28},{17,29},{18,30},{19,31},{20,24},{21,25},{22,26},{23,27},{2... | collective-permute-start | bytes 786440 | tf_op jit(solution)/shard_map/ppermute | solution.py:359
  94.1 1.9 %collective-permute-start.6 = (bf16[32,4096]{1,0:T(8,128)(2,1)S(1)}, bf16[32,4096]{1,0:T(8,128)(2,1)S(1)}, u32[]{:S(2)}, u32[]{:S(2)}) collective-permute-start(bf16[32,4096]{1,0:T(8,128)(2,1)S(1)} %add_convert_fusion.1.refs_0_), channel_id=1, source_target_pairs={{16,24},{17,25},{18,26},{19,27},{20,28},{21,29},{22,30},{23,31},{2... | collective-permute-start | bytes 786440 | tf_op jit(solution)/shard_map/ppermute | solution.py:359
  96.1 2.2 %collective-permute-start.5 = (bf16[32,4096]{1,0:T(8,128)(2,1)S(1)}, bf16[32,4096]{1,0:T(8,128)(2,1)S(1)}, u32[]{:S(2)}, u32[]{:S(2)}) collective-permute-start(bf16[32,4096]{1,0:T(8,128)(2,1)S(1)} %add_convert_fusion.1.refs_0_), channel_id=1, source_target_pairs={{16,20},{17,21},{18,22},{19,23},{20,16},{21,17},{22,18},{23,19},{2... | collective-permute-start | bytes 786440 | tf_op jit(solution)/shard_map/ppermute | solution.py:359
  99.0 3.2 %collective-permute-start.23 = (bf16[32,4096]{1,0:T(8,128)(2,1)S(1)}, bf16[32,4096]{1,0:T(8,128)(2,1)S(1)}, u32[]{:S(2)}, u32[]{:S(2)}) collective-permute-start(bf16[32,4096]{1,0:T(8,128)(2,1)S(1)} %get-tuple-element.40), channel_id=1, source_target_pairs={{16,18},{17,19},{18,16},{19,17},{20,22},{21,23},{22,20},{23,21},{2... | collective-permute-start | bytes 786440 | tf_op jit(solution)/shard_map/ppermute | solution.py:359
  102.2 1.3 collective-permute-start.12
  103.6 2.7 %collective-permute-done.6.refs_2_ = bf16[32,4096]{1,0:T(8,128)(2,1)S(1)} collective-permute-done((bf16[32,4096]{1,0:T(8,128)(2,1)S(1)}, bf16[32,4096]{1,0:T(8,128)(2,1)S(1)}, u32[]{:S(2)}, u32[]{:S(2)}) %collective-permute-start.6) | collective-permute-done | bytes 262176 | tf_op jit(solution)/shard_map/ppermute | solution.py:359
  107.0 3.2 %collective-permute-start.8 = (bf16[32,4096]{1,0:T(8,128)(2,1)S(1)}, bf16[32,4096]{1,0:T(8,128)(2,1)S(1)}, u32[]{:S(2)}, u32[]{:S(2)}) collective-permute-start(bf16[32,4096]{1,0:T(8,128)(2,1)S(1)} %get-tuple-element.31), channel_id=1, source_target_pairs={{16,18},{17,19},{18,16},{19,17},{20,22},{21,23},{22,20},{23,21},{2... | collective-permute-start | bytes 786440 | tf_op jit(solution)/shard_map/ppermute | solution.py:359
  118.2 1.7 shard_map.110
  119.9 1.4 collective-permute-start.27
  122.7 1.7 shard_map.107
  127.0 21.9 %collective-permute-start.30 = (bf16[64,4096]{1,0:T(8,128)(2,1)S(1)}, bf16[64,4096]{1,0:T(8,128)(2,1)S(1)}, u32[]{:S(2)}, u32[]{:S(2)}) collective-permute-start(bf16[64,4096]{1,0:T(8,128)(2,1)S(1)} %copy-done.3), channel_id=1, source_target_pairs={{16,0},{17,1},{18,2},{19,3},{20,4},{21,5},{22,6},{23,7},{24,8},{25... | collective-permute-start | bytes 1572872 | tf_op jit(solution)/shard_map/ppermute | solution.py:359
  150.2 11.6 %shard_map.111 = (bf16[64,4096]{1,0:T(8,128)(2,1)}, bf16[64,4096]{1,0:T(8,128)(2,1)}, bf16[64,4096]{1,0:T(8,128)(2,1)}) custom-call(s32[8]{0:T(128)} %pad_add_fusion.1.plan, s32[2,2]{1,0:T(2,128)} %lengths.15, bf16[1,4096]{1,0:T(2,128)(2,1)} %gain.15, bf16[128,4096]{1,0:T(8,128)(2,1)S(1)} %collective-permute-done.26.refs_0_, ...), custom_call_target="tpu_custom_call" | custom-call | flops 5368709120 | bytes 41943040 | tf_op jit(solution)/shard_map/pallas_call | solution.py:243
  161.9 2.2 %collective-permute-start.28 = (bf16[64,4096]{1,0:T(8,128)(2,1)}, bf16[64,4096]{1,0:T(8,128)(2,1)S(1)}, u32[]{:S(2)}, u32[]{:S(2)}) collective-permute-start(bf16[64,4096]{1,0:T(8,128)(2,1)} %get-tuple-element.43), channel_id=1, source_target_pairs={{16,17},{17,16},{18,19},{19,18},{20,21},{21,20},{22,23},{23,22},{2... | collective-permute-start | bytes 1572872 | tf_op jit(solution)/shard_map/ppermute | solution.py:359
  164.1 1.5 collective-permute-start.29
  165.6 11.4 %shard_map.108 = (bf16[64,4096]{1,0:T(8,128)(2,1)}, bf16[64,4096]{1,0:T(8,128)(2,1)}, bf16[64,4096]{1,0:T(8,128)(2,1)}) custom-call(s32[8]{0:T(128)} %pad_add_fusion.1.plan, s32[2,2]{1,0:T(2,128)} %lengths.15, bf16[1,4096]{1,0:T(2,128)(2,1)} %gain.15, bf16[128,4096]{1,0:T(8,128)(2,1)S(1)} %collective-permute-done.13.refs_0_, ...), custom_call_target="tpu_custom_call" | custom-call | flops 5368709120 | bytes 41943040 | tf_op jit(solution)/shard_map/pallas_call | solution.py:243
  177.0 3.1 %collective-permute-start.15 = (bf16[64,4096]{1,0:T(8,128)(2,1)}, bf16[64,4096]{1,0:T(8,128)(2,1)S(1)}, u32[]{:S(2)}, u32[]{:S(2)}) collective-permute-start(bf16[64,4096]{1,0:T(8,128)(2,1)} %get-tuple-element.34), channel_id=1, source_target_pairs={{16,17},{17,16},{18,19},{19,18},{20,21},{21,20},{22,23},{23,22},{2... | collective-permute-start | bytes 1572872 | tf_op jit(solution)/shard_map/ppermute | solution.py:359
  181.5 1.7 shard_map.112
  183.2 1.7 shard_map.113
  184.9 1.7 shard_map.114
  189.2 1.7 shard_map.115
  (81 shorter events, 29.3 us)
Async XLA Ops:
  0.6 13.4 %collective-permute-start = (bf16[2,32,4096]{2,1,0:T(8,128)(2,1)}, bf16[2,32,4096]{2,1,0:T(8,128)(2,1)S(1)}, u32[]{:S(2)}, u32[]{:S(2)}) collective-permute-start(bf16[2,32,4096]{2,1,0:T(8,128)(2,1)} %refs_0_.3), channel_id=1, source_target_pairs={{0,1},{1,0},{2,3},{3,2},{4,5},{5,4},{6,7},{7,6},{8,9},{9,8},{10,11... | collective-permute-start | bytes 1572872 | tf_op jit(solution)/shard_map/ppermute | solution.py:359
  2.6 11.5 %collective-permute-start.1 = (bf16[1,2,32,4096]{3,2,1,0:T(8,128)(2,1)S(1)}, bf16[1,2,32,4096]{3,2,1,0:T(8,128)(2,1)S(1)}, u32[]{:S(2)}, u32[]{:S(2)}) collective-permute-start(bf16[1,2,32,4096]{3,2,1,0:T(8,128)(2,1)S(1)} %get-tuple-element.51), channel_id=1, source_target_pairs={{0,1},{1,0},{2,3},{3,2},{4,5},{5,4},{6,7},{7,6},{8,9},{9,8},{10,11... | collective-permute-start | bytes 1572872 | tf_op jit(solution)/shard_map/ppermute | solution.py:359
  21.9 25.8 %collective-permute-start.18 = (bf16[128,4096]{1,0:T(8,128)(2,1)}, bf16[128,4096]{1,0:T(8,128)(2,1)S(1)}, u32[]{:S(2)}, u32[]{:S(2)}) collective-permute-start(bf16[128,4096]{1,0:T(8,128)(2,1)} %get-tuple-element.35), channel_id=1, source_target_pairs={{0,17},{1,16},{2,19},{3,18},{4,21},{5,20},{6,23},{7,22},{8,25},{9,... | collective-permute-start | bytes 3145736 | tf_op jit(solution)/shard_map/ppermute | solution.py:359
  23.2 24.5 %collective-permute-start.17 = (bf16[128,4096]{1,0:T(8,128)(2,1)}, bf16[128,4096]{1,0:T(8,128)(2,1)S(1)}, u32[]{:S(2)}, u32[]{:S(2)}) collective-permute-start(bf16[128,4096]{1,0:T(8,128)(2,1)} %get-tuple-element.35), channel_id=1, source_target_pairs={{0,16},{1,17},{2,18},{3,19},{4,20},{5,21},{6,22},{7,23},{8,24},{9,... | collective-permute-start | bytes 3145736 | tf_op jit(solution)/shard_map/ppermute | solution.py:359
  26.2 38.4 %collective-permute-start.3 = (bf16[128,4096]{1,0:T(8,128)(2,1)}, bf16[128,4096]{1,0:T(8,128)(2,1)S(1)}, u32[]{:S(2)}, u32[]{:S(2)}) collective-permute-start(bf16[128,4096]{1,0:T(8,128)(2,1)} %shard_map.105), channel_id=1, source_target_pairs={{0,17},{1,16},{2,19},{3,18},{4,21},{5,20},{6,23},{7,22},{8,25},{9,... | collective-permute-start | bytes 3145736 | tf_op jit(solution)/shard_map/ppermute | solution.py:359
  27.5 37.1 %collective-permute-start.2 = (bf16[128,4096]{1,0:T(8,128)(2,1)}, bf16[128,4096]{1,0:T(8,128)(2,1)S(1)}, u32[]{:S(2)}, u32[]{:S(2)}) collective-permute-start(bf16[128,4096]{1,0:T(8,128)(2,1)} %shard_map.105), channel_id=1, source_target_pairs={{0,16},{1,17},{2,18},{3,19},{4,20},{5,21},{6,22},{7,23},{8,24},{9,... | collective-permute-start | bytes 3145736 | tf_op jit(solution)/shard_map/ppermute | solution.py:359
  59.1 19.0 %collective-permute-start.19 = (bf16[64,4096]{1,0:T(8,128)(2,1)}, bf16[64,4096]{1,0:T(8,128)(2,1)S(1)}, u32[]{:S(2)}, u32[]{:S(2)}) collective-permute-start(bf16[64,4096]{1,0:T(8,128)(2,1)} %get-tuple-element.38), channel_id=1, source_target_pairs={{16,17},{17,16},{18,19},{19,18},{20,21},{21,20},{22,23},{23,22},{2... | collective-permute-start | bytes 1572872 | tf_op jit(solution)/shard_map/ppermute | solution.py:359
  61.1 41.2 %collective-permute-start.11 = (bf16[1,2,32,4096]{3,2,1,0:T(8,128)(2,1)S(1)}, bf16[1,2,32,4096]{3,2,1,0:T(8,128)(2,1)S(1)}, u32[]{:S(2)}, u32[]{:S(2)}) collective-permute-start(bf16[1,2,32,4096]{3,2,1,0:T(8,128)(2,1)S(1)} %get-tuple-element.50), channel_id=1, source_target_pairs={{16,17},{17,16},{18,19},{19,18},{20,21},{21,20},{22,23},{23,22},{2... | collective-permute-start | bytes 1572872 | tf_op jit(solution)/shard_map/ppermute | solution.py:359
  76.2 11.6 %collective-permute-start.4 = (bf16[64,4096]{1,0:T(8,128)(2,1)}, bf16[64,4096]{1,0:T(8,128)(2,1)S(1)}, u32[]{:S(2)}, u32[]{:S(2)}) collective-permute-start(bf16[64,4096]{1,0:T(8,128)(2,1)} %get-tuple-element.29), channel_id=1, source_target_pairs={{16,17},{17,16},{18,19},{19,18},{20,21},{21,20},{22,23},{23,22},{2... | collective-permute-start | bytes 1572872 | tf_op jit(solution)/shard_map/ppermute | solution.py:359
  78.3 15.9 %collective-permute-start.22 = (bf16[32,4096]{1,0:T(8,128)(2,1)S(1)}, bf16[32,4096]{1,0:T(8,128)(2,1)S(1)}, u32[]{:S(2)}, u32[]{:S(2)}) collective-permute-start(bf16[32,4096]{1,0:T(8,128)(2,1)S(1)} %add_convert_fusion.refs_0_), channel_id=1, source_target_pairs={{16,28},{17,29},{18,30},{19,31},{20,24},{21,25},{22,26},{23,27},{2... | collective-permute-start | bytes 786440 | tf_op jit(solution)/shard_map/ppermute | solution.py:359
  83.7 12.4 %collective-permute-start.21 = (bf16[32,4096]{1,0:T(8,128)(2,1)S(1)}, bf16[32,4096]{1,0:T(8,128)(2,1)S(1)}, u32[]{:S(2)}, u32[]{:S(2)}) collective-permute-start(bf16[32,4096]{1,0:T(8,128)(2,1)S(1)} %add_convert_fusion.refs_0_), channel_id=1, source_target_pairs={{16,24},{17,25},{18,26},{19,27},{20,28},{21,29},{22,30},{23,31},{2... | collective-permute-start | bytes 786440 | tf_op jit(solution)/shard_map/ppermute | solution.py:359
  85.6 12.7 %collective-permute-start.20 = (bf16[32,4096]{1,0:T(8,128)(2,1)S(1)}, bf16[32,4096]{1,0:T(8,128)(2,1)S(1)}, u32[]{:S(2)}, u32[]{:S(2)}) collective-permute-start(bf16[32,4096]{1,0:T(8,128)(2,1)S(1)} %add_convert_fusion.refs_0_), channel_id=1, source_target_pairs={{16,20},{17,21},{18,22},{19,23},{20,16},{21,17},{22,18},{23,19},{2... | collective-permute-start | bytes 786440 | tf_op jit(solution)/shard_map/ppermute | solution.py:359
  89.0 14.6 %collective-permute-start.7 = (bf16[32,4096]{1,0:T(8,128)(2,1)S(1)}, bf16[32,4096]{1,0:T(8,128)(2,1)S(1)}, u32[]{:S(2)}, u32[]{:S(2)}) collective-permute-start(bf16[32,4096]{1,0:T(8,128)(2,1)S(1)} %add_convert_fusion.1.refs_0_), channel_id=1, source_target_pairs={{16,28},{17,29},{18,30},{19,31},{20,24},{21,25},{22,26},{23,27},{2... | collective-permute-start | bytes 786440 | tf_op jit(solution)/shard_map/ppermute | solution.py:359
  94.1 12.1 %collective-permute-start.6 = (bf16[32,4096]{1,0:T(8,128)(2,1)S(1)}, bf16[32,4096]{1,0:T(8,128)(2,1)S(1)}, u32[]{:S(2)}, u32[]{:S(2)}) collective-permute-start(bf16[32,4096]{1,0:T(8,128)(2,1)S(1)} %add_convert_fusion.1.refs_0_), channel_id=1, source_target_pairs={{16,24},{17,25},{18,26},{19,27},{20,28},{21,29},{22,30},{23,31},{2... | collective-permute-start | bytes 786440 | tf_op jit(solution)/shard_map/ppermute | solution.py:359
  96.1 10.2 %collective-permute-start.5 = (bf16[32,4096]{1,0:T(8,128)(2,1)S(1)}, bf16[32,4096]{1,0:T(8,128)(2,1)S(1)}, u32[]{:S(2)}, u32[]{:S(2)}) collective-permute-start(bf16[32,4096]{1,0:T(8,128)(2,1)S(1)} %add_convert_fusion.1.refs_0_), channel_id=1, source_target_pairs={{16,20},{17,21},{18,22},{19,23},{20,16},{21,17},{22,18},{23,19},{2... | collective-permute-start | bytes 786440 | tf_op jit(solution)/shard_map/ppermute | solution.py:359
  99.0 11.1 %collective-permute-start.23 = (bf16[32,4096]{1,0:T(8,128)(2,1)S(1)}, bf16[32,4096]{1,0:T(8,128)(2,1)S(1)}, u32[]{:S(2)}, u32[]{:S(2)}) collective-permute-start(bf16[32,4096]{1,0:T(8,128)(2,1)S(1)} %get-tuple-element.40), channel_id=1, source_target_pairs={{16,18},{17,19},{18,16},{19,17},{20,22},{21,23},{22,20},{23,21},{2... | collective-permute-start | bytes 786440 | tf_op jit(solution)/shard_map/ppermute | solution.py:359
  102.2 15.1 %collective-permute-start.12 = (bf16[1,2,32,4096]{3,2,1,0:T(8,128)(2,1)S(1)}, bf16[1,2,32,4096]{3,2,1,0:T(8,128)(2,1)S(1)}, u32[]{:S(2)}, u32[]{:S(2)}) collective-permute-start(bf16[1,2,32,4096]{3,2,1,0:T(8,128)(2,1)S(1)} %collective-permute-done.11), channel_id=1, source_target_pairs={{16,0},{17,1},{18,2},{19,3},{20,4},{21,5},{22,6},{23,7},{24,8},{25... | collective-permute-start | bytes 1572872 | tf_op jit(solution)/shard_map/ppermute | solution.py:359
  107.0 7.1 %collective-permute-start.8 = (bf16[32,4096]{1,0:T(8,128)(2,1)S(1)}, bf16[32,4096]{1,0:T(8,128)(2,1)S(1)}, u32[]{:S(2)}, u32[]{:S(2)}) collective-permute-start(bf16[32,4096]{1,0:T(8,128)(2,1)S(1)} %get-tuple-element.31), channel_id=1, source_target_pairs={{16,18},{17,19},{18,16},{19,17},{20,22},{21,23},{22,20},{23,21},{2... | collective-permute-start | bytes 786440 | tf_op jit(solution)/shard_map/ppermute | solution.py:359
  110.8 6.6 %collective-permute-start.25 = (bf16[32,4096]{1,0:T(8,128)(2,1)S(1)}, bf16[32,4096]{1,0:T(8,128)(2,1)S(1)}, u32[]{:S(2)}, u32[]{:S(2)}) collective-permute-start(bf16[32,4096]{1,0:T(8,128)(2,1)S(1)} %pick.7), channel_id=1, source_target_pairs={{16,1},{17,0},{18,3},{19,2},{20,5},{21,4},{22,7},{23,6},{24,9},{25... | collective-permute-start | bytes 786440 | tf_op jit(solution)/shard_map/ppermute | solution.py:359
  112.1 5.3 %collective-permute-start.24 = (bf16[32,4096]{1,0:T(8,128)(2,1)S(1)}, bf16[32,4096]{1,0:T(8,128)(2,1)S(1)}, u32[]{:S(2)}, u32[]{:S(2)}) collective-permute-start(bf16[32,4096]{1,0:T(8,128)(2,1)S(1)} %pick.7), channel_id=1, source_target_pairs={{16,0},{17,1},{18,2},{19,3},{20,4},{21,5},{22,6},{23,7},{24,8},{25... | collective-permute-start | bytes 786440 | tf_op jit(solution)/shard_map/ppermute | solution.py:359
  114.7 8.0 %collective-permute-start.10 = (bf16[32,4096]{1,0:T(8,128)(2,1)S(1)}, bf16[32,4096]{1,0:T(8,128)(2,1)S(1)}, u32[]{:S(2)}, u32[]{:S(2)}) collective-permute-start(bf16[32,4096]{1,0:T(8,128)(2,1)S(1)} %pick.5), channel_id=1, source_target_pairs={{16,1},{17,0},{18,3},{19,2},{20,5},{21,4},{22,7},{23,6},{24,9},{25... | collective-permute-start | bytes 786440 | tf_op jit(solution)/shard_map/ppermute | solution.py:359
  116.0 6.7 %collective-permute-start.9 = (bf16[32,4096]{1,0:T(8,128)(2,1)S(1)}, bf16[32,4096]{1,0:T(8,128)(2,1)S(1)}, u32[]{:S(2)}, u32[]{:S(2)}) collective-permute-start(bf16[32,4096]{1,0:T(8,128)(2,1)S(1)} %pick.5), channel_id=1, source_target_pairs={{16,0},{17,1},{18,2},{19,3},{20,4},{21,5},{22,6},{23,7},{24,8},{25... | collective-permute-start | bytes 786440 | tf_op jit(solution)/shard_map/ppermute | solution.py:359
  119.9 29.0 %collective-permute-start.27 = (bf16[128,4096]{1,0:T(8,128)(2,1)}, bf16[128,4096]{1,0:T(8,128)(2,1)S(1)}, u32[]{:S(2)}, u32[]{:S(2)}) collective-permute-start(bf16[128,4096]{1,0:T(8,128)(2,1)} %shard_map.110), channel_id=1, source_target_pairs={{0,17},{1,16},{2,19},{3,18},{4,21},{5,20},{6,23},{7,22},{8,25},{9,... | collective-permute-start | bytes 3145736 | tf_op jit(solution)/shard_map/ppermute | solution.py:359
  121.3 28.9 %collective-permute-start.26 = (bf16[128,4096]{1,0:T(8,128)(2,1)}, bf16[128,4096]{1,0:T(8,128)(2,1)S(1)}, u32[]{:S(2)}, u32[]{:S(2)}) collective-permute-start(bf16[128,4096]{1,0:T(8,128)(2,1)} %shard_map.110), channel_id=1, source_target_pairs={{0,16},{1,17},{2,18},{3,19},{4,20},{5,21},{6,22},{7,23},{8,24},{9,... | collective-permute-start | bytes 3145736 | tf_op jit(solution)/shard_map/ppermute | solution.py:359
  124.4 39.6 %collective-permute-start.14 = (bf16[128,4096]{1,0:T(8,128)(2,1)}, bf16[128,4096]{1,0:T(8,128)(2,1)S(1)}, u32[]{:S(2)}, u32[]{:S(2)}) collective-permute-start(bf16[128,4096]{1,0:T(8,128)(2,1)} %shard_map.107), channel_id=1, source_target_pairs={{0,17},{1,16},{2,19},{3,18},{4,21},{5,20},{6,23},{7,22},{8,25},{9,... | collective-permute-start | bytes 3145736 | tf_op jit(solution)/shard_map/ppermute | solution.py:359
  125.7 39.8 %collective-permute-start.13 = (bf16[128,4096]{1,0:T(8,128)(2,1)}, bf16[128,4096]{1,0:T(8,128)(2,1)S(1)}, u32[]{:S(2)}, u32[]{:S(2)}) collective-permute-start(bf16[128,4096]{1,0:T(8,128)(2,1)} %shard_map.107), channel_id=1, source_target_pairs={{0,16},{1,17},{2,18},{3,19},{4,20},{5,21},{6,22},{7,23},{8,24},{9,... | collective-permute-start | bytes 3145736 | tf_op jit(solution)/shard_map/ppermute | solution.py:359
  127.0 56.1 %collective-permute-start.30 = (bf16[64,4096]{1,0:T(8,128)(2,1)S(1)}, bf16[64,4096]{1,0:T(8,128)(2,1)S(1)}, u32[]{:S(2)}, u32[]{:S(2)}) collective-permute-start(bf16[64,4096]{1,0:T(8,128)(2,1)S(1)} %copy-done.3), channel_id=1, source_target_pairs={{16,0},{17,1},{18,2},{19,3},{20,4},{21,5},{22,6},{23,7},{24,8},{25... | collective-permute-start | bytes 1572872 | tf_op jit(solution)/shard_map/ppermute | solution.py:359
  148.9 31.2 %collective-permute-start.31 = (bf16[64,4096]{1,0:T(8,128)(2,1)S(1)}, bf16[64,4096]{1,0:T(8,128)(2,1)S(1)}, u32[]{:S(2)}, u32[]{:S(2)}) collective-permute-start(bf16[64,4096]{1,0:T(8,128)(2,1)S(1)} %copy-done.1), channel_id=1, source_target_pairs={{16,0},{17,1},{18,2},{19,3},{20,4},{21,5},{22,6},{23,7},{24,8},{25... | collective-permute-start | bytes 1572872 | tf_op jit(solution)/shard_map/ppermute | solution.py:359
  161.9 23.0 %collective-permute-start.28 = (bf16[64,4096]{1,0:T(8,128)(2,1)}, bf16[64,4096]{1,0:T(8,128)(2,1)S(1)}, u32[]{:S(2)}, u32[]{:S(2)}) collective-permute-start(bf16[64,4096]{1,0:T(8,128)(2,1)} %get-tuple-element.43), channel_id=1, source_target_pairs={{16,17},{17,16},{18,19},{19,18},{20,21},{21,20},{22,23},{23,22},{2... | collective-permute-start | bytes 1572872 | tf_op jit(solution)/shard_map/ppermute | solution.py:359
  164.1 20.8 %collective-permute-start.29 = (bf16[64,4096]{1,0:T(8,128)(2,1)}, bf16[64,4096]{1,0:T(8,128)(2,1)S(1)}, u32[]{:S(2)}, u32[]{:S(2)}) collective-permute-start(bf16[64,4096]{1,0:T(8,128)(2,1)} %get-tuple-element.41.x_own), channel_id=1, source_target_pairs={{16,0},{17,1},{18,2},{19,3},{20,4},{21,5},{22,6},{23,7},{24,8},{25... | collective-permute-start | bytes 1572872 | tf_op jit(solution)/shard_map/ppermute | solution.py:359
  177.0 10.1 %collective-permute-start.15 = (bf16[64,4096]{1,0:T(8,128)(2,1)}, bf16[64,4096]{1,0:T(8,128)(2,1)S(1)}, u32[]{:S(2)}, u32[]{:S(2)}) collective-permute-start(bf16[64,4096]{1,0:T(8,128)(2,1)} %get-tuple-element.34), channel_id=1, source_target_pairs={{16,17},{17,16},{18,19},{19,18},{20,21},{21,20},{22,23},{23,22},{2... | collective-permute-start | bytes 1572872 | tf_op jit(solution)/shard_map/ppermute | solution.py:359
  180.1 7.0 %collective-permute-start.16 = (bf16[64,4096]{1,0:T(8,128)(2,1)}, bf16[64,4096]{1,0:T(8,128)(2,1)S(1)}, u32[]{:S(2)}, u32[]{:S(2)}) collective-permute-start(bf16[64,4096]{1,0:T(8,128)(2,1)} %get-tuple-element.32.x_own), channel_id=1, source_target_pairs={{16,0},{17,1},{18,2},{19,3},{20,4},{21,5},{22,6},{23,7},{24,8},{25... | collective-permute-start | bytes 1572872 | tf_op jit(solution)/shard_map/ppermute | solution.py:359
  (11 other events, 159.6 us)

commit v3 on v2

--- a/solution.py
+++ b/solution.py
@@ -23,10 +23,6 @@
 F32 = jnp.float32
 
 
-def rows_of(count, width):
-    return jax.ShapeDtypeStruct((count, width), BF16)
-
-
 def column(j):
     return pl.ds(pl.multiple_of(j * TILE, TILE), TILE)
 
@@ -36,14 +32,11 @@
     return weights.at[first + j // per_slab, pl.ds(pl.multiple_of(j % per_slab * q_dim, q_dim), q_dim)]
 
 
-def load_kernel(plan, w_query, w_key, value_weight, weights, sem):
-    copies = []
-    for source in (w_query, w_key, value_weight):
-        for j in range(source.shape[1] // TILE):
-            n = len(copies)
-            copies.append(
-                pltpu.make_async_copy(source.at[:, pl.ds(j * TILE, TILE)], weights.at[n], sem.at[n])
-            )
+def load_kernel(plan, w_query, weights, sem):
+    copies = [
+        pltpu.make_async_copy(w_query.at[:, pl.ds(n * TILE, TILE)], weights.at[n], sem.at[n])
+        for n in range(w_query.shape[1] // TILE)
+    ]
     for copy in copies:
         copy.start()
     for copy in copies:
@@ -52,20 +45,21 @@
 
 def load_weights(plan, w_query, w_key, value_weight, w_out):
     width = w_query.shape[0]
+    loaded = w_query.shape[1] // TILE
     tiles = (w_query.shape[1] + w_key.shape[1] + value_weight.shape[1]) // TILE
     slabs = tiles + w_out.shape[0] * w_out.shape[1] // (width * TILE)
     return pl.pallas_call(
         load_kernel,
         out_shape=pltpu.VMEM((slabs, width, TILE), BF16),
-        in_specs=[SMEM] + [HBM] * 3,
+        in_specs=[SMEM, HBM],
         out_specs=VMEM,
-        scratch_shapes=[pltpu.SemaphoreType.DMA((tiles,))],
+        scratch_shapes=[pltpu.SemaphoreType.DMA((loaded,))],
         compiler_params=pltpu.CompilerParams(vmem_limit_bytes=VMEM_SMALL),
         cost_estimate=pl.CostEstimate(
-            flops=0, bytes_accessed=2 * tiles * TILE * width, transcendentals=0
+            flops=0, bytes_accessed=2 * loaded * TILE * width, transcendentals=0
         ),
         name="load_weights",
-    )(plan, w_query, w_key, value_weight)
+    )(plan, w_query)
 
 
 def section_kernel(cfg, plan, lengths, gain, *refs):
@@ -73,7 +67,7 @@
     refs = list(refs)
     blocks = [refs.pop(0) for _ in range(1 + max(s[0] for s in spots))]
     weights = refs.pop(0)
-    w_out_in = refs.pop(0) if load else None
+    w_key, value_weight, w_out_in = [refs.pop(0) for _ in range(3)] if load else [None] * 3
     if want:
         own_term, peer_term, x_own = [refs.pop(0) for _ in range(3)]
     else:
@@ -83,7 +77,7 @@
     x, normed, qkv, attended = [refs.pop(0) for _ in range(4)]
     t_other = refs.pop(0) if want else None
     sem_in = refs.pop(0)
-    sem_out = refs.pop(0) if load else None
+    sem_kv, sem_out = [refs.pop(0) for _ in range(2)] if load else [None] * 2
     qkv_tiles, out_tiles = q_tiles + 2 * k_tiles, weights.shape[1] // TILE
     rows, q_dim = attended.shape
     nm = half - ns
@@ -105,26 +99,42 @@
     def out_copy(j):
         return pltpu.make_async_copy(w_out_in.at[:, column(j)], out_tile(weights, qkv_tiles, q_dim, j), sem_out.at[j])
 
+    def kv_copies():
+        return [
+            pltpu.make_async_copy(
+                source.at[:, pl.ds(j * TILE, TILE)],
+                weights.at[q_tiles + n * k_tiles + j],
+                sem_kv.at[n * k_tiles + j],
+            )
+            for n, source in enumerate((w_key, value_weight))
+            for j in range(k_tiles)
+        ]
+
     active = plan[0] == want
+    ahead = min(4, out_tiles)
 
     @pl.when(active)
     def _():
         for copy in in_copies():
             copy.start()
 
-    def start_out():
-        for j in range(out_tiles):
-            out_copy(j).start()
-
     if load:
-        pl.when(jnp.logical_not(active))(start_out)
+
+        @pl.when(jnp.logical_not(active))
+        def _():
+            copies = kv_copies() + [out_copy(j) for j in range(out_tiles)]
+            for copy in copies:
+                copy.start()
+            for copy in copies:
+                copy.wait()
 
     @pl.when(active)
     def _():
         for copy in in_copies():
             copy.wait()
         if load:
-            start_out()
+            for copy in kv_copies():
+                copy.start()
         step = 16
 
         @pl.loop(0, rows // step)
@@ -142,11 +152,25 @@
             scale = lax.rsqrt(jnp.mean(values * values, axis=-1, keepdims=True) + EPSILON)
             normed[at, :] = (values * scale * gain[...].astype(F32)).astype(BF16)
 
-        @pl.loop(0, qkv_tiles // 2)
-        def _(pair):
-            for u in range(2):
-                j = pair * 2 + u
-                qkv[j] = jnp.dot(normed[...], weights[j], preferred_element_type=F32).astype(BF16)
+        def project(j):
+            qkv[j] = jnp.dot(normed[...], weights[j], preferred_element_type=F32).astype(BF16)
+
+        def project_pairs(first, last):
+            @pl.loop(first, last)
+            def _(pair):
+                for u in range(2):
+                    project(pair * 2 + u)
+
+        if load:
+            project_pairs(0, 1)
+            for j in range(ahead):
+                out_copy(j).start()
+            project_pairs(1, q_tiles // 2)
+            for copy in kv_copies():
+                copy.wait()
+            project_pairs(q_tiles // 2, qkv_tiles // 2)
+        else:
+            project_pairs(0, qkv_tiles // 2)
 
         mp = plan[1]
         length = lengths[round_index, slot]
@@ -189,6 +213,11 @@
                 j = pair * 2 + u
                 if load:
                     out_copy(j).wait()
+
+                    @pl.when(j + ahead < out_tiles)
+                    def _(j=j):
+                        out_copy(j + ahead).start()
+
                 term = jnp.dot(
                     attended[...],
                     out_tile(weights, qkv_tiles, q_dim, j)[...],
@@ -202,17 +231,10 @@
                     term_out[:half, column(j)] = own.astype(BF16)
                     term_out[half:, column(j)] = term[half:]
 
-    if load:
-
-        @pl.when(jnp.logical_not(active))
-        def _():
-            for j in range(out_tiles):
-                out_copy(j).wait()
-
 
 def section(plan, lengths, gain, blocks, spots, weights, w_out, dims, round_index, slot, want):
     q_tiles, k_tiles, half, ns = dims
-    load = w_out is not None
+    load = bool(w_out)
     width = weights.shape[1]
     rows, q_dim, qkv_tiles = 2 * half, q_tiles * TILE, q_tiles + 2 * k_tiles
     weights = pltpu.with_memory_space_constraint(weights, pltpu.VMEM)
@@ -222,9 +244,9 @@
         for n, b in enumerate(blocks)
     ]
     if want:
-        out_shape = [rows_of(half, width)] * 3
+        out_shape = [pltpu.VMEM((half, width), BF16)] * 3
     else:
-        out_shape = [rows_of(rows, width)]
+        out_shape = [pltpu.VMEM((rows, width), BF16)]
     aliases = {}
     if load:
         aliases[3 + len(blocks)] = len(out_shape)
@@ -239,6 +261,7 @@
         scratch.append(pltpu.VMEM((rows, width), BF16))
     scratch.append(pltpu.SemaphoreType.DMA((len(spots),)))
     if load:
+        scratch.append(pltpu.SemaphoreType.DMA((2 * k_tiles,)))
         scratch.append(pltpu.SemaphoreType.DMA((width // TILE,)))
     return pl.pallas_call(
         functools.partial(
@@ -246,7 +269,7 @@
             (round_index, slot, want, load, tuple(spots), q_tiles, k_tiles, half, ns),
         ),
         out_shape=out_shape,
-        in_specs=[SMEM, SMEM, VMEM] + [ANY] * len(blocks) + [VMEM] + [HBM] * load,
+        in_specs=[SMEM, SMEM, VMEM] + [ANY] * len(blocks) + [VMEM] + [HBM] * len(w_out),
         out_specs=[VMEM] * len(out_shape),
         scratch_shapes=scratch,
         input_output_aliases=aliases,
@@ -256,7 +279,7 @@
             bytes_accessed=2 * width * (qkv_tiles * TILE + q_dim),
             transcendentals=0,
         ),
-    )(plan, lengths, gain, *blocks, weights, *([w_out] if load else []))
+    )(plan, lengths, gain, *blocks, weights, *w_out)
 
 
 def pick_kernel(entries, count, plan, *refs):
@@ -433,7 +456,7 @@
                     (2, (), 0, False, half, nm),
                     (3, (r - 1, m), 0, False, half + nm, ns),
                 ]
-            last = w_out[0] if r == 0 and m == 0 else None
+            last = (w_key[0], value_weight[0], w_out[0]) if r == 0 and m == 0 else ()
             result = section(
                 plan, seg_lengths, norm_gain, blocks, spots, weights, last, dims, r, m, 0
             )
@@ -450,7 +473,7 @@
         next_own, next_peer = [], []
         for m in range(slots):
             own_term, peer_term, x_own = section(
-                plan, seg_lengths, norm_gain, sent[m], spots, weights, None, dims, r, m, 1
+                plan, seg_lengths, norm_gain, sent[m], spots, weights, (), dims, r, m, 1
             )
             arrived = send(peer_term, within(1))
             back = send(x_own, across(1, False))
@@ -464,7 +487,9 @@
                 next_own.append(send(routed, across(1, False)))
             values = (x_own, own_term, arrived, back)
             if r + 1 == rounds:
-                values = [pltpu.with_memory_space_constraint(v, pltpu.VMEM) for v in values]
+                values = values[:2] + tuple(
+                    pltpu.with_memory_space_constraint(v, pltpu.VMEM) for v in values[2:]
+                )
             outs = finish(plan, values, outs, shapes, r, m, nm)
         mem_own, mem_peer = next_own, next_peer
     return tuple(outs)

time: 193 us -> 190 us (0.984)
  Pallas kernels: 77.3 us -> 71.7 us
  waiting for transfers between devices: 23 us -> 26 us
  starting transfers between devices: 82.1 us -> 84.4 us
    pallas_call x8, Pallas kernels: 59.1 us -> 54.9 us  [section(): pl.pallas_call(functools.partial(section_kernel, (round_index, slot, want...]
    ppermute x32, waiting for transfers between devices: 23 us -> 26 us  [send(): return lax.ppermute(value, AXES, pairs)]
    pallas_call x1, Pallas kernels: 9.02 us -> 6.6 us  [load_weights(): pl.pallas_call(load_kernel, out_shape=pltpu.VMEM((slabs, width, TILE), BF...]
    ppermute x32, starting transfers between devices: 82.1 us -> 84.4 us  [send(): return lax.ppermute(value, AXES, pairs)]
  transfers between devices with their start and end apart: 32 -> 32, of which waited for: 5 -> 4; matrix products, arithmetic and copies ran while one was open for 2% -> 2% of each run, Pallas kernels for 36% -> 32%
where the time goes in v3:
time: 190 us; the launch traced here: 188 us
  starting transfers between devices  84.4 us (44%)
  Pallas kernels  71.7 us (38%)
  waiting for transfers between devices  26 us (14%)
  local copies, waits for them, and re-layouts  2.93 us (2%)
    ppermute x32, starting transfers between devices, send(): return lax.ppermute(value, AXES, pairs)  84.4 us
    pallas_call x8, Pallas kernels, section(): pl.pallas_call(functools.partial(section_kernel, (round_index, slot, want...  54.9 us
    ppermute x32, waiting for transfers between devices, send(): return lax.ppermute(value, AXES, pairs)  26 us
    pallas_call x4, Pallas kernels, finish(): pl.pallas_call(functools.partial(finish_kernel, (round_index, slot, nm)),...  7.69 us
    pallas_call x1, Pallas kernels, load_weights(): pl.pallas_call(load_kernel, out_shape=pltpu.VMEM((slabs, width, TILE), BF...  6.6 us
  transfers between devices with their start and end apart: 32, of which 4 were waited for; matrix products, arithmetic and copies ran while one was open for 2% of the time, Pallas kernels for 32%

profile of v3, /device:TPU:1, one launch (start us, length us, event | category | flops | bytes accessed | tf_op | source)
XLA Modules:
  0.0 188.4 jit_solution(14578790205293013067)
XLA Ops:
  5.1 6.6 %load_weights.1.refs_4_ = bf16[10,4096,512]{2,1,0:T(8,128)(2,1)S(1)} custom-call(s32[8]{0:T(128)} %pad_add_fusion.1.plan, bf16[4096,2048]{1,0:T(8,128)(2,1)} %bitcast.6), custom_call_target="tpu_custom_call" | custom-call | bytes 16777216 | tf_op jit(solution)/shard_map/load_weights/pallas_call | solution.py:51
  11.7 9.2 %shard_map.104 = (bf16[128,4096]{1,0:T(8,128)(2,1)S(1)}, bf16[10,4096,512]{2,1,0:T(8,128)(2,1)S(1)}) custom-call(s32[8]{0:T(128)} %pad_add_fusion.1.plan, s32[2,2]{1,0:T(2,128)} %lengths.15, bf16[1,4096]{1,0:T(2,128)(2,1)} %gain.15, bf16[2,32,4096]{2,1,0:T(8,128)(2,1)} %refs_0_.3, bf16[2,2,32,4096]{3,2,1,0:T(8,128)(2,1)} %refs_1_.7, ...), custom_call_target="tpu_custom_call", output_to_operand_aliasing={{1}: (7, {})} | custom-call | flops 5368709120 | bytes 41943040 | tf_op jit(solution)/shard_map/pallas_call | solution.py:266
  26.9 18.6 %collective-permute-done.18.refs_1_ = bf16[128,4096]{1,0:T(8,128)(2,1)S(1)} collective-permute-done((bf16[128,4096]{1,0:T(8,128)(2,1)S(1)}, bf16[128,4096]{1,0:T(8,128)(2,1)S(1)}, u32[]{:S(2)}, u32[]{:S(2)}) %collective-permute-start.18) | collective-permute-done | bytes 1048608 | tf_op jit(solution)/shard_map/ppermute | solution.py:382
  45.5 10.2 %shard_map.109 = (bf16[64,4096]{1,0:T(8,128)(2,1)S(1)}, bf16[64,4096]{1,0:T(8,128)(2,1)S(1)}, bf16[64,4096]{1,0:T(8,128)(2,1)S(1)}) custom-call(s32[8]{0:T(128)} %pad_add_fusion.1.plan, s32[2,2]{1,0:T(2,128)} %lengths.15, bf16[1,4096]{1,0:T(2,128)(2,1)} %gain.15, bf16[128,4096]{1,0:T(8,128)(2,1)S(1)} %collective-permute-done.17.refs_0_, ...), custom_call_target="tpu_custom_call" | custom-call | flops 5368709120 | bytes 41943040 | tf_op jit(solution)/shard_map/pallas_call | solution.py:266
  55.8 1.9 %collective-permute-start.19 = (bf16[64,4096]{1,0:T(8,128)(2,1)S(1)}, bf16[64,4096]{1,0:T(8,128)(2,1)S(1)}, u32[]{:S(2)}, u32[]{:S(2)}) collective-permute-start(bf16[64,4096]{1,0:T(8,128)(2,1)S(1)} %get-tuple-element.38), channel_id=1, source_target_pairs={{16,17},{17,16},{18,19},{19,18},{20,21},{21,20},{22,23},{23,22},{2... | collective-permute-start | bytes 1572872 | tf_op jit(solution)/shard_map/ppermute | solution.py:382
  57.7 3.4 %collective-permute-start.11 = (bf16[1,2,32,4096]{3,2,1,0:T(8,128)(2,1)S(1)}, bf16[1,2,32,4096]{3,2,1,0:T(8,128)(2,1)S(1)}, u32[]{:S(2)}, u32[]{:S(2)}) collective-permute-start(bf16[1,2,32,4096]{3,2,1,0:T(8,128)(2,1)S(1)} %get-tuple-element.50), channel_id=1, source_target_pairs={{16,17},{17,16},{18,19},{19,18},{20,21},{21,20},{22,23},{23,22},{2... | collective-permute-start | bytes 1572872 | tf_op jit(solution)/shard_map/ppermute | solution.py:382
  61.1 10.4 %shard_map.106 = (bf16[64,4096]{1,0:T(8,128)(2,1)S(1)}, bf16[64,4096]{1,0:T(8,128)(2,1)S(1)}, bf16[64,4096]{1,0:T(8,128)(2,1)S(1)}) custom-call(s32[8]{0:T(128)} %pad_add_fusion.1.plan, s32[2,2]{1,0:T(2,128)} %lengths.15, bf16[1,4096]{1,0:T(2,128)(2,1)} %gain.15, bf16[128,4096]{1,0:T(8,128)(2,1)S(1)} %collective-permute-done.2.refs_0_, ...), custom_call_target="tpu_custom_call" | custom-call | flops 5368709120 | bytes 41943040 | tf_op jit(solution)/shard_map/pallas_call | solution.py:266
  71.5 1.9 %collective-permute-start.4 = (bf16[64,4096]{1,0:T(8,128)(2,1)S(1)}, bf16[64,4096]{1,0:T(8,128)(2,1)S(1)}, u32[]{:S(2)}, u32[]{:S(2)}) collective-permute-start(bf16[64,4096]{1,0:T(8,128)(2,1)S(1)} %get-tuple-element.29), channel_id=1, source_target_pairs={{16,17},{17,16},{18,19},{19,18},{20,21},{21,20},{22,23},{23,22},{2... | collective-permute-start | bytes 1572872 | tf_op jit(solution)/shard_map/ppermute | solution.py:382
  73.6 5.5 %collective-permute-start.22 = (bf16[32,4096]{1,0:T(8,128)(2,1)S(1)}, bf16[32,4096]{1,0:T(8,128)(2,1)S(1)}, u32[]{:S(2)}, u32[]{:S(2)}) collective-permute-start(bf16[32,4096]{1,0:T(8,128)(2,1)S(1)} %add_convert_fusion.refs_0_), channel_id=1, source_target_pairs={{16,28},{17,29},{18,30},{19,31},{20,24},{21,25},{22,26},{23,27},{2... | collective-permute-start | bytes 786440 | tf_op jit(solution)/shard_map/ppermute | solution.py:382
  79.1 1.9 %collective-permute-start.21 = (bf16[32,4096]{1,0:T(8,128)(2,1)S(1)}, bf16[32,4096]{1,0:T(8,128)(2,1)S(1)}, u32[]{:S(2)}, u32[]{:S(2)}) collective-permute-start(bf16[32,4096]{1,0:T(8,128)(2,1)S(1)} %add_convert_fusion.refs_0_), channel_id=1, source_target_pairs={{16,24},{17,25},{18,26},{19,27},{20,28},{21,29},{22,30},{23,31},{2... | collective-permute-start | bytes 786440 | tf_op jit(solution)/shard_map/ppermute | solution.py:382
  81.0 2.2 %collective-permute-start.20 = (bf16[32,4096]{1,0:T(8,128)(2,1)S(1)}, bf16[32,4096]{1,0:T(8,128)(2,1)S(1)}, u32[]{:S(2)}, u32[]{:S(2)}) collective-permute-start(bf16[32,4096]{1,0:T(8,128)(2,1)S(1)} %add_convert_fusion.refs_0_), channel_id=1, source_target_pairs={{16,20},{17,21},{18,22},{19,23},{20,16},{21,17},{22,18},{23,19},{2... | collective-permute-start | bytes 786440 | tf_op jit(solution)/shard_map/ppermute | solution.py:382
  83.3 5.2 %collective-permute-start.7 = (bf16[32,4096]{1,0:T(8,128)(2,1)S(1)}, bf16[32,4096]{1,0:T(8,128)(2,1)S(1)}, u32[]{:S(2)}, u32[]{:S(2)}) collective-permute-start(bf16[32,4096]{1,0:T(8,128)(2,1)S(1)} %add_convert_fusion.1.refs_0_), channel_id=1, source_target_pairs={{16,28},{17,29},{18,30},{19,31},{20,24},{21,25},{22,26},{23,27},{2... | collective-permute-start | bytes 786440 | tf_op jit(solution)/shard_map/ppermute | solution.py:382
  88.5 2.3 %collective-permute-start.6 = (bf16[32,4096]{1,0:T(8,128)(2,1)S(1)}, bf16[32,4096]{1,0:T(8,128)(2,1)S(1)}, u32[]{:S(2)}, u32[]{:S(2)}) collective-permute-start(bf16[32,4096]{1,0:T(8,128)(2,1)S(1)} %add_convert_fusion.1.refs_0_), channel_id=1, source_target_pairs={{16,24},{17,25},{18,26},{19,27},{20,28},{21,29},{22,30},{23,31},{2... | collective-permute-start | bytes 786440 | tf_op jit(solution)/shard_map/ppermute | solution.py:382
  90.8 5.3 %collective-permute-done.21.refs_2_ = bf16[32,4096]{1,0:T(8,128)(2,1)S(1)} collective-permute-done((bf16[32,4096]{1,0:T(8,128)(2,1)S(1)}, bf16[32,4096]{1,0:T(8,128)(2,1)S(1)}, u32[]{:S(2)}, u32[]{:S(2)}) %collective-permute-start.21) | collective-permute-done | bytes 262176 | tf_op jit(solution)/shard_map/ppermute | solution.py:382
  96.0 1.9 %collective-permute-start.5 = (bf16[32,4096]{1,0:T(8,128)(2,1)S(1)}, bf16[32,4096]{1,0:T(8,128)(2,1)S(1)}, u32[]{:S(2)}, u32[]{:S(2)}) collective-permute-start(bf16[32,4096]{1,0:T(8,128)(2,1)S(1)} %add_convert_fusion.1.refs_0_), channel_id=1, source_target_pairs={{16,20},{17,21},{18,22},{19,23},{20,16},{21,17},{22,18},{23,19},{2... | collective-permute-start | bytes 786440 | tf_op jit(solution)/shard_map/ppermute | solution.py:382
  98.6 3.1 %collective-permute-start.23 = (bf16[32,4096]{1,0:T(8,128)(2,1)S(1)}, bf16[32,4096]{1,0:T(8,128)(2,1)S(1)}, u32[]{:S(2)}, u32[]{:S(2)}) collective-permute-start(bf16[32,4096]{1,0:T(8,128)(2,1)S(1)} %get-tuple-element.40), channel_id=1, source_target_pairs={{16,18},{17,19},{18,16},{19,17},{20,22},{21,23},{22,20},{23,21},{2... | collective-permute-start | bytes 786440 | tf_op jit(solution)/shard_map/ppermute | solution.py:382
  101.8 1.3 collective-permute-start.12
  105.1 3.1 %collective-permute-start.8 = (bf16[32,4096]{1,0:T(8,128)(2,1)S(1)}, bf16[32,4096]{1,0:T(8,128)(2,1)S(1)}, u32[]{:S(2)}, u32[]{:S(2)}) collective-permute-start(bf16[32,4096]{1,0:T(8,128)(2,1)S(1)} %get-tuple-element.31), channel_id=1, source_target_pairs={{16,18},{17,19},{18,16},{19,17},{20,22},{21,23},{22,20},{23,21},{2... | collective-permute-start | bytes 786440 | tf_op jit(solution)/shard_map/ppermute | solution.py:382
  108.9 1.3 collective-permute-start.25
  110.2 1.3 collective-permute-start.24
  123.0 23.6 %collective-permute-start.30 = (bf16[64,4096]{1,0:T(8,128)(2,1)S(1)}, bf16[64,4096]{1,0:T(8,128)(2,1)}, u32[]{:S(2)}, u32[]{:S(2)}) collective-permute-start(bf16[64,4096]{1,0:T(8,128)(2,1)S(1)} %get-tuple-element.27.x_own), channel_id=1, source_target_pairs={{16,0},{17,1},{18,2},{19,3},{20,4},{21,5},{22,6},{23,7},{24,8},{25... | collective-permute-start | bytes 1572872 | tf_op jit(solution)/shard_map/ppermute | solution.py:382
  146.6 2.1 %collective-permute-start.31 = (bf16[64,4096]{1,0:T(8,128)(2,1)S(1)}, bf16[64,4096]{1,0:T(8,128)(2,1)}, u32[]{:S(2)}, u32[]{:S(2)}) collective-permute-start(bf16[64,4096]{1,0:T(8,128)(2,1)S(1)} %get-tuple-element.36.x_own), channel_id=1, source_target_pairs={{16,0},{17,1},{18,2},{19,3},{20,4},{21,5},{22,6},{23,7},{24,8},{25... | collective-permute-start | bytes 1572872 | tf_op jit(solution)/shard_map/ppermute | solution.py:382
  148.7 12.5 %shard_map.111 = (bf16[64,4096]{1,0:T(8,128)(2,1)S(1)}, bf16[64,4096]{1,0:T(8,128)(2,1)}, bf16[64,4096]{1,0:T(8,128)(2,1)}) custom-call(s32[8]{0:T(128)} %pad_add_fusion.1.plan, s32[2,2]{1,0:T(2,128)} %lengths.15, bf16[1,4096]{1,0:T(2,128)(2,1)} %gain.15, bf16[128,4096]{1,0:T(8,128)(2,1)} %collective-permute-done.26.refs_0_, ...), custom_call_target="tpu_custom_call" | custom-call | flops 5368709120 | bytes 41943040 | tf_op jit(solution)/shard_map/pallas_call | solution.py:266
  162.0 2.2 %collective-permute-start.28 = (bf16[64,4096]{1,0:T(8,128)(2,1)}, bf16[64,4096]{1,0:T(8,128)(2,1)S(1)}, u32[]{:S(2)}, u32[]{:S(2)}) collective-permute-start(bf16[64,4096]{1,0:T(8,128)(2,1)} %get-tuple-element.43), channel_id=1, source_target_pairs={{16,17},{17,16},{18,19},{19,18},{20,21},{21,20},{22,23},{23,22},{2... | collective-permute-start | bytes 1572872 | tf_op jit(solution)/shard_map/ppermute | solution.py:382
  164.2 1.5 collective-permute-start.29
  165.7 10.2 %shard_map.108 = (bf16[64,4096]{1,0:T(8,128)(2,1)S(1)}, bf16[64,4096]{1,0:T(8,128)(2,1)S(1)}, bf16[64,4096]{1,0:T(8,128)(2,1)S(1)}) custom-call(s32[8]{0:T(128)} %pad_add_fusion.1.plan, s32[2,2]{1,0:T(2,128)} %lengths.15, bf16[1,4096]{1,0:T(2,128)(2,1)} %gain.15, bf16[128,4096]{1,0:T(8,128)(2,1)S(1)} %collective-permute-done.13.refs_0_, ...), custom_call_target="tpu_custom_call" | custom-call | flops 5368709120 | bytes 41943040 | tf_op jit(solution)/shard_map/pallas_call | solution.py:266
  175.9 3.1 %collective-permute-start.15 = (bf16[64,4096]{1,0:T(8,128)(2,1)S(1)}, bf16[64,4096]{1,0:T(8,128)(2,1)S(1)}, u32[]{:S(2)}, u32[]{:S(2)}) collective-permute-start(bf16[64,4096]{1,0:T(8,128)(2,1)S(1)} %get-tuple-element.34), channel_id=1, source_target_pairs={{16,17},{17,16},{18,19},{19,18},{20,21},{21,20},{22,23},{23,22},{2... | collective-permute-start | bytes 1572872 | tf_op jit(solution)/shard_map/ppermute | solution.py:382
  179.1 1.3 collective-permute-start.16
  180.4 1.7 shard_map.112
  182.1 1.7 shard_map.113
  183.8 2.6 %shard_map.114 = (bf16[1,2,2,32,4096]{4,3,2,1,0:T(8,128)(2,1)}, bf16[1,2,2,32,4096]{4,3,2,1,0:T(8,128)(2,1)}) custom-call(s32[8]{0:T(128)S(1)} %copy-done.3, bf16[64,4096]{1,0:T(8,128)(2,1)} %get-tuple-element.41.x_own, bf16[64,4096]{1,0:T(8,128)(2,1)S(1)} %copy-done.1, ...), custom_call_target="tpu_custom_call", output_to_operand_aliasing={{0}: (5, {}), {1}: (6, {})} | custom-call | tf_op jit(solution)/shard_map/pallas_call | solution.py:355
  186.5 1.7 shard_map.115
  (69 shorter events, 26.0 us)
Async XLA Ops:
  0.6 11.1 %collective-permute-start = (bf16[2,32,4096]{2,1,0:T(8,128)(2,1)}, bf16[2,32,4096]{2,1,0:T(8,128)(2,1)S(1)}, u32[]{:S(2)}, u32[]{:S(2)}) collective-permute-start(bf16[2,32,4096]{2,1,0:T(8,128)(2,1)} %refs_0_.3), channel_id=1, source_target_pairs={{0,1},{1,0},{2,3},{3,2},{4,5},{5,4},{6,7},{7,6},{8,9},{9,8},{10,11... | collective-permute-start | bytes 1572872 | tf_op jit(solution)/shard_map/ppermute | solution.py:382
  2.6 9.1 %collective-permute-start.1 = (bf16[1,2,32,4096]{3,2,1,0:T(8,128)(2,1)S(1)}, bf16[1,2,32,4096]{3,2,1,0:T(8,128)(2,1)S(1)}, u32[]{:S(2)}, u32[]{:S(2)}) collective-permute-start(bf16[1,2,32,4096]{3,2,1,0:T(8,128)(2,1)S(1)} %get-tuple-element.51), channel_id=1, source_target_pairs={{0,1},{1,0},{2,3},{3,2},{4,5},{5,4},{6,7},{7,6},{8,9},{9,8},{10,11... | collective-permute-start | bytes 1572872 | tf_op jit(solution)/shard_map/ppermute | solution.py:382
  20.9 24.6 %collective-permute-start.18 = (bf16[128,4096]{1,0:T(8,128)(2,1)S(1)}, bf16[128,4096]{1,0:T(8,128)(2,1)S(1)}, u32[]{:S(2)}, u32[]{:S(2)}) collective-permute-start(bf16[128,4096]{1,0:T(8,128)(2,1)S(1)} %get-tuple-element.35), channel_id=1, source_target_pairs={{0,17},{1,16},{2,19},{3,18},{4,21},{5,20},{6,23},{7,22},{8,25},{9,... | collective-permute-start | bytes 3145736 | tf_op jit(solution)/shard_map/ppermute | solution.py:382
  22.2 23.3 %collective-permute-start.17 = (bf16[128,4096]{1,0:T(8,128)(2,1)S(1)}, bf16[128,4096]{1,0:T(8,128)(2,1)S(1)}, u32[]{:S(2)}, u32[]{:S(2)}) collective-permute-start(bf16[128,4096]{1,0:T(8,128)(2,1)S(1)} %get-tuple-element.35), channel_id=1, source_target_pairs={{0,16},{1,17},{2,18},{3,19},{4,20},{5,21},{6,22},{7,23},{8,24},{9,... | collective-permute-start | bytes 3145736 | tf_op jit(solution)/shard_map/ppermute | solution.py:382
  24.3 36.8 %collective-permute-start.3 = (bf16[128,4096]{1,0:T(8,128)(2,1)S(1)}, bf16[128,4096]{1,0:T(8,128)(2,1)S(1)}, u32[]{:S(2)}, u32[]{:S(2)}) collective-permute-start(bf16[128,4096]{1,0:T(8,128)(2,1)S(1)} %shard_map.105), channel_id=1, source_target_pairs={{0,17},{1,16},{2,19},{3,18},{4,21},{5,20},{6,23},{7,22},{8,25},{9,... | collective-permute-start | bytes 3145736 | tf_op jit(solution)/shard_map/ppermute | solution.py:382
  25.6 35.5 %collective-permute-start.2 = (bf16[128,4096]{1,0:T(8,128)(2,1)S(1)}, bf16[128,4096]{1,0:T(8,128)(2,1)S(1)}, u32[]{:S(2)}, u32[]{:S(2)}) collective-permute-start(bf16[128,4096]{1,0:T(8,128)(2,1)S(1)} %shard_map.105), channel_id=1, source_target_pairs={{0,16},{1,17},{2,18},{3,19},{4,20},{5,21},{6,22},{7,23},{8,24},{9,... | collective-permute-start | bytes 3145736 | tf_op jit(solution)/shard_map/ppermute | solution.py:382
  55.8 17.7 %collective-permute-start.19 = (bf16[64,4096]{1,0:T(8,128)(2,1)S(1)}, bf16[64,4096]{1,0:T(8,128)(2,1)S(1)}, u32[]{:S(2)}, u32[]{:S(2)}) collective-permute-start(bf16[64,4096]{1,0:T(8,128)(2,1)S(1)} %get-tuple-element.38), channel_id=1, source_target_pairs={{16,17},{17,16},{18,19},{19,18},{20,21},{21,20},{22,23},{23,22},{2... | collective-permute-start | bytes 1572872 | tf_op jit(solution)/shard_map/ppermute | solution.py:382
  57.7 44.1 %collective-permute-start.11 = (bf16[1,2,32,4096]{3,2,1,0:T(8,128)(2,1)S(1)}, bf16[1,2,32,4096]{3,2,1,0:T(8,128)(2,1)S(1)}, u32[]{:S(2)}, u32[]{:S(2)}) collective-permute-start(bf16[1,2,32,4096]{3,2,1,0:T(8,128)(2,1)S(1)} %get-tuple-element.50), channel_id=1, source_target_pairs={{16,17},{17,16},{18,19},{19,18},{20,21},{21,20},{22,23},{23,22},{2... | collective-permute-start | bytes 1572872 | tf_op jit(solution)/shard_map/ppermute | solution.py:382
  71.5 11.7 %collective-permute-start.4 = (bf16[64,4096]{1,0:T(8,128)(2,1)S(1)}, bf16[64,4096]{1,0:T(8,128)(2,1)S(1)}, u32[]{:S(2)}, u32[]{:S(2)}) collective-permute-start(bf16[64,4096]{1,0:T(8,128)(2,1)S(1)} %get-tuple-element.29), channel_id=1, source_target_pairs={{16,17},{17,16},{18,19},{19,18},{20,21},{21,20},{22,23},{23,22},{2... | collective-permute-start | bytes 1572872 | tf_op jit(solution)/shard_map/ppermute | solution.py:382
  73.6 14.9 %collective-permute-start.22 = (bf16[32,4096]{1,0:T(8,128)(2,1)S(1)}, bf16[32,4096]{1,0:T(8,128)(2,1)S(1)}, u32[]{:S(2)}, u32[]{:S(2)}) collective-permute-start(bf16[32,4096]{1,0:T(8,128)(2,1)S(1)} %add_convert_fusion.refs_0_), channel_id=1, source_target_pairs={{16,28},{17,29},{18,30},{19,31},{20,24},{21,25},{22,26},{23,27},{2... | collective-permute-start | bytes 786440 | tf_op jit(solution)/shard_map/ppermute | solution.py:382
  79.1 17.0 %collective-permute-start.21 = (bf16[32,4096]{1,0:T(8,128)(2,1)S(1)}, bf16[32,4096]{1,0:T(8,128)(2,1)S(1)}, u32[]{:S(2)}, u32[]{:S(2)}) collective-permute-start(bf16[32,4096]{1,0:T(8,128)(2,1)S(1)} %add_convert_fusion.refs_0_), channel_id=1, source_target_pairs={{16,24},{17,25},{18,26},{19,27},{20,28},{21,29},{22,30},{23,31},{2... | collective-permute-start | bytes 786440 | tf_op jit(solution)/shard_map/ppermute | solution.py:382
  81.0 17.0 %collective-permute-start.20 = (bf16[32,4096]{1,0:T(8,128)(2,1)S(1)}, bf16[32,4096]{1,0:T(8,128)(2,1)S(1)}, u32[]{:S(2)}, u32[]{:S(2)}) collective-permute-start(bf16[32,4096]{1,0:T(8,128)(2,1)S(1)} %add_convert_fusion.refs_0_), channel_id=1, source_target_pairs={{16,20},{17,21},{18,22},{19,23},{20,16},{21,17},{22,18},{23,19},{2... | collective-permute-start | bytes 786440 | tf_op jit(solution)/shard_map/ppermute | solution.py:382
  83.3 19.8 %collective-permute-start.7 = (bf16[32,4096]{1,0:T(8,128)(2,1)S(1)}, bf16[32,4096]{1,0:T(8,128)(2,1)S(1)}, u32[]{:S(2)}, u32[]{:S(2)}) collective-permute-start(bf16[32,4096]{1,0:T(8,128)(2,1)S(1)} %add_convert_fusion.1.refs_0_), channel_id=1, source_target_pairs={{16,28},{17,29},{18,30},{19,31},{20,24},{21,25},{22,26},{23,27},{2... | collective-permute-start | bytes 786440 | tf_op jit(solution)/shard_map/ppermute | solution.py:382
  88.5 14.7 %collective-permute-start.6 = (bf16[32,4096]{1,0:T(8,128)(2,1)S(1)}, bf16[32,4096]{1,0:T(8,128)(2,1)S(1)}, u32[]{:S(2)}, u32[]{:S(2)}) collective-permute-start(bf16[32,4096]{1,0:T(8,128)(2,1)S(1)} %add_convert_fusion.1.refs_0_), channel_id=1, source_target_pairs={{16,24},{17,25},{18,26},{19,27},{20,28},{21,29},{22,30},{23,31},{2... | collective-permute-start | bytes 786440 | tf_op jit(solution)/shard_map/ppermute | solution.py:382
  96.0 8.4 %collective-permute-start.5 = (bf16[32,4096]{1,0:T(8,128)(2,1)S(1)}, bf16[32,4096]{1,0:T(8,128)(2,1)S(1)}, u32[]{:S(2)}, u32[]{:S(2)}) collective-permute-start(bf16[32,4096]{1,0:T(8,128)(2,1)S(1)} %add_convert_fusion.1.refs_0_), channel_id=1, source_target_pairs={{16,20},{17,21},{18,22},{19,23},{20,16},{21,17},{22,18},{23,19},{2... | collective-permute-start | bytes 786440 | tf_op jit(solution)/shard_map/ppermute | solution.py:382
  98.6 9.6 %collective-permute-start.23 = (bf16[32,4096]{1,0:T(8,128)(2,1)S(1)}, bf16[32,4096]{1,0:T(8,128)(2,1)S(1)}, u32[]{:S(2)}, u32[]{:S(2)}) collective-permute-start(bf16[32,4096]{1,0:T(8,128)(2,1)S(1)} %get-tuple-element.40), channel_id=1, source_target_pairs={{16,18},{17,19},{18,16},{19,17},{20,22},{21,23},{22,20},{23,21},{2... | collective-permute-start | bytes 786440 | tf_op jit(solution)/shard_map/ppermute | solution.py:382
  101.8 13.7 %collective-permute-start.12 = (bf16[1,2,32,4096]{3,2,1,0:T(8,128)(2,1)S(1)}, bf16[1,2,32,4096]{3,2,1,0:T(8,128)(2,1)S(1)}, u32[]{:S(2)}, u32[]{:S(2)}) collective-permute-start(bf16[1,2,32,4096]{3,2,1,0:T(8,128)(2,1)S(1)} %collective-permute-done.11), channel_id=1, source_target_pairs={{16,0},{17,1},{18,2},{19,3},{20,4},{21,5},{22,6},{23,7},{24,8},{25... | collective-permute-start | bytes 1572872 | tf_op jit(solution)/shard_map/ppermute | solution.py:382
  105.1 7.1 %collective-permute-start.8 = (bf16[32,4096]{1,0:T(8,128)(2,1)S(1)}, bf16[32,4096]{1,0:T(8,128)(2,1)S(1)}, u32[]{:S(2)}, u32[]{:S(2)}) collective-permute-start(bf16[32,4096]{1,0:T(8,128)(2,1)S(1)} %get-tuple-element.31), channel_id=1, source_target_pairs={{16,18},{17,19},{18,16},{19,17},{20,22},{21,23},{22,20},{23,21},{2... | collective-permute-start | bytes 786440 | tf_op jit(solution)/shard_map/ppermute | solution.py:382
  108.9 6.6 %collective-permute-start.25 = (bf16[32,4096]{1,0:T(8,128)(2,1)S(1)}, bf16[32,4096]{1,0:T(8,128)(2,1)S(1)}, u32[]{:S(2)}, u32[]{:S(2)}) collective-permute-start(bf16[32,4096]{1,0:T(8,128)(2,1)S(1)} %pick.7), channel_id=1, source_target_pairs={{16,1},{17,0},{18,3},{19,2},{20,5},{21,4},{22,7},{23,6},{24,9},{25... | collective-permute-start | bytes 786440 | tf_op jit(solution)/shard_map/ppermute | solution.py:382
  110.2 5.3 %collective-permute-start.24 = (bf16[32,4096]{1,0:T(8,128)(2,1)S(1)}, bf16[32,4096]{1,0:T(8,128)(2,1)S(1)}, u32[]{:S(2)}, u32[]{:S(2)}) collective-permute-start(bf16[32,4096]{1,0:T(8,128)(2,1)S(1)} %pick.7), channel_id=1, source_target_pairs={{16,0},{17,1},{18,2},{19,3},{20,4},{21,5},{22,6},{23,7},{24,8},{25... | collective-permute-start | bytes 786440 | tf_op jit(solution)/shard_map/ppermute | solution.py:382
  112.8 6.8 %collective-permute-start.10 = (bf16[32,4096]{1,0:T(8,128)(2,1)S(1)}, bf16[32,4096]{1,0:T(8,128)(2,1)S(1)}, u32[]{:S(2)}, u32[]{:S(2)}) collective-permute-start(bf16[32,4096]{1,0:T(8,128)(2,1)S(1)} %pick.5), channel_id=1, source_target_pairs={{16,1},{17,0},{18,3},{19,2},{20,5},{21,4},{22,7},{23,6},{24,9},{25... | collective-permute-start | bytes 786440 | tf_op jit(solution)/shard_map/ppermute | solution.py:382
  114.1 5.5 %collective-permute-start.9 = (bf16[32,4096]{1,0:T(8,128)(2,1)S(1)}, bf16[32,4096]{1,0:T(8,128)(2,1)S(1)}, u32[]{:S(2)}, u32[]{:S(2)}) collective-permute-start(bf16[32,4096]{1,0:T(8,128)(2,1)S(1)} %pick.5), channel_id=1, source_target_pairs={{16,0},{17,1},{18,2},{19,3},{20,4},{21,5},{22,6},{23,7},{24,8},{25... | collective-permute-start | bytes 786440 | tf_op jit(solution)/shard_map/ppermute | solution.py:382
  117.0 29.6 %collective-permute-start.27 = (bf16[128,4096]{1,0:T(8,128)(2,1)S(1)}, bf16[128,4096]{1,0:T(8,128)(2,1)S(1)}, u32[]{:S(2)}, u32[]{:S(2)}) collective-permute-start(bf16[128,4096]{1,0:T(8,128)(2,1)S(1)} %shard_map.110), channel_id=1, source_target_pairs={{0,17},{1,16},{2,19},{3,18},{4,21},{5,20},{6,23},{7,22},{8,25},{9,... | collective-permute-start | bytes 3145736 | tf_op jit(solution)/shard_map/ppermute | solution.py:382
  118.3 30.4 %collective-permute-start.26 = (bf16[128,4096]{1,0:T(8,128)(2,1)S(1)}, bf16[128,4096]{1,0:T(8,128)(2,1)}, u32[]{:S(2)}, u32[]{:S(2)}) collective-permute-start(bf16[128,4096]{1,0:T(8,128)(2,1)S(1)} %shard_map.110), channel_id=1, source_target_pairs={{0,16},{1,17},{2,18},{3,19},{4,20},{5,21},{6,22},{7,23},{8,24},{9,... | collective-permute-start | bytes 3145736 | tf_op jit(solution)/shard_map/ppermute | solution.py:382
  120.5 43.7 %collective-permute-start.14 = (bf16[128,4096]{1,0:T(8,128)(2,1)S(1)}, bf16[128,4096]{1,0:T(8,128)(2,1)S(1)}, u32[]{:S(2)}, u32[]{:S(2)}) collective-permute-start(bf16[128,4096]{1,0:T(8,128)(2,1)S(1)} %shard_map.107), channel_id=1, source_target_pairs={{0,17},{1,16},{2,19},{3,18},{4,21},{5,20},{6,23},{7,22},{8,25},{9,... | collective-permute-start | bytes 3145736 | tf_op jit(solution)/shard_map/ppermute | solution.py:382
  121.8 43.9 %collective-permute-start.13 = (bf16[128,4096]{1,0:T(8,128)(2,1)S(1)}, bf16[128,4096]{1,0:T(8,128)(2,1)S(1)}, u32[]{:S(2)}, u32[]{:S(2)}) collective-permute-start(bf16[128,4096]{1,0:T(8,128)(2,1)S(1)} %shard_map.107), channel_id=1, source_target_pairs={{0,16},{1,17},{2,18},{3,19},{4,20},{5,21},{6,22},{7,23},{8,24},{9,... | collective-permute-start | bytes 3145736 | tf_op jit(solution)/shard_map/ppermute | solution.py:382
  123.0 59.0 %collective-permute-start.30 = (bf16[64,4096]{1,0:T(8,128)(2,1)S(1)}, bf16[64,4096]{1,0:T(8,128)(2,1)}, u32[]{:S(2)}, u32[]{:S(2)}) collective-permute-start(bf16[64,4096]{1,0:T(8,128)(2,1)S(1)} %get-tuple-element.27.x_own), channel_id=1, source_target_pairs={{16,0},{17,1},{18,2},{19,3},{20,4},{21,5},{22,6},{23,7},{24,8},{25... | collective-permute-start | bytes 1572872 | tf_op jit(solution)/shard_map/ppermute | solution.py:382
  146.6 32.4 %collective-permute-start.31 = (bf16[64,4096]{1,0:T(8,128)(2,1)S(1)}, bf16[64,4096]{1,0:T(8,128)(2,1)}, u32[]{:S(2)}, u32[]{:S(2)}) collective-permute-start(bf16[64,4096]{1,0:T(8,128)(2,1)S(1)} %get-tuple-element.36.x_own), channel_id=1, source_target_pairs={{16,0},{17,1},{18,2},{19,3},{20,4},{21,5},{22,6},{23,7},{24,8},{25... | collective-permute-start | bytes 1572872 | tf_op jit(solution)/shard_map/ppermute | solution.py:382
  162.0 21.8 %collective-permute-start.28 = (bf16[64,4096]{1,0:T(8,128)(2,1)}, bf16[64,4096]{1,0:T(8,128)(2,1)S(1)}, u32[]{:S(2)}, u32[]{:S(2)}) collective-permute-start(bf16[64,4096]{1,0:T(8,128)(2,1)} %get-tuple-element.43), channel_id=1, source_target_pairs={{16,17},{17,16},{18,19},{19,18},{20,21},{21,20},{22,23},{23,22},{2... | collective-permute-start | bytes 1572872 | tf_op jit(solution)/shard_map/ppermute | solution.py:382
  164.2 19.6 %collective-permute-start.29 = (bf16[64,4096]{1,0:T(8,128)(2,1)}, bf16[64,4096]{1,0:T(8,128)(2,1)S(1)}, u32[]{:S(2)}, u32[]{:S(2)}) collective-permute-start(bf16[64,4096]{1,0:T(8,128)(2,1)} %get-tuple-element.41.x_own), channel_id=1, source_target_pairs={{16,0},{17,1},{18,2},{19,3},{20,4},{21,5},{22,6},{23,7},{24,8},{25... | collective-permute-start | bytes 1572872 | tf_op jit(solution)/shard_map/ppermute | solution.py:382
  175.9 10.5 %collective-permute-start.15 = (bf16[64,4096]{1,0:T(8,128)(2,1)S(1)}, bf16[64,4096]{1,0:T(8,128)(2,1)S(1)}, u32[]{:S(2)}, u32[]{:S(2)}) collective-permute-start(bf16[64,4096]{1,0:T(8,128)(2,1)S(1)} %get-tuple-element.34), channel_id=1, source_target_pairs={{16,17},{17,16},{18,19},{19,18},{20,21},{21,20},{22,23},{23,22},{2... | collective-permute-start | bytes 1572872 | tf_op jit(solution)/shard_map/ppermute | solution.py:382
  179.1 7.4 %collective-permute-start.16 = (bf16[64,4096]{1,0:T(8,128)(2,1)S(1)}, bf16[64,4096]{1,0:T(8,128)(2,1)S(1)}, u32[]{:S(2)}, u32[]{:S(2)}) collective-permute-start(bf16[64,4096]{1,0:T(8,128)(2,1)S(1)} %get-tuple-element.32.x_own), channel_id=1, source_target_pairs={{16,0},{17,1},{18,2},{19,3},{20,4},{21,5},{22,6},{23,7},{24,8},{25... | collective-permute-start | bytes 1572872 | tf_op jit(solution)/shard_map/ppermute | solution.py:382
  (5 other events, 77.7 us)

commit v4 on v3

--- a/solution.py
+++ b/solution.py
@@ -419,7 +419,18 @@
 
     def route(m, rows):
         base = 2 + m * entries
-        held = [rows] + [send(rows, along(k, 0)) for k in range(1, outer)]
+        held = {0: rows}
+        if outer & (outer - 1) == 0:
+            bit = outer // 2
+            while bit:
+                for k in sorted(held, reverse=True):
+                    if k ^ bit not in held:
+                        held[k ^ bit] = send(held[k], along(bit, 0))
+                bit //= 2
+        else:
+            for k in range(1, outer):
+                held[k] = send(rows, along(k, 0))
+        held = [held[k] for k in range(outer)]
         picked = pick(plan, [base + k for k in range(inner)], held)
         if inner == 1:
             return picked[0]

time: 190 us -> 188 us (0.989)
  transfers between devices with their start and end apart: 32 -> 32, of which waited for: 4 -> 6; matrix products, arithmetic and copies ran while one was open for 2% -> 2% of each run, Pallas kernels for 32% -> 33%
where the time goes in v4:
time: 188 us; the launch traced here: 186 us
  starting transfers between devices  83.5 us (44%)
  Pallas kernels  71.7 us (38%)
  waiting for transfers between devices  24.9 us (13%)
  local copies, waits for them, and re-layouts  2.93 us (2%)
    ppermute x32, starting transfers between devices, send(): return lax.ppermute(value, AXES, pairs)  83.5 us
    pallas_call x8, Pallas kernels, section(): pl.pallas_call(functools.partial(section_kernel, (round_index, slot, want...  54.9 us
    ppermute x32, waiting for transfers between devices, send(): return lax.ppermute(value, AXES, pairs)  24.9 us
    pallas_call x4, Pallas kernels, finish(): pl.pallas_call(functools.partial(finish_kernel, (round_index, slot, nm)),...  7.68 us
    pallas_call x1, Pallas kernels, load_weights(): pl.pallas_call(load_kernel, out_shape=pltpu.VMEM((slabs, width, TILE), BF...  6.6 us
  transfers between devices with their start and end apart: 32, of which 6 were waited for; matrix products, arithmetic and copies ran while one was open for 2% of the time, Pallas kernels for 33%

profile of v4, /device:TPU:1, one launch (start us, length us, event | category | flops | bytes accessed | tf_op | source)
XLA Modules:
  0.0 186.3 jit_solution(9089695708628909171)
XLA Ops:
  5.1 6.6 %load_weights.1.refs_4_ = bf16[10,4096,512]{2,1,0:T(8,128)(2,1)S(1)} custom-call(s32[8]{0:T(128)} %pad_add_fusion.1.plan, bf16[4096,2048]{1,0:T(8,128)(2,1)} %bitcast.6), custom_call_target="tpu_custom_call" | custom-call | bytes 16777216 | tf_op jit(solution)/shard_map/load_weights/pallas_call | solution.py:51
  11.7 9.2 %shard_map.104 = (bf16[128,4096]{1,0:T(8,128)(2,1)S(1)}, bf16[10,4096,512]{2,1,0:T(8,128)(2,1)S(1)}) custom-call(s32[8]{0:T(128)} %pad_add_fusion.1.plan, s32[2,2]{1,0:T(2,128)} %lengths.15, bf16[1,4096]{1,0:T(2,128)(2,1)} %gain.15, bf16[2,32,4096]{2,1,0:T(8,128)(2,1)} %refs_0_.3, bf16[2,2,32,4096]{3,2,1,0:T(8,128)(2,1)} %refs_1_.7, ...), custom_call_target="tpu_custom_call", output_to_operand_aliasing={{1}: (7, {})} | custom-call | flops 5368709120 | bytes 41943040 | tf_op jit(solution)/shard_map/pallas_call | solution.py:266
  26.9 18.6 %collective-permute-done.18.refs_1_ = bf16[128,4096]{1,0:T(8,128)(2,1)S(1)} collective-permute-done((bf16[128,4096]{1,0:T(8,128)(2,1)S(1)}, bf16[128,4096]{1,0:T(8,128)(2,1)S(1)}, u32[]{:S(2)}, u32[]{:S(2)}) %collective-permute-start.18) | collective-permute-done | bytes 1048608 | tf_op jit(solution)/shard_map/ppermute | solution.py:382
  45.5 10.2 %shard_map.109 = (bf16[64,4096]{1,0:T(8,128)(2,1)S(1)}, bf16[64,4096]{1,0:T(8,128)(2,1)S(1)}, bf16[64,4096]{1,0:T(8,128)(2,1)S(1)}) custom-call(s32[8]{0:T(128)} %pad_add_fusion.1.plan, s32[2,2]{1,0:T(2,128)} %lengths.15, bf16[1,4096]{1,0:T(2,128)(2,1)} %gain.15, bf16[128,4096]{1,0:T(8,128)(2,1)S(1)} %collective-permute-done.17.refs_0_, ...), custom_call_target="tpu_custom_call" | custom-call | flops 5368709120 | bytes 41943040 | tf_op jit(solution)/shard_map/pallas_call | solution.py:266
  55.8 1.9 %collective-permute-start.19 = (bf16[64,4096]{1,0:T(8,128)(2,1)S(1)}, bf16[64,4096]{1,0:T(8,128)(2,1)S(1)}, u32[]{:S(2)}, u32[]{:S(2)}) collective-permute-start(bf16[64,4096]{1,0:T(8,128)(2,1)S(1)} %get-tuple-element.38), channel_id=1, source_target_pairs={{16,17},{17,16},{18,19},{19,18},{20,21},{21,20},{22,23},{23,22},{2... | collective-permute-start | bytes 1572872 | tf_op jit(solution)/shard_map/ppermute | solution.py:382
  57.7 3.4 %collective-permute-start.11 = (bf16[1,2,32,4096]{3,2,1,0:T(8,128)(2,1)S(1)}, bf16[1,2,32,4096]{3,2,1,0:T(8,128)(2,1)S(1)}, u32[]{:S(2)}, u32[]{:S(2)}) collective-permute-start(bf16[1,2,32,4096]{3,2,1,0:T(8,128)(2,1)S(1)} %get-tuple-element.50), channel_id=1, source_target_pairs={{16,17},{17,16},{18,19},{19,18},{20,21},{21,20},{22,23},{23,22},{2... | collective-permute-start | bytes 1572872 | tf_op jit(solution)/shard_map/ppermute | solution.py:382
  61.1 10.4 %shard_map.106 = (bf16[64,4096]{1,0:T(8,128)(2,1)S(1)}, bf16[64,4096]{1,0:T(8,128)(2,1)S(1)}, bf16[64,4096]{1,0:T(8,128)(2,1)S(1)}) custom-call(s32[8]{0:T(128)} %pad_add_fusion.1.plan, s32[2,2]{1,0:T(2,128)} %lengths.15, bf16[1,4096]{1,0:T(2,128)(2,1)} %gain.15, bf16[128,4096]{1,0:T(8,128)(2,1)S(1)} %collective-permute-done.2.refs_0_, ...), custom_call_target="tpu_custom_call" | custom-call | flops 5368709120 | bytes 41943040 | tf_op jit(solution)/shard_map/pallas_call | solution.py:266
  71.5 1.9 %collective-permute-start.4 = (bf16[64,4096]{1,0:T(8,128)(2,1)S(1)}, bf16[64,4096]{1,0:T(8,128)(2,1)S(1)}, u32[]{:S(2)}, u32[]{:S(2)}) collective-permute-start(bf16[64,4096]{1,0:T(8,128)(2,1)S(1)} %get-tuple-element.29), channel_id=1, source_target_pairs={{16,17},{17,16},{18,19},{19,18},{20,21},{21,20},{22,23},{23,22},{2... | collective-permute-start | bytes 1572872 | tf_op jit(solution)/shard_map/ppermute | solution.py:382
  73.6 4.5 %collective-permute-start.21 = (bf16[32,4096]{1,0:T(8,128)(2,1)S(1)}, bf16[32,4096]{1,0:T(8,128)(2,1)S(1)}, u32[]{:S(2)}, u32[]{:S(2)}) collective-permute-start(bf16[32,4096]{1,0:T(8,128)(2,1)S(1)} %add_convert_fusion.refs_0_), channel_id=1, source_target_pairs={{16,24},{17,25},{18,26},{19,27},{20,28},{21,29},{22,30},{23,31},{2... | collective-permute-start | bytes 786440 | tf_op jit(solution)/shard_map/ppermute | solution.py:382
  78.0 3.4 %collective-permute-done.4.arrived = bf16[64,4096]{1,0:T(8,128)(2,1)S(1)} collective-permute-done((bf16[64,4096]{1,0:T(8,128)(2,1)S(1)}, bf16[64,4096]{1,0:T(8,128)(2,1)S(1)}, u32[]{:S(2)}, u32[]{:S(2)}) %collective-permute-start.4) | collective-permute-done | bytes 524320 | tf_op jit(solution)/shard_map/ppermute | solution.py:382
  81.5 4.2 %collective-permute-start.6 = (bf16[32,4096]{1,0:T(8,128)(2,1)S(1)}, bf16[32,4096]{1,0:T(8,128)(2,1)S(1)}, u32[]{:S(2)}, u32[]{:S(2)}) collective-permute-start(bf16[32,4096]{1,0:T(8,128)(2,1)S(1)} %add_convert_fusion.1.refs_0_), channel_id=1, source_target_pairs={{16,24},{17,25},{18,26},{19,27},{20,28},{21,29},{22,30},{23,31},{2... | collective-permute-start | bytes 786440 | tf_op jit(solution)/shard_map/ppermute | solution.py:382
  85.8 3.2 %collective-permute-start.20 = (bf16[32,4096]{1,0:T(8,128)(2,1)S(1)}, bf16[32,4096]{1,0:T(8,128)(2,1)S(1)}, u32[]{:S(2)}, u32[]{:S(2)}) collective-permute-start(bf16[32,4096]{1,0:T(8,128)(2,1)S(1)} %add_convert_fusion.refs_0_), channel_id=1, source_target_pairs={{16,20},{17,21},{18,22},{19,23},{20,16},{21,17},{22,18},{23,19},{2... | collective-permute-start | bytes 786440 | tf_op jit(solution)/shard_map/ppermute | solution.py:382
  89.0 2.1 %collective-permute-start.22 = (bf16[32,4096]{1,0:T(8,128)(2,1)S(1)}, bf16[32,4096]{1,0:T(8,128)(2,1)S(1)}, u32[]{:S(2)}, u32[]{:S(2)}) collective-permute-start(bf16[32,4096]{1,0:T(8,128)(2,1)S(1)} %collective-permute-done.21.refs_2_), channel_id=1, source_target_pairs={{16,20},{17,21},{18,22},{19,23},{20,16},{21,17},{22,18},{23,19},{2... | collective-permute-start | bytes 786440 | tf_op jit(solution)/shard_map/ppermute | solution.py:382
  91.1 3.2 %collective-permute-start.5 = (bf16[32,4096]{1,0:T(8,128)(2,1)S(1)}, bf16[32,4096]{1,0:T(8,128)(2,1)S(1)}, u32[]{:S(2)}, u32[]{:S(2)}) collective-permute-start(bf16[32,4096]{1,0:T(8,128)(2,1)S(1)} %add_convert_fusion.1.refs_0_), channel_id=1, source_target_pairs={{16,20},{17,21},{18,22},{19,23},{20,16},{21,17},{22,18},{23,19},{2... | collective-permute-start | bytes 786440 | tf_op jit(solution)/shard_map/ppermute | solution.py:382
  94.3 2.1 %collective-permute-start.7 = (bf16[32,4096]{1,0:T(8,128)(2,1)S(1)}, bf16[32,4096]{1,0:T(8,128)(2,1)S(1)}, u32[]{:S(2)}, u32[]{:S(2)}) collective-permute-start(bf16[32,4096]{1,0:T(8,128)(2,1)S(1)} %collective-permute-done.6.refs_2_), channel_id=1, source_target_pairs={{16,20},{17,21},{18,22},{19,23},{20,16},{21,17},{22,18},{23,19},{2... | collective-permute-start | bytes 786440 | tf_op jit(solution)/shard_map/ppermute | solution.py:382
  98.1 3.2 %collective-permute-start.23 = (bf16[32,4096]{1,0:T(8,128)(2,1)S(1)}, bf16[32,4096]{1,0:T(8,128)(2,1)S(1)}, u32[]{:S(2)}, u32[]{:S(2)}) collective-permute-start(bf16[32,4096]{1,0:T(8,128)(2,1)S(1)} %get-tuple-element.40), channel_id=1, source_target_pairs={{16,18},{17,19},{18,16},{19,17},{20,22},{21,23},{22,20},{23,21},{2... | collective-permute-start | bytes 786440 | tf_op jit(solution)/shard_map/ppermute | solution.py:382
  101.2 1.3 collective-permute-start.12
  103.7 3.2 %collective-permute-start.8 = (bf16[32,4096]{1,0:T(8,128)(2,1)S(1)}, bf16[32,4096]{1,0:T(8,128)(2,1)S(1)}, u32[]{:S(2)}, u32[]{:S(2)}) collective-permute-start(bf16[32,4096]{1,0:T(8,128)(2,1)S(1)} %get-tuple-element.31), channel_id=1, source_target_pairs={{16,18},{17,19},{18,16},{19,17},{20,22},{21,23},{22,20},{23,21},{2... | collective-permute-start | bytes 786440 | tf_op jit(solution)/shard_map/ppermute | solution.py:382
  107.5 1.3 collective-permute-start.25
  108.8 1.3 collective-permute-start.24
  121.9 22.3 %collective-permute-start.30 = (bf16[64,4096]{1,0:T(8,128)(2,1)S(1)}, bf16[64,4096]{1,0:T(8,128)(2,1)}, u32[]{:S(2)}, u32[]{:S(2)}) collective-permute-start(bf16[64,4096]{1,0:T(8,128)(2,1)S(1)} %get-tuple-element.27.x_own), channel_id=1, source_target_pairs={{16,0},{17,1},{18,2},{19,3},{20,4},{21,5},{22,6},{23,7},{24,8},{25... | collective-permute-start | bytes 1572872 | tf_op jit(solution)/shard_map/ppermute | solution.py:382
  144.2 2.1 %collective-permute-start.31 = (bf16[64,4096]{1,0:T(8,128)(2,1)S(1)}, bf16[64,4096]{1,0:T(8,128)(2,1)}, u32[]{:S(2)}, u32[]{:S(2)}) collective-permute-start(bf16[64,4096]{1,0:T(8,128)(2,1)S(1)} %get-tuple-element.36.x_own), channel_id=1, source_target_pairs={{16,0},{17,1},{18,2},{19,3},{20,4},{21,5},{22,6},{23,7},{24,8},{25... | collective-permute-start | bytes 1572872 | tf_op jit(solution)/shard_map/ppermute | solution.py:382
  146.3 12.5 %shard_map.111 = (bf16[64,4096]{1,0:T(8,128)(2,1)S(1)}, bf16[64,4096]{1,0:T(8,128)(2,1)}, bf16[64,4096]{1,0:T(8,128)(2,1)}) custom-call(s32[8]{0:T(128)} %pad_add_fusion.1.plan, s32[2,2]{1,0:T(2,128)} %lengths.15, bf16[1,4096]{1,0:T(2,128)(2,1)} %gain.15, bf16[128,4096]{1,0:T(8,128)(2,1)} %collective-permute-done.26.refs_0_, ...), custom_call_target="tpu_custom_call" | custom-call | flops 5368709120 | bytes 41943040 | tf_op jit(solution)/shard_map/pallas_call | solution.py:266
  159.6 3.1 %collective-permute-start.28 = (bf16[64,4096]{1,0:T(8,128)(2,1)}, bf16[64,4096]{1,0:T(8,128)(2,1)S(1)}, u32[]{:S(2)}, u32[]{:S(2)}) collective-permute-start(bf16[64,4096]{1,0:T(8,128)(2,1)} %get-tuple-element.43), channel_id=1, source_target_pairs={{16,17},{17,16},{18,19},{19,18},{20,21},{21,20},{22,23},{23,22},{2... | collective-permute-start | bytes 1572872 | tf_op jit(solution)/shard_map/ppermute | solution.py:382
  162.8 1.5 collective-permute-start.29
  164.2 10.2 %shard_map.108 = (bf16[64,4096]{1,0:T(8,128)(2,1)S(1)}, bf16[64,4096]{1,0:T(8,128)(2,1)S(1)}, bf16[64,4096]{1,0:T(8,128)(2,1)S(1)}) custom-call(s32[8]{0:T(128)} %pad_add_fusion.1.plan, s32[2,2]{1,0:T(2,128)} %lengths.15, bf16[1,4096]{1,0:T(2,128)(2,1)} %gain.15, bf16[128,4096]{1,0:T(8,128)(2,1)S(1)} %collective-permute-done.13.refs_0_, ...), custom_call_target="tpu_custom_call" | custom-call | flops 5368709120 | bytes 41943040 | tf_op jit(solution)/shard_map/pallas_call | solution.py:266
  174.5 2.1 %collective-permute-start.15 = (bf16[64,4096]{1,0:T(8,128)(2,1)S(1)}, bf16[64,4096]{1,0:T(8,128)(2,1)S(1)}, u32[]{:S(2)}, u32[]{:S(2)}) collective-permute-start(bf16[64,4096]{1,0:T(8,128)(2,1)S(1)} %get-tuple-element.34), channel_id=1, source_target_pairs={{16,17},{17,16},{18,19},{19,18},{20,21},{21,20},{22,23},{23,22},{2... | collective-permute-start | bytes 1572872 | tf_op jit(solution)/shard_map/ppermute | solution.py:382
  176.7 1.3 collective-permute-start.16
  178.0 1.7 shard_map.112
  179.7 1.7 shard_map.113
  181.4 2.6 %shard_map.114 = (bf16[1,2,2,32,4096]{4,3,2,1,0:T(8,128)(2,1)}, bf16[1,2,2,32,4096]{4,3,2,1,0:T(8,128)(2,1)}) custom-call(s32[8]{0:T(128)S(1)} %copy-done.3, bf16[64,4096]{1,0:T(8,128)(2,1)} %get-tuple-element.41.x_own, bf16[64,4096]{1,0:T(8,128)(2,1)S(1)} %copy-done.1, ...), custom_call_target="tpu_custom_call", output_to_operand_aliasing={{0}: (5, {}), {1}: (6, {})} | custom-call | tf_op jit(solution)/shard_map/pallas_call | solution.py:355
  184.4 1.7 shard_map.115
  (69 shorter events, 26.8 us)
Async XLA Ops:
  0.6 11.1 %collective-permute-start = (bf16[2,32,4096]{2,1,0:T(8,128)(2,1)}, bf16[2,32,4096]{2,1,0:T(8,128)(2,1)S(1)}, u32[]{:S(2)}, u32[]{:S(2)}) collective-permute-start(bf16[2,32,4096]{2,1,0:T(8,128)(2,1)} %refs_0_.3), channel_id=1, source_target_pairs={{0,1},{1,0},{2,3},{3,2},{4,5},{5,4},{6,7},{7,6},{8,9},{9,8},{10,11... | collective-permute-start | bytes 1572872 | tf_op jit(solution)/shard_map/ppermute | solution.py:382
  2.6 9.1 %collective-permute-start.1 = (bf16[1,2,32,4096]{3,2,1,0:T(8,128)(2,1)S(1)}, bf16[1,2,32,4096]{3,2,1,0:T(8,128)(2,1)S(1)}, u32[]{:S(2)}, u32[]{:S(2)}) collective-permute-start(bf16[1,2,32,4096]{3,2,1,0:T(8,128)(2,1)S(1)} %get-tuple-element.51), channel_id=1, source_target_pairs={{0,1},{1,0},{2,3},{3,2},{4,5},{5,4},{6,7},{7,6},{8,9},{9,8},{10,11... | collective-permute-start | bytes 1572872 | tf_op jit(solution)/shard_map/ppermute | solution.py:382
  20.9 24.6 %collective-permute-start.18 = (bf16[128,4096]{1,0:T(8,128)(2,1)S(1)}, bf16[128,4096]{1,0:T(8,128)(2,1)S(1)}, u32[]{:S(2)}, u32[]{:S(2)}) collective-permute-start(bf16[128,4096]{1,0:T(8,128)(2,1)S(1)} %get-tuple-element.35), channel_id=1, source_target_pairs={{0,17},{1,16},{2,19},{3,18},{4,21},{5,20},{6,23},{7,22},{8,25},{9,... | collective-permute-start | bytes 3145736 | tf_op jit(solution)/shard_map/ppermute | solution.py:382
  22.2 23.3 %collective-permute-start.17 = (bf16[128,4096]{1,0:T(8,128)(2,1)S(1)}, bf16[128,4096]{1,0:T(8,128)(2,1)S(1)}, u32[]{:S(2)}, u32[]{:S(2)}) collective-permute-start(bf16[128,4096]{1,0:T(8,128)(2,1)S(1)} %get-tuple-element.35), channel_id=1, source_target_pairs={{0,16},{1,17},{2,18},{3,19},{4,20},{5,21},{6,22},{7,23},{8,24},{9,... | collective-permute-start | bytes 3145736 | tf_op jit(solution)/shard_map/ppermute | solution.py:382
  24.3 36.8 %collective-permute-start.3 = (bf16[128,4096]{1,0:T(8,128)(2,1)S(1)}, bf16[128,4096]{1,0:T(8,128)(2,1)S(1)}, u32[]{:S(2)}, u32[]{:S(2)}) collective-permute-start(bf16[128,4096]{1,0:T(8,128)(2,1)S(1)} %shard_map.105), channel_id=1, source_target_pairs={{0,17},{1,16},{2,19},{3,18},{4,21},{5,20},{6,23},{7,22},{8,25},{9,... | collective-permute-start | bytes 3145736 | tf_op jit(solution)/shard_map/ppermute | solution.py:382
  25.6 35.5 %collective-permute-start.2 = (bf16[128,4096]{1,0:T(8,128)(2,1)S(1)}, bf16[128,4096]{1,0:T(8,128)(2,1)S(1)}, u32[]{:S(2)}, u32[]{:S(2)}) collective-permute-start(bf16[128,4096]{1,0:T(8,128)(2,1)S(1)} %shard_map.105), channel_id=1, source_target_pairs={{0,16},{1,17},{2,18},{3,19},{4,20},{5,21},{6,22},{7,23},{8,24},{9,... | collective-permute-start | bytes 3145736 | tf_op jit(solution)/shard_map/ppermute | solution.py:382
  55.8 17.7 %collective-permute-start.19 = (bf16[64,4096]{1,0:T(8,128)(2,1)S(1)}, bf16[64,4096]{1,0:T(8,128)(2,1)S(1)}, u32[]{:S(2)}, u32[]{:S(2)}) collective-permute-start(bf16[64,4096]{1,0:T(8,128)(2,1)S(1)} %get-tuple-element.38), channel_id=1, source_target_pairs={{16,17},{17,16},{18,19},{19,18},{20,21},{21,20},{22,23},{23,22},{2... | collective-permute-start | bytes 1572872 | tf_op jit(solution)/shard_map/ppermute | solution.py:382
  57.7 43.5 %collective-permute-start.11 = (bf16[1,2,32,4096]{3,2,1,0:T(8,128)(2,1)S(1)}, bf16[1,2,32,4096]{3,2,1,0:T(8,128)(2,1)S(1)}, u32[]{:S(2)}, u32[]{:S(2)}) collective-permute-start(bf16[1,2,32,4096]{3,2,1,0:T(8,128)(2,1)S(1)} %get-tuple-element.50), channel_id=1, source_target_pairs={{16,17},{17,16},{18,19},{19,18},{20,21},{21,20},{22,23},{23,22},{2... | collective-permute-start | bytes 1572872 | tf_op jit(solution)/shard_map/ppermute | solution.py:382
  71.5 9.9 %collective-permute-start.4 = (bf16[64,4096]{1,0:T(8,128)(2,1)S(1)}, bf16[64,4096]{1,0:T(8,128)(2,1)S(1)}, u32[]{:S(2)}, u32[]{:S(2)}) collective-permute-start(bf16[64,4096]{1,0:T(8,128)(2,1)S(1)} %get-tuple-element.29), channel_id=1, source_target_pairs={{16,17},{17,16},{18,19},{19,18},{20,21},{21,20},{22,23},{23,22},{2... | collective-permute-start | bytes 1572872 | tf_op jit(solution)/shard_map/ppermute | solution.py:382
  73.6 15.4 %collective-permute-start.21 = (bf16[32,4096]{1,0:T(8,128)(2,1)S(1)}, bf16[32,4096]{1,0:T(8,128)(2,1)S(1)}, u32[]{:S(2)}, u32[]{:S(2)}) collective-permute-start(bf16[32,4096]{1,0:T(8,128)(2,1)S(1)} %add_convert_fusion.refs_0_), channel_id=1, source_target_pairs={{16,24},{17,25},{18,26},{19,27},{20,28},{21,29},{22,30},{23,31},{2... | collective-permute-start | bytes 786440 | tf_op jit(solution)/shard_map/ppermute | solution.py:382
  81.5 12.8 %collective-permute-start.6 = (bf16[32,4096]{1,0:T(8,128)(2,1)S(1)}, bf16[32,4096]{1,0:T(8,128)(2,1)S(1)}, u32[]{:S(2)}, u32[]{:S(2)}) collective-permute-start(bf16[32,4096]{1,0:T(8,128)(2,1)S(1)} %add_convert_fusion.1.refs_0_), channel_id=1, source_target_pairs={{16,24},{17,25},{18,26},{19,27},{20,28},{21,29},{22,30},{23,31},{2... | collective-permute-start | bytes 786440 | tf_op jit(solution)/shard_map/ppermute | solution.py:382
  85.8 10.6 %collective-permute-start.20 = (bf16[32,4096]{1,0:T(8,128)(2,1)S(1)}, bf16[32,4096]{1,0:T(8,128)(2,1)S(1)}, u32[]{:S(2)}, u32[]{:S(2)}) collective-permute-start(bf16[32,4096]{1,0:T(8,128)(2,1)S(1)} %add_convert_fusion.refs_0_), channel_id=1, source_target_pairs={{16,20},{17,21},{18,22},{19,23},{20,16},{21,17},{22,18},{23,19},{2... | collective-permute-start | bytes 786440 | tf_op jit(solution)/shard_map/ppermute | solution.py:382
  89.0 8.4 %collective-permute-start.22 = (bf16[32,4096]{1,0:T(8,128)(2,1)S(1)}, bf16[32,4096]{1,0:T(8,128)(2,1)S(1)}, u32[]{:S(2)}, u32[]{:S(2)}) collective-permute-start(bf16[32,4096]{1,0:T(8,128)(2,1)S(1)} %collective-permute-done.21.refs_2_), channel_id=1, source_target_pairs={{16,20},{17,21},{18,22},{19,23},{20,16},{21,17},{22,18},{23,19},{2... | collective-permute-start | bytes 786440 | tf_op jit(solution)/shard_map/ppermute | solution.py:382
  91.1 11.5 %collective-permute-start.5 = (bf16[32,4096]{1,0:T(8,128)(2,1)S(1)}, bf16[32,4096]{1,0:T(8,128)(2,1)S(1)}, u32[]{:S(2)}, u32[]{:S(2)}) collective-permute-start(bf16[32,4096]{1,0:T(8,128)(2,1)S(1)} %add_convert_fusion.1.refs_0_), channel_id=1, source_target_pairs={{16,20},{17,21},{18,22},{19,23},{20,16},{21,17},{22,18},{23,19},{2... | collective-permute-start | bytes 786440 | tf_op jit(solution)/shard_map/ppermute | solution.py:382
  94.3 8.7 %collective-permute-start.7 = (bf16[32,4096]{1,0:T(8,128)(2,1)S(1)}, bf16[32,4096]{1,0:T(8,128)(2,1)S(1)}, u32[]{:S(2)}, u32[]{:S(2)}) collective-permute-start(bf16[32,4096]{1,0:T(8,128)(2,1)S(1)} %collective-permute-done.6.refs_2_), channel_id=1, source_target_pairs={{16,20},{17,21},{18,22},{19,23},{20,16},{21,17},{22,18},{23,19},{2... | collective-permute-start | bytes 786440 | tf_op jit(solution)/shard_map/ppermute | solution.py:382
  98.1 8.8 %collective-permute-start.23 = (bf16[32,4096]{1,0:T(8,128)(2,1)S(1)}, bf16[32,4096]{1,0:T(8,128)(2,1)S(1)}, u32[]{:S(2)}, u32[]{:S(2)}) collective-permute-start(bf16[32,4096]{1,0:T(8,128)(2,1)S(1)} %get-tuple-element.40), channel_id=1, source_target_pairs={{16,18},{17,19},{18,16},{19,17},{20,22},{21,23},{22,20},{23,21},{2... | collective-permute-start | bytes 786440 | tf_op jit(solution)/shard_map/ppermute | solution.py:382
  101.2 13.1 %collective-permute-start.12 = (bf16[1,2,32,4096]{3,2,1,0:T(8,128)(2,1)S(1)}, bf16[1,2,32,4096]{3,2,1,0:T(8,128)(2,1)S(1)}, u32[]{:S(2)}, u32[]{:S(2)}) collective-permute-start(bf16[1,2,32,4096]{3,2,1,0:T(8,128)(2,1)S(1)} %collective-permute-done.11), channel_id=1, source_target_pairs={{16,0},{17,1},{18,2},{19,3},{20,4},{21,5},{22,6},{23,7},{24,8},{25... | collective-permute-start | bytes 1572872 | tf_op jit(solution)/shard_map/ppermute | solution.py:382
  103.7 7.4 %collective-permute-start.8 = (bf16[32,4096]{1,0:T(8,128)(2,1)S(1)}, bf16[32,4096]{1,0:T(8,128)(2,1)S(1)}, u32[]{:S(2)}, u32[]{:S(2)}) collective-permute-start(bf16[32,4096]{1,0:T(8,128)(2,1)S(1)} %get-tuple-element.31), channel_id=1, source_target_pairs={{16,18},{17,19},{18,16},{19,17},{20,22},{21,23},{22,20},{23,21},{2... | collective-permute-start | bytes 786440 | tf_op jit(solution)/shard_map/ppermute | solution.py:382
  107.5 6.9 %collective-permute-start.25 = (bf16[32,4096]{1,0:T(8,128)(2,1)S(1)}, bf16[32,4096]{1,0:T(8,128)(2,1)S(1)}, u32[]{:S(2)}, u32[]{:S(2)}) collective-permute-start(bf16[32,4096]{1,0:T(8,128)(2,1)S(1)} %pick.7), channel_id=1, source_target_pairs={{16,1},{17,0},{18,3},{19,2},{20,5},{21,4},{22,7},{23,6},{24,9},{25... | collective-permute-start | bytes 786440 | tf_op jit(solution)/shard_map/ppermute | solution.py:382
  108.8 5.6 %collective-permute-start.24 = (bf16[32,4096]{1,0:T(8,128)(2,1)S(1)}, bf16[32,4096]{1,0:T(8,128)(2,1)S(1)}, u32[]{:S(2)}, u32[]{:S(2)}) collective-permute-start(bf16[32,4096]{1,0:T(8,128)(2,1)S(1)} %pick.7), channel_id=1, source_target_pairs={{16,0},{17,1},{18,2},{19,3},{20,4},{21,5},{22,6},{23,7},{24,8},{25... | collective-permute-start | bytes 786440 | tf_op jit(solution)/shard_map/ppermute | solution.py:382
  111.7 6.8 %collective-permute-start.10 = (bf16[32,4096]{1,0:T(8,128)(2,1)S(1)}, bf16[32,4096]{1,0:T(8,128)(2,1)S(1)}, u32[]{:S(2)}, u32[]{:S(2)}) collective-permute-start(bf16[32,4096]{1,0:T(8,128)(2,1)S(1)} %pick.5), channel_id=1, source_target_pairs={{16,1},{17,0},{18,3},{19,2},{20,5},{21,4},{22,7},{23,6},{24,9},{25... | collective-permute-start | bytes 786440 | tf_op jit(solution)/shard_map/ppermute | solution.py:382
  113.0 5.5 %collective-permute-start.9 = (bf16[32,4096]{1,0:T(8,128)(2,1)S(1)}, bf16[32,4096]{1,0:T(8,128)(2,1)S(1)}, u32[]{:S(2)}, u32[]{:S(2)}) collective-permute-start(bf16[32,4096]{1,0:T(8,128)(2,1)S(1)} %pick.5), channel_id=1, source_target_pairs={{16,0},{17,1},{18,2},{19,3},{20,4},{21,5},{22,6},{23,7},{24,8},{25... | collective-permute-start | bytes 786440 | tf_op jit(solution)/shard_map/ppermute | solution.py:382
  115.9 28.3 %collective-permute-start.27 = (bf16[128,4096]{1,0:T(8,128)(2,1)S(1)}, bf16[128,4096]{1,0:T(8,128)(2,1)S(1)}, u32[]{:S(2)}, u32[]{:S(2)}) collective-permute-start(bf16[128,4096]{1,0:T(8,128)(2,1)S(1)} %shard_map.110), channel_id=1, source_target_pairs={{0,17},{1,16},{2,19},{3,18},{4,21},{5,20},{6,23},{7,22},{8,25},{9,... | collective-permute-start | bytes 3145736 | tf_op jit(solution)/shard_map/ppermute | solution.py:382
  117.2 29.1 %collective-permute-start.26 = (bf16[128,4096]{1,0:T(8,128)(2,1)S(1)}, bf16[128,4096]{1,0:T(8,128)(2,1)}, u32[]{:S(2)}, u32[]{:S(2)}) collective-permute-start(bf16[128,4096]{1,0:T(8,128)(2,1)S(1)} %shard_map.110), channel_id=1, source_target_pairs={{0,16},{1,17},{2,18},{3,19},{4,20},{5,21},{6,22},{7,23},{8,24},{9,... | collective-permute-start | bytes 3145736 | tf_op jit(solution)/shard_map/ppermute | solution.py:382
  119.3 43.4 %collective-permute-start.14 = (bf16[128,4096]{1,0:T(8,128)(2,1)S(1)}, bf16[128,4096]{1,0:T(8,128)(2,1)S(1)}, u32[]{:S(2)}, u32[]{:S(2)}) collective-permute-start(bf16[128,4096]{1,0:T(8,128)(2,1)S(1)} %shard_map.107), channel_id=1, source_target_pairs={{0,17},{1,16},{2,19},{3,18},{4,21},{5,20},{6,23},{7,22},{8,25},{9,... | collective-permute-start | bytes 3145736 | tf_op jit(solution)/shard_map/ppermute | solution.py:382
  120.6 43.6 %collective-permute-start.13 = (bf16[128,4096]{1,0:T(8,128)(2,1)S(1)}, bf16[128,4096]{1,0:T(8,128)(2,1)S(1)}, u32[]{:S(2)}, u32[]{:S(2)}) collective-permute-start(bf16[128,4096]{1,0:T(8,128)(2,1)S(1)} %shard_map.107), channel_id=1, source_target_pairs={{0,16},{1,17},{2,18},{3,19},{4,20},{5,21},{6,22},{7,23},{8,24},{9,... | collective-permute-start | bytes 3145736 | tf_op jit(solution)/shard_map/ppermute | solution.py:382
  121.9 57.8 %collective-permute-start.30 = (bf16[64,4096]{1,0:T(8,128)(2,1)S(1)}, bf16[64,4096]{1,0:T(8,128)(2,1)}, u32[]{:S(2)}, u32[]{:S(2)}) collective-permute-start(bf16[64,4096]{1,0:T(8,128)(2,1)S(1)} %get-tuple-element.27.x_own), channel_id=1, source_target_pairs={{16,0},{17,1},{18,2},{19,3},{20,4},{21,5},{22,6},{23,7},{24,8},{25... | collective-permute-start | bytes 1572872 | tf_op jit(solution)/shard_map/ppermute | solution.py:382
  144.2 32.4 %collective-permute-start.31 = (bf16[64,4096]{1,0:T(8,128)(2,1)S(1)}, bf16[64,4096]{1,0:T(8,128)(2,1)}, u32[]{:S(2)}, u32[]{:S(2)}) collective-permute-start(bf16[64,4096]{1,0:T(8,128)(2,1)S(1)} %get-tuple-element.36.x_own), channel_id=1, source_target_pairs={{16,0},{17,1},{18,2},{19,3},{20,4},{21,5},{22,6},{23,7},{24,8},{25... | collective-permute-start | bytes 1572872 | tf_op jit(solution)/shard_map/ppermute | solution.py:382
  159.6 21.8 %collective-permute-start.28 = (bf16[64,4096]{1,0:T(8,128)(2,1)}, bf16[64,4096]{1,0:T(8,128)(2,1)S(1)}, u32[]{:S(2)}, u32[]{:S(2)}) collective-permute-start(bf16[64,4096]{1,0:T(8,128)(2,1)} %get-tuple-element.43), channel_id=1, source_target_pairs={{16,17},{17,16},{18,19},{19,18},{20,21},{21,20},{22,23},{23,22},{2... | collective-permute-start | bytes 1572872 | tf_op jit(solution)/shard_map/ppermute | solution.py:382
  162.8 18.6 %collective-permute-start.29 = (bf16[64,4096]{1,0:T(8,128)(2,1)}, bf16[64,4096]{1,0:T(8,128)(2,1)S(1)}, u32[]{:S(2)}, u32[]{:S(2)}) collective-permute-start(bf16[64,4096]{1,0:T(8,128)(2,1)} %get-tuple-element.41.x_own), channel_id=1, source_target_pairs={{16,0},{17,1},{18,2},{19,3},{20,4},{21,5},{22,6},{23,7},{24,8},{25... | collective-permute-start | bytes 1572872 | tf_op jit(solution)/shard_map/ppermute | solution.py:382
  174.5 9.9 %collective-permute-start.15 = (bf16[64,4096]{1,0:T(8,128)(2,1)S(1)}, bf16[64,4096]{1,0:T(8,128)(2,1)S(1)}, u32[]{:S(2)}, u32[]{:S(2)}) collective-permute-start(bf16[64,4096]{1,0:T(8,128)(2,1)S(1)} %get-tuple-element.34), channel_id=1, source_target_pairs={{16,17},{17,16},{18,19},{19,18},{20,21},{21,20},{22,23},{23,22},{2... | collective-permute-start | bytes 1572872 | tf_op jit(solution)/shard_map/ppermute | solution.py:382
  176.7 7.8 %collective-permute-start.16 = (bf16[64,4096]{1,0:T(8,128)(2,1)S(1)}, bf16[64,4096]{1,0:T(8,128)(2,1)S(1)}, u32[]{:S(2)}, u32[]{:S(2)}) collective-permute-start(bf16[64,4096]{1,0:T(8,128)(2,1)S(1)} %get-tuple-element.32.x_own), channel_id=1, source_target_pairs={{16,0},{17,1},{18,2},{19,3},{20,4},{21,5},{22,6},{23,7},{24,8},{25... | collective-permute-start | bytes 1572872 | tf_op jit(solution)/shard_map/ppermute | solution.py:382
  (5 other events, 75.2 us)
